TPU v7x, 32 devices: a whole 2x2x4 slice. The times are simulated.
32 devices in a mesh: groups: 2 (over y), dp: 16 (over z, x, core).
Axes of the slice: x: 2, y: 2, z: 4, core: 2. Of those that a mesh axis runs over, the one named last changes fastest.
Arguments:
- layer_inputs: bfloat16 [2, 32, 1344, 512], P(None, ('groups', 'dp')), parts along dimension 1, may hold values from -6 to 6
- out_grads: bfloat16 [2, 32, 1344, 512], P(None, ('groups', 'dp')), parts along dimension 1, may hold values from -6 to 6
- error_prev: bfloat16 [2, 49152, 512], P(None, ('groups', 'dp')), parts along dimension 1, may hold values from -4 to 4
- q_start: float32 [2, 512, 64], replicated, may hold values from -0.25 to 0.25
Outputs:
- panels: float32 [4, 1536, 64], P('groups'), parts along dimension 0
- factors: float32 [4, 512, 64], P('groups'), parts along dimension 0
- error_next: bfloat16 [2, 49152, 512], P(None, ('groups', 'dp')), parts along dimension 1
There are 2 independent parts, one for each index of `groups`. A program takes and returns all parts, laid end to end along the dimension named above; an argument that names none is the same for every part. Nothing has to cross between parts.
All inputs are finite; a program needn't handle non-finite values.
Results may differ from a plain program's by a relative error of at most 0.001.
Values sent between devices are 32-bit elements; how exact they have to be, the bound alone decides.
No kernel may reach another device: no remote copies, remote signals or barrier semaphores. Data moves between devices by JAX's collectives and lax.ppermute only.
A program may use at most 64 MiB of HBM per device.

v0:
```python
import math

import jax
import jax.numpy as jnp
from jax import lax
from jax.sharding import PartitionSpec as P

C = 512
RANK = 64
LEN = 1344
LAYERS = 2
DILATION = 64


def unfold_rows(seqs, spacing):
    length = seqs.shape[1]
    padded = jnp.pad(seqs, ((0, 0), (spacing, spacing), (0, 0)))
    pieces = [padded[:, offset * spacing : offset * spacing + length] for offset in range(3)]
    return jnp.concatenate(pieces, axis=2)


def layer_grads(seqs, grads_out, errors, spacing, scale):
    columns = unfold_rows(seqs, spacing).reshape(-1, 3 * C)
    flat_grads = grads_out.reshape(-1, C)
    product = lax.dot_general(
        columns, flat_grads, (((0,), (0,)), ((), ())), preferred_element_type=jnp.float32
    )
    return product * scale + errors.astype(jnp.float32)


def orthogonal_rows(rows_block, gram):
    lower_all = jnp.linalg.cholesky(gram)
    shaped = rows_block.reshape(rows_block.shape[0], LAYERS, RANK)
    solved = [
        lax.linalg.triangular_solve(
            lower_all[layer_no], shaped[:, layer_no], left_side=False, lower=True, transpose_a=True
        )
        for layer_no in range(LAYERS)
    ]
    return jnp.concatenate(solved, axis=1)


def gram_terms(rows_block):
    shaped = rows_block.reshape(rows_block.shape[0], LAYERS, RANK)
    return jnp.einsum("rla,rlb->lab", shaped, shaped, precision=lax.Precision.HIGHEST)


def body(layer_inputs, out_grads, error_prev, q_start):
    high = lax.Precision.HIGHEST
    seq_dev = layer_inputs.shape[1]
    scale = 1.0 / math.sqrt(seq_dev * LEN)
    devices = lax.axis_size("dp")
    rows_three = 3 * C
    grads_list = []
    for layer_no in range(LAYERS):
        spacing = DILATION // 2 ** (LAYERS - 1 - layer_no)
        grads_list.append(
            layer_grads(
                layer_inputs[layer_no], out_grads[layer_no], error_prev[layer_no], spacing, scale
            )
        )

    def panel_terms():
        parts_list = [
            jnp.dot(grads_list[layer_no], q_start[layer_no], precision=high)
            for layer_no in range(LAYERS)
        ]
        return jnp.concatenate(parts_list, axis=1)

    summed = lax.psum(panel_terms(), "dp") / math.sqrt(devices)
    gram = gram_terms(summed) / rows_three
    panel_all = orthogonal_rows(summed, gram)
    factor_parts = [
        lax.dot_general(
            grads_list[layer_no],
            panel_all[:, layer_no * RANK : (layer_no + 1) * RANK],
            (((0,), (0,)), ((), ())),
            precision=high,
            preferred_element_type=jnp.float32,
        )
        for layer_no in range(LAYERS)
    ]
    norm_factor = math.sqrt(rows_three * devices)
    factor_all = lax.psum(jnp.concatenate(factor_parts, axis=1), "dp") / norm_factor
    panel_list = []
    factor_list = []
    error_list = []
    for layer_no in range(LAYERS):
        panel_one = panel_all[:, layer_no * RANK : (layer_no + 1) * RANK]
        factor_one = factor_all[:, layer_no * RANK : (layer_no + 1) * RANK]
        approx = jnp.dot(panel_one, factor_one.T, precision=high) / norm_factor
        error_list.append((grads_list[layer_no] - approx).astype(jnp.bfloat16))
        panel_list.append(panel_one)
        factor_list.append(factor_one)
    return (jnp.stack(panel_list), jnp.stack(factor_list), jnp.stack(error_list))


def solution(mesh):
    in_specs = (
        P(None, ("groups", "dp"), None, None),
        P(None, ("groups", "dp"), None, None),
        P(None, ("groups", "dp"), None),
        P(),
    )
    out_specs = (P("groups", None, None), P("groups", None, None), P(None, ("groups", "dp"), None))
    return jax.shard_map(body, mesh=mesh, in_specs=in_specs, out_specs=out_specs, check_vma=False)
```

profile of v0, /device:TPU:0, one launch (start us, length us, event | category | flops | bytes accessed | tf_op | source)
XLA Modules:
  0.0 264.4 jit_solution(4416453338482522758)
XLA Ops:
  7.2 0.0 all-reduce.5.cloned.1.call-start
  7.2 1.9 slice_bitcast_fusion.1
  9.1 0.0 copy-start.7
  9.2 0.0 copy-start.8
  9.2 0.6 pad_slice_fusion.1
  9.8 1.2 copy-done.7
  11.0 0.8 copy-done.8
  11.9 0.0 copy-start.6
  11.9 2.7 %fusion.14 = f32[1536,512]{1,0:T(8,128)S(1)} fusion(bf16[1,1344,512]{2,1,0:T(8,128)(2,1)S(1)} %get-tuple-element.14, bf16[1,1344,512]{2,1,0:T(8,128)(2,1)S(1)} %get-tuple-element.4, bf16[1,1344,512]{2,1,0:T(8,128)(2,1)S(1)} %get-tuple-element.15, bf16[2,1536,512]{2,1,0:T(8,128)(2,1)S(1)} %copy-done.7, bf16[2,1,1344,512]{3,2,1,0:T(8,128)(2,1)S(1)} %copy-done.8), kind=kOutput, calls=%fused_computation.18 | convolution fusion | flops 2128674816 | bytes 10223616 | tf_op jit(solution)/shard_map/dot_general | solution.py:25
  14.6 0.0 copy-done.6
  14.6 3.2 %fusion.34 = f32[1536,64]{0,1:T(8,128)S(1)} fusion(f32[1536,512]{1,0:T(8,128)S(1)} %fusion.14, f32[2,512,64]{1,2,0:T(8,128)S(1)} %copy-done.6), kind=kOutput, calls=%fused_computation.53 | convolution fusion | flops 603979776 | bytes 3670016 | tf_op jit(solution)/shard_map/dot_general | solution.py:65
  17.8 2.7 %fusion.15 = f32[1536,512]{1,0:T(8,128)S(1)} fusion(bf16[1,1344,512]{2,1,0:T(8,128)(2,1)S(1)} %get-tuple-element.9, bf16[1,1344,512]{2,1,0:T(8,128)(2,1)S(1)} %get-tuple-element.5, bf16[1,1344,512]{2,1,0:T(8,128)(2,1)S(1)} %get-tuple-element.8, bf16[2,1536,512]{2,1,0:T(8,128)(2,1)S(1)} %copy-done.7, bf16[2,1,1344,512]{3,2,1,0:T(8,128)(2,1)S(1)} %copy-done.8), kind=kOutput, calls=%fused_computation.19 | convolution fusion | flops 2128674816 | bytes 10223616 | tf_op jit(solution)/shard_map/dot_general | solution.py:25
  20.4 0.0 copy-start
  20.4 1.7 copy-done
  22.1 3.2 %fusion.32 = f32[1536,64]{0,1:T(8,128)S(1)} fusion(f32[1536,512]{1,0:T(8,128)S(1)} %fusion.15, f32[2,512,64]{1,2,0:T(8,128)S(1)} %copy-done.6), kind=kOutput, calls=%fused_computation.51 | convolution fusion | flops 603979776 | bytes 3670016 | tf_op jit(solution)/shard_map/dot_general | solution.py:65
  25.3 0.9 pad_maximum_fusion.1
  26.2 0.0 all-reduce.5.cloned.1.call-update
  26.2 0.0 all-reduce.7.cloned.1.call-start
  26.3 94.8 %all-reduce.5.cloned.1.call-done = f32[1536,128]{0,1:T(8,128)} async-done(((f32[1536,128]{0,1:T(8,128)}), f32[1536,128]{0,1:T(8,128)}) %all-reduce.5.cloned.1.call-update) | async-done | bytes 786448 | tf_op jit(solution)/shard_map/psum | solution.py:70
  121.2 1.2 broadcast_multiply_fusion
  122.4 0.0 copy-start.2
  122.4 0.9 copy-done.2
  123.3 0.8 convolution_multiply_fusion.2
  124.1 0.1 copy.10
  124.2 11.9 %custom-call.7 = f32[2,64,64]{2,1,0:T(8,128)S(1)} custom-call(f32[2,64,64]{2,1,0:T(8,128)S(1)} %fusion.40), custom_call_target="Cholesky" | custom-call | tf_op jit(solution)/shard_map/jit(cholesky)/cholesky | solution.py:32
  136.1 0.1 compare_reduce_fusion
  136.3 0.1 select_select_fusion
  136.3 0.6 fusion.44
  136.9 5.5 %custom-call.9 = f32[1,64,64]{1,2,0:T(8,128)} custom-call(f32[1,64,64]{2,1,0:T(8,128)S(1)} %get-tuple-element.12), custom_call_target="InvertDiagBlocksLowerTriangular" | custom-call | tf_op jit(solution)/shard_map/triangular_solve/custom-call.0 | solution.py:35
  142.5 1.5 fusion.25
  144.0 2.8 %fusion.29 = f32[512,64]{0,1:T(8,128)} fusion(f32[1536,512]{1,0:T(8,128)S(1)} %fusion.14, f32[64,1536]{1,0:T(8,128)S(1)} %fusion.25), kind=kOutput, calls=%fused_computation.45 | convolution fusion | flops 603979776 | bytes 3670016 | tf_op jit(solution)/shard_map/dot_general | solution.py:74
  146.8 6.3 %custom-call.10 = f32[1,64,64]{1,2,0:T(8,128)} custom-call(f32[1,64,64]{2,1,0:T(8,128)} %get-tuple-element.13), custom_call_target="InvertDiagBlocksLowerTriangular" | custom-call | tf_op jit(solution)/shard_map/triangular_solve/custom-call.0 | solution.py:35
  153.1 1.6 fusion.24
  154.7 0.0 copy-start.3
  154.7 0.7 copy-done.3
  155.4 4.0 %fusion.26 = f32[512,64]{0,1:T(8,128)S(1)} fusion(f32[1536,512]{1,0:T(8,128)} %copy-done, f32[64,1536]{1,0:T(8,128)S(1)} %fusion.24), kind=kOutput, calls=%fused_computation.42 | convolution fusion | flops 603979776 | bytes 3670016 | tf_op jit(solution)/shard_map/dot_general | solution.py:74
  159.4 0.0 copy-done.5
  159.4 0.7 pad_maximum_fusion.3
  160.1 0.0 all-reduce.7.cloned.1.call-update
  160.2 1.9 pad_maximum_fusion.2
  162.1 86.1 %all-reduce.7.cloned.1.call-done = f32[512,128]{0,1:T(8,128)} async-done(((f32[512,128]{0,1:T(8,128)}), f32[512,128]{0,1:T(8,128)}) %all-reduce.7.cloned.1.call-update) | async-done | bytes 262160 | tf_op jit(solution)/shard_map/psum | solution.py:84
  248.2 1.1 broadcast_multiply_fusion.1
  249.3 2.7 %fusion.18 = bf16[1,1536,512]{2,1,0:T(8,128)(2,1)S(1)} fusion(f32[1536,512]{1,0:T(8,128)S(1)} %fusion.14, f32[64,1536]{1,0:T(8,128)S(1)} %fusion.25, f32[512,128]{0,1:T(8,128)S(1)} %broadcast_multiply_fusion.1), kind=kOutput, calls=%fused_computation.23 | convolution fusion | flops 606339072 | bytes 5242880 | tf_op jit(solution)/shard_map/dot_general | solution.py:91
  252.0 0.0 copy-done.1
  252.0 0.0 copy-done.4
  252.0 2.9 %fusion.19 = bf16[1,1536,512]{2,1,0:T(8,128)(2,1)S(1)} fusion(f32[1536,512]{1,0:T(8,128)S(1)} %copy-done.1, f32[64,1536]{1,0:T(8,128)S(1)} %copy-done.4, f32[512,128]{0,1:T(8,128)S(1)} %broadcast_multiply_fusion.1), kind=kOutput, calls=%fused_computation.24 | convolution fusion | flops 606339072 | bytes 5242880 | tf_op jit(solution)/shard_map/dot_general | solution.py:91
  254.9 1.9 pad_maximum_fusion
  256.9 0.7 pad_maximum_fusion.4
  (8 shorter events, 0.1 us)
Async XLA Ops:
  7.2 114.0 %all-reduce.5.cloned.1.call-start = ((), (), s32[]{:S(2)}) async-start(), calls=%async_computation | async-start | bytes 1572864 | tf_op jit(solution)/shard_map/psum | solution.py:70
  9.1 1.9 copy-start.7
  9.2 2.7 %copy-start.8 = (bf16[2,1,1344,512]{3,2,1,0:T(8,128)(2,1)S(1)}, bf16[2,1,1344,512]{3,2,1,0:T(8,128)(2,1)}, u32[]{:S(2)}) copy-start(bf16[2,1,1344,512]{3,2,1,0:T(8,128)(2,1)} %param.7) | copy-start | bytes 8257540
  11.9 2.7 %copy-start.6 = (f32[2,512,64]{1,2,0:T(8,128)S(1)}, f32[2,512,64]{1,2,0:T(8,128)}, u32[]{:S(2)}) copy-start(f32[2,512,64]{1,2,0:T(8,128)} %param.9) | copy-start | bytes 786436
  20.4 1.7 copy-start
  26.2 221.9 %all-reduce.7.cloned.1.call-start = ((), (), s32[]{:S(2)}) async-start(), calls=%async_computation.1 | async-start | bytes 524288 | tf_op jit(solution)/shard_map/psum | solution.py:84
  122.4 0.9 copy-start.2
  153.1 6.3 %copy-start.5 = (f32[512,64]{0,1:T(8,128)S(1)}, f32[512,64]{0,1:T(8,128)}, u32[]{:S(2)}) copy-start(f32[512,64]{0,1:T(8,128)} %fusion.29) | copy-start | bytes 393220
  154.7 0.7 copy-start.3
  248.2 3.9 %copy-start.1 = (f32[1536,512]{1,0:T(8,128)S(1)}, f32[1536,512]{1,0:T(8,128)}, u32[]{:S(2)}) copy-start(f32[1536,512]{1,0:T(8,128)} %copy-done) | copy-start | bytes 9437188
  248.2 3.9 %copy-start.4 = (f32[64,1536]{1,0:T(8,128)S(1)}, f32[64,1536]{1,0:T(8,128)}, u32[]{:S(2)}) copy-start(f32[64,1536]{1,0:T(8,128)} %copy-done.3) | copy-start | bytes 1179652
Sparse Core Ops, SparseCore 0:
  26.4 94.7 all-reduce.4
  160.3 87.8 all-reduce.6
where the time goes:
time: 265 us; the launch traced here: 264 us
  waiting for transfers between devices  181 us (68%)
  other arithmetic  33.1 us (12%)
  matrix products  28 us (11%)
  between operations  14.2 us (5%)
  local copies, waits for them, and re-layouts  8.03 us (3%)
    psum x1, waiting for transfers between devices, body(): summed = lax.psum(panel_terms(), 'dp') / math.sqrt(devices)  94.8 us
    psum x1, waiting for transfers between devices, body(): lax.psum(jnp.concatenate(factor_parts, axis=1), 'dp') / norm_factor  86.1 us
    another operation x4, other arithmetic, orthogonal_rows(): lax.linalg.triangular_solve(lower_all[layer_no], shaped[:, layer_no], lef...  12.4 us
    another operation x4, other arithmetic, orthogonal_rows(): lower_all = jnp.linalg.cholesky(gram)  12.1 us
    dot_general x2, matrix products, body(): lax.dot_general(grads_list[layer_no], panel_all[:, layer_no * RANK:(layer...  6.79 us
    dot_general x2, matrix products, panel_terms(): jnp.dot(grads_list[layer_no], q_start[layer_no], precision=high)  6.36 us
    dot_general x2, matrix products, body(): approx = jnp.dot(panel_one, factor_one.T, precision=high) / norm_factor  5.58 us
    unnamed x18, local copies, waits for them, and re-layouts  5.36 us
  transfers between devices with their start and end apart: 2, of which 2 were waited for; matrix products, arithmetic and copies ran while one was open for 1% of the time, Pallas kernels for 0%

commit v1 on v0

v1 whole, which is shorter than its diff:
```python
import functools
import math

import jax
import jax.numpy as jnp
from jax import lax
from jax.experimental import pallas as pl
from jax.experimental.pallas import tpu as pltpu
from jax.sharding import PartitionSpec as P

C = 512
RANK = 64
LEN = 1344
LAYERS = 2
DILATION = 64
PAD = 64
HALF = RANK // 2
F32 = jnp.float32
BF16 = jnp.bfloat16
HIGH = lax.Precision.HIGHEST
VMEM_LIMIT = 56 << 20


def first_bits(devices):
    bits = list(range(1, devices.bit_length() - 1))
    return bits, bits[1:] + bits[:1]


def dot_nn(a, b):
    return lax.dot_general(a, b, (((1,), (0,)), ((), ())), preferred_element_type=F32)


def dot_nt(a, b):
    return lax.dot_general(a, b, (((1,), (1,)), ((), ())), preferred_element_type=F32)


def dot_tn(a, b):
    return lax.dot_general(a, b, (((0,), (0,)), ((), ())), preferred_element_type=F32)


def split2(v):
    hi = v.astype(BF16)
    return hi, (v - hi.astype(F32)).astype(BF16)


def place(devices, which):
    me = lax.axis_index("dp")
    core = lax.rem(me, 2)
    layer = core if which == 0 else 1 - core
    orders = first_bits(devices)
    shift = jnp.where(layer == 0, orders[0][0], orders[1][0])
    return layer, (me >> shift) & 1


def kernel_sums(devices, which, x_hbm, o_hbm, e_hbm, q_ref, out_ref, x_buf, o_buf, e_buf, sems):
    layer, keep = place(devices, which)
    copies = [
        pltpu.make_async_copy(o_hbm.at[layer, 0], o_buf.at[pl.ds(0, LEN)], sems.at[0]),
        pltpu.make_async_copy(x_hbm.at[layer, 0], x_buf.at[pl.ds(0, LEN)], sems.at[1]),
        pltpu.make_async_copy(e_hbm.at[layer], e_buf, sems.at[2]),
    ]
    for copy in copies:
        copy.start()
    o_buf[pl.ds(LEN, PAD)] = jnp.zeros((PAD, C), BF16)
    x_buf[pl.ds(LEN, PAD)] = jnp.zeros((PAD, C), BF16)
    q_t = q_ref[layer].T * (1.0 / math.sqrt(devices))
    q_hi, q_rest = q_t.astype(BF16), None
    q_rest = q_t - q_hi.astype(F32)
    q_mid = q_rest.astype(BF16)
    q_low = (q_rest - q_mid.astype(F32)).astype(BF16)
    q_all = jnp.concatenate([q_hi, q_mid, q_low], axis=0)
    copies[0].wait()
    oq_all = dot_nt(q_all, o_buf[...])
    oq = (oq_all[:RANK] + oq_all[RANK : 2 * RANK] + oq_all[2 * RANK :]) * (1.0 / math.sqrt(LEN))
    spacing = (DILATION // 2) * (1 + layer)
    width = LEN + PAD
    pieces = []
    for shifted in (pltpu.roll(oq, width - spacing, 1), oq, pltpu.roll(oq, spacing, 1)):
        pieces.extend(split2(shifted))
    lhs = jnp.concatenate(pieces, axis=0)
    copies[1].wait()
    prod = dot_nn(lhs, x_buf[...])
    copies[2].wait()
    for k in range(3):
        eq_all = dot_nt(q_all, e_buf[pl.ds(k * C, C)])
        eq = eq_all[:RANK] + eq_all[RANK : 2 * RANK] + eq_all[2 * RANK :]
        total = prod[k * 128 : k * 128 + RANK] + prod[k * 128 + RANK : k * 128 + 128] + eq
        for half in range(2):
            slot = jnp.where(keep == half, 1, 0)
            out_ref[slot, k] = total[half * HALF : (half + 1) * HALF]


def sums(devices, which, x, o, e, q):
    any_spec = pl.BlockSpec(memory_space=pl.ANY)
    vmem = pl.BlockSpec(memory_space=pltpu.VMEM)
    return pl.pallas_call(
        functools.partial(kernel_sums, devices, which),
        out_shape=jax.ShapeDtypeStruct((2, 3, HALF, C), F32),
        in_specs=[any_spec, any_spec, any_spec, vmem],
        out_specs=vmem,
        scratch_shapes=[
            pltpu.VMEM((LEN + PAD, C), BF16),
            pltpu.VMEM((LEN + PAD, C), BF16),
            pltpu.VMEM((3 * C, C), BF16),
            pltpu.SemaphoreType.DMA((3,)),
        ],
        compiler_params=pltpu.CompilerParams(vmem_limit_bytes=VMEM_LIMIT),
        name=f"sums_{which}",
    )(x, o, e, q)


def kernel_grads(devices, which, x_hbm, o_hbm, e_hbm, tie_ref, g_ref, hi_ref, lo_ref, x_buf, o_buf, e_buf, sems):
    layer, _ = place(devices, which)
    copies = [
        pltpu.make_async_copy(x_hbm.at[layer, 0], x_buf, sems.at[0]),
        pltpu.make_async_copy(o_hbm.at[layer, 0], o_buf.at[pl.ds(PAD, LEN)], sems.at[1]),
        pltpu.make_async_copy(e_hbm.at[layer], e_buf, sems.at[2]),
    ]
    for copy in copies:
        copy.start()
    o_buf[pl.ds(0, PAD)] = jnp.zeros((PAD, C), BF16)
    o_buf[pl.ds(PAD + LEN, PAD)] = jnp.zeros((PAD, C), BF16)
    spacing = (DILATION // 2) * (1 + layer)
    for copy in copies:
        copy.wait()
    for k in range(3):
        start = pl.multiple_of(PAD - (k - 1) * spacing, 32)
        prod = dot_tn(x_buf[...], o_buf[pl.ds(start, LEN)])
        rows = pl.ds(k * C, C)
        g = prod * (1.0 / math.sqrt(LEN)) + e_buf[rows].astype(F32)
        g_ref[rows] = g
        hi, lo = split2(g)
        hi_ref[rows] = hi
        lo_ref[rows] = lo


def grads(devices, which, x, o, e, tie):
    any_spec = pl.BlockSpec(memory_space=pl.ANY)
    vmem = pl.BlockSpec(memory_space=pltpu.VMEM)
    return pl.pallas_call(
        functools.partial(kernel_grads, devices, which),
        out_shape=[
            jax.ShapeDtypeStruct((3 * C, C), F32),
            jax.ShapeDtypeStruct((3 * C, C), BF16),
            jax.ShapeDtypeStruct((3 * C, C), BF16),
        ],
        in_specs=[any_spec, any_spec, any_spec, any_spec],
        out_specs=[vmem, vmem, vmem],
        scratch_shapes=[
            pltpu.VMEM((LEN, C), BF16),
            pltpu.VMEM((LEN + 2 * PAD, C), BF16),
            pltpu.VMEM((3 * C, C), BF16),
            pltpu.SemaphoreType.DMA((3,)),
        ],
        compiler_params=pltpu.CompilerParams(vmem_limit_bytes=VMEM_LIMIT),
        name=f"grads_{which}",
    )(x, o, e, tie)


def kernel_right(devices, which, kept_ref, sent_ref, hi_ref, lo_ref, f_ref):
    _, keep = place(devices, which)
    acc = jnp.zeros((2 * RANK, C), F32)
    acc_low = jnp.zeros((RANK, C), F32)
    for k in range(3):
        s = jnp.concatenate([kept_ref[k], sent_ref[k]], axis=0)
        s_hi, s_lo = split2(s)
        rows = pl.ds(k * C, C)
        acc += dot_nn(jnp.concatenate([s_hi, s_lo], axis=0), hi_ref[rows])
        acc_low += dot_nn(s_hi, lo_ref[rows])
    f = acc[:RANK] + acc[RANK:] + acc_low
    f_ref[pl.ds(pl.multiple_of(keep * HALF, HALF), HALF)] = f[:HALF]
    f_ref[pl.ds(pl.multiple_of((1 - keep) * HALF, HALF), HALF)] = f[HALF:]


def right(devices, which, kept, sent, hi, lo):
    vmem = pl.BlockSpec(memory_space=pltpu.VMEM)
    return pl.pallas_call(
        functools.partial(kernel_right, devices, which),
        out_shape=jax.ShapeDtypeStruct((RANK, C), F32),
        in_specs=[vmem] * 4,
        out_specs=vmem,
        compiler_params=pltpu.CompilerParams(vmem_limit_bytes=VMEM_LIMIT),
        name=f"right_{which}",
    )(kept, sent, hi, lo)


def kernel_factor(devices, kept0_ref, sent0_ref, kept1_ref, sent1_ref, inv_ref, p_ref, pp0_ref, pp1_ref, s_buf):
    mats = []
    layers = []
    eye = (
        lax.broadcasted_iota(jnp.int32, (RANK, RANK), 0) == lax.broadcasted_iota(jnp.int32, (RANK, RANK), 1)
    ).astype(F32)
    for which, kept_ref, sent_ref in ((0, kept0_ref, sent0_ref), (1, kept1_ref, sent1_ref)):
        layer, keep = place(devices, which)
        layers.append(layer)
        for k in range(3):
            s_buf[which, k, pl.ds(pl.multiple_of(keep * HALF, HALF), HALF)] = kept_ref[k]
            s_buf[which, k, pl.ds(pl.multiple_of((1 - keep) * HALF, HALF), HALF)] = sent_ref[k]
        gram = jnp.zeros((RANK, RANK), F32)
        for k in range(3):
            s = s_buf[which, k]
            gram += lax.dot_general(s, s, (((1,), (1,)), ((), ())), precision=HIGH, preferred_element_type=F32)
        mats.append(jnp.concatenate([gram * (1.0 / (3 * C)), eye], axis=1))
    row_no = lax.broadcasted_iota(jnp.int32, (RANK, 1), 0)
    for j in range(RANK):
        for which in range(2):
            m = mats[which]
            row = m[j : j + 1, :]
            scaled = row / row[:, j : j + 1]
            col = jnp.where(row_no > j, m[:, j : j + 1], 0.0)
            mats[which] = m - col * scaled
    for which, pp_ref in ((0, pp0_ref), (1, pp1_ref)):
        m = mats[which]
        diag = jnp.sum(m[:, :RANK] * eye, axis=1, keepdims=True)
        inv = m[:, RANK:] * (1.0 / jnp.sqrt(diag))
        inv_ref[which] = inv
        for k in range(3):
            p_t = lax.dot_general(
                inv, s_buf[which, k], (((1,), (0,)), ((), ())), precision=HIGH, preferred_element_type=F32
            )
            p = p_t.T
            p_ref[layers[which], pl.ds(k * C, C)] = p
            hi, lo = split2(p)
            pp_ref[pl.ds(k * C, C)] = jnp.concatenate([hi, lo, hi], axis=1)


def factor(devices, kept0, sent0, kept1, sent1):
    vmem = pl.BlockSpec(memory_space=pltpu.VMEM)
    return pl.pallas_call(
        functools.partial(kernel_factor, devices),
        out_shape=[
            jax.ShapeDtypeStruct((LAYERS, RANK, RANK), F32),
            jax.ShapeDtypeStruct((LAYERS, 3 * C, RANK), F32),
            jax.ShapeDtypeStruct((3 * C, 3 * RANK), BF16),
            jax.ShapeDtypeStruct((3 * C, 3 * RANK), BF16),
        ],
        in_specs=[vmem] * 4,
        out_specs=[vmem] * 4,
        scratch_shapes=[pltpu.VMEM((LAYERS, 3, RANK, C), F32)],
        compiler_params=pltpu.CompilerParams(vmem_limit_bytes=VMEM_LIMIT),
        name="factor",
    )(kept0, sent0, kept1, sent1)


def kernel_errors(devices, f0_ref, f1_ref, inv_ref, pp0_ref, pp1_ref, g0_ref, g1_ref, factor_ref, err_hbm, err_buf, sems):
    norm = 1.0 / math.sqrt(3 * C * devices)
    copies = []
    for which, f_ref, pp_ref, g_ref in ((0, f0_ref, pp0_ref, g0_ref), (1, f1_ref, pp1_ref, g1_ref)):
        layer, _ = place(devices, which)
        f_t = (
            lax.dot_general(
                inv_ref[which], f_ref[...], (((1,), (0,)), ((), ())), precision=HIGH, preferred_element_type=F32
            )
            * norm
        )
        factor_ref[layer] = f_t.T
        hi, lo = split2(f_t * norm)
        rhs = jnp.concatenate([hi, hi, lo], axis=0)
        for k in range(3):
            rows = pl.ds(k * C, C)
            err_buf[which, rows] = (g_ref[rows] - dot_nn(pp_ref[rows], rhs)).astype(BF16)
            copy = pltpu.make_async_copy(err_buf.at[which, rows], err_hbm.at[layer, rows], sems.at[which, k])
            copy.start()
            copies.append(copy)
    for copy in copies:
        copy.wait()


def errors(devices, f0, f1, inv, pp0, pp1, g0, g1):
    vmem = pl.BlockSpec(memory_space=pltpu.VMEM)
    return pl.pallas_call(
        functools.partial(kernel_errors, devices),
        out_shape=[
            jax.ShapeDtypeStruct((LAYERS, C, RANK), F32),
            jax.ShapeDtypeStruct((LAYERS, 3 * C, C), BF16),
        ],
        in_specs=[vmem] * 7,
        out_specs=[vmem, pl.BlockSpec(memory_space=pl.ANY)],
        scratch_shapes=[pltpu.VMEM((LAYERS, 3 * C, C), BF16), pltpu.SemaphoreType.DMA((2, 3))],
        compiler_params=pltpu.CompilerParams(vmem_limit_bytes=VMEM_LIMIT),
        name="errors",
    )(f0, f1, inv, pp0, pp1, g0, g1)


def body(devices, x, o, e, q):
    orders = first_bits(devices)
    steps = len(orders[0])

    def swap_core(v):
        return lax.ppermute(v, "dp", [(i, i ^ 1) for i in range(devices)])

    def swap(v, step):
        return lax.ppermute(v, "dp", [(i, i ^ (1 << orders[i & 1][step])) for i in range(devices)])

    other = sums(devices, 1, x, o, e, q)
    got = swap_core(other)
    own = sums(devices, 0, x, o, e, q)
    chip = own + got
    part = chip[1] + swap(chip[0], 0)
    g0, hi0, lo0 = grads(devices, 0, x, o, e, own)
    g1, hi1, lo1 = grads(devices, 1, x, o, e, part)
    for step in range(1, steps):
        part = part + swap(part, step)
    kept0 = part
    sent0 = swap(part, 0)
    kept1 = swap_core(kept0)
    sent1 = swap_core(sent0)
    f0 = right(devices, 0, kept0, sent0, hi0, lo0)
    f1 = right(devices, 1, kept1, sent1, hi1, lo1)
    f0 = f0 + swap_core(f1)
    inv, panel, pp0, pp1 = factor(devices, kept0, sent0, kept1, sent1)
    for step in range(steps):
        f0 = f0 + swap(f0, step)
    f1 = swap_core(f0)
    factors, error = errors(devices, f0, f1, inv, pp0, pp1, g0, g1)
    return panel, factors, error


def solution(mesh):
    devices = mesh.shape["dp"]
    in_specs = (
        P(None, ("groups", "dp"), None, None),
        P(None, ("groups", "dp"), None, None),
        P(None, ("groups", "dp"), None),
        P(),
    )
    out_specs = (P("groups", None, None), P("groups", None, None), P(None, ("groups", "dp"), None))
    return jax.shard_map(
        functools.partial(body, devices), mesh=mesh, in_specs=in_specs, out_specs=out_specs, check_vma=False
    )
```

time: 265 us -> 108 us (0.41)
  waiting for transfers between devices: 181 us -> 31.2 us
  Pallas kernels: 0 us -> 50.8 us
  other arithmetic: 33.1 us -> 2.12 us
  matrix products: 28 us -> 0 us
  starting transfers between devices: 0.08 us -> 14.2 us
  between operations: 14.2 us -> 0.82 us
    psum x2 -> x0, waiting for transfers between devices: 181 us -> none  [the longest x1 94.8 us: body(): summed = lax.psum(panel_terms(), 'dp') / math.sqrt(devices)]
    pallas_call x0 -> x8, Pallas kernels: none -> 50.8 us  [the longest x2 15.5 us: grads(): pl.pallas_call(functools.partial(kernel_grads, devices, which), out_shape...]
    ppermute x0 -> x12, waiting for transfers between devices: none -> 31.2 us  [the longest x7 31.1 us: swap(): lax.ppermute(v, 'dp', [(i, i ^ 1 << orders[i & 1][step]) for i in range(d...]
    another operation x11 -> x0, other arithmetic: 29.1 us -> none  [the longest x4 12.4 us: orthogonal_rows(): lax.linalg.triangular_solve(lower_all[layer_no], shaped[:, layer_no], lef...]
    dot_general x9 -> x0, matrix products: 24.9 us -> none  [the longest x2 6.79 us: body(): lax.dot_general(grads_list[layer_no], panel_all[:, layer_no * RANK:(layer...]
    ppermute x0 -> x12, starting transfers between devices: none -> 14.2 us  [the longest x7 13.2 us: swap(): lax.ppermute(v, 'dp', [(i, i ^ 1 << orders[i & 1][step]) for i in range(d...]
    another operation x2 -> x0, matrix products: 3.1 us -> none  [orthogonal_rows(): lax.linalg.triangular_solve(lower_all[layer_no], shaped[:, layer_no], lef...]
    unnamed x18 -> x17, local copies, waits for them, and re-layouts: 5.36 us -> 8.03 us
  transfers between devices with their start and end apart: 2 -> 12, of which waited for: 2 -> 7; matrix products, arithmetic and copies ran while one was open for 1% -> 3% of each run, Pallas kernels for 0% -> 33%
where the time goes in v1:
time: 108 us; the launch traced here: 107 us
  Pallas kernels  50.8 us (47%)
  waiting for transfers between devices  31.2 us (29%)
  starting transfers between devices  14.2 us (13%)
  local copies, waits for them, and re-layouts  8.04 us (7%)
  other arithmetic  2.12 us (2%)
    ppermute x7, waiting for transfers between devices, swap(): lax.ppermute(v, 'dp', [(i, i ^ 1 << orders[i & 1][step]) for i in range(d...  31.1 us
    pallas_call x2, Pallas kernels, grads(): pl.pallas_call(functools.partial(kernel_grads, devices, which), out_shape...  15.5 us
    ppermute x7, starting transfers between devices, swap(): lax.ppermute(v, 'dp', [(i, i ^ 1 << orders[i & 1][step]) for i in range(d...  13.2 us
    pallas_call x1, Pallas kernels, factor(): pl.pallas_call(functools.partial(kernel_factor, devices), out_shape=[jax....  11.1 us
    pallas_call x2, Pallas kernels, sums(): pl.pallas_call(functools.partial(kernel_sums, devices, which), out_shape=...  10.8 us
    unnamed x17, local copies, waits for them, and re-layouts  8.03 us
    pallas_call x2, Pallas kernels, right(): pl.pallas_call(functools.partial(kernel_right, devices, which), out_shape...  6.79 us
    pallas_call x1, Pallas kernels, errors(): pl.pallas_call(functools.partial(kernel_errors, devices), out_shape=[jax....  6.69 us
  transfers between devices with their start and end apart: 12, of which 7 were waited for; matrix products, arithmetic and copies ran while one was open for 3% of the time, Pallas kernels for 33%

profile of v1, /device:TPU:0, one launch (start us, length us, event | category | flops | bytes accessed | tf_op | source)
XLA Modules:
  0.0 107.2 jit_solution(10220782801708856712)
XLA Ops:
  0.6 1.9 %copy.7.q_ref = f32[2,512,64]{2,1,0:T(8,128)} copy(f32[2,512,64]{1,2,0:T(8,128)} %param.7) | data formatting | bytes 524288 | tf_op args[3]
  2.6 5.4 %sums_1.1 = f32[2,3,32,512]{3,2,1,0:T(8,128)} custom-call(bf16[2,1,1344,512]{3,2,1,0:T(8,128)(2,1)} %x_hbm.7, bf16[2,1,1344,512]{3,2,1,0:T(8,128)(2,1)} %o_hbm.7, bf16[2,1536,512]{2,1,0:T(8,128)(2,1)} %e_hbm.7, f32[2,512,64]{2,1,0:T(8,128)} %copy.7.q_ref), custom_call_target="tpu_custom_call" | custom-call | tf_op jit(solution)/shard_map/sums_1/pallas_call | solution.py:96
  7.9 0.5 collective-permute-start
  8.5 5.4 %sums_0.1.tie_ref = f32[2,3,32,512]{3,2,1,0:T(8,128)} custom-call(bf16[2,1,1344,512]{3,2,1,0:T(8,128)(2,1)} %x_hbm.7, bf16[2,1,1344,512]{3,2,1,0:T(8,128)(2,1)} %o_hbm.7, bf16[2,1536,512]{2,1,0:T(8,128)(2,1)} %e_hbm.7, f32[2,512,64]{2,1,0:T(8,128)} %copy.7.q_ref), custom_call_target="tpu_custom_call" | custom-call | tf_op jit(solution)/shard_map/sums_0/pallas_call | solution.py:96
  13.9 0.0 collective-permute-done
  13.9 1.1 add.24
  15.0 2.6 %collective-permute-start.1 = (f32[3,32,512]{2,1,0:T(8,128)S(1)}, f32[3,32,512]{2,1,0:T(8,128)S(1)}, u32[]{:S(2)}, u32[]{:S(2)}) collective-permute-start(f32[3,32,512]{2,1,0:T(8,128)S(1)} %slice_bitcast_fusion), channel_id=1, source_target_pairs={{0,2},{1,5},{2,0},{3,7},{4,6},{5,1},{6,4},{7,3},{8,10},{9,13},{10,... | collective-permute-start | bytes 589832 | tf_op jit(solution)/shard_map/ppermute | solution.py:293
  17.5 3.6 %collective-permute-done.1 = f32[3,32,512]{2,1,0:T(8,128)S(1)} collective-permute-done((f32[3,32,512]{2,1,0:T(8,128)S(1)}, f32[3,32,512]{2,1,0:T(8,128)S(1)}, u32[]{:S(2)}, u32[]{:S(2)}) %collective-permute-start.1) | collective-permute-done | bytes 196640 | tf_op jit(solution)/shard_map/ppermute | solution.py:293
  21.2 0.0 copy-start.1
  21.2 2.2 %collective-permute-start.2 = (f32[3,32,512]{2,1,0:T(8,128)S(1)}, f32[3,32,512]{2,1,0:T(8,128)S(1)}, u32[]{:S(2)}, u32[]{:S(2)}) collective-permute-start(f32[3,32,512]{2,1,0:T(8,128)S(1)} %fusion.tie_ref), channel_id=1, source_target_pairs={{0,4},{1,9},{2,6},{3,11},{4,0},{5,13},{6,2},{7,15},{8,12},{9,1},{1... | collective-permute-start | bytes 589832 | tf_op jit(solution)/shard_map/ppermute | solution.py:293
  23.4 5.4 %collective-permute-done.2 = f32[3,32,512]{2,1,0:T(8,128)S(1)} collective-permute-done((f32[3,32,512]{2,1,0:T(8,128)S(1)}, f32[3,32,512]{2,1,0:T(8,128)S(1)}, u32[]{:S(2)}, u32[]{:S(2)}) %collective-permute-start.2) | collective-permute-done | bytes 196640 | tf_op jit(solution)/shard_map/ppermute | solution.py:293
  28.8 2.5 %collective-permute-start.3 = (f32[3,32,512]{2,1,0:T(8,128)S(1)}, f32[3,32,512]{2,1,0:T(8,128)S(1)}, u32[]{:S(2)}, u32[]{:S(2)}) collective-permute-start(f32[3,32,512]{2,1,0:T(8,128)S(1)} %add.26), channel_id=1, source_target_pairs={{0,8},{1,3},{2,10},{3,1},{4,12},{5,7},{6,14},{7,5},{8,0},{9,11},{1... | collective-permute-start | bytes 589832 | tf_op jit(solution)/shard_map/ppermute | solution.py:293
  31.3 6.4 %collective-permute-done.3 = f32[3,32,512]{2,1,0:T(8,128)S(1)} collective-permute-done((f32[3,32,512]{2,1,0:T(8,128)S(1)}, f32[3,32,512]{2,1,0:T(8,128)S(1)}, u32[]{:S(2)}, u32[]{:S(2)}) %collective-permute-start.3) | collective-permute-done | bytes 196640 | tf_op jit(solution)/shard_map/ppermute | solution.py:293
  37.7 0.0 copy-start
  37.7 1.6 %collective-permute-start.4 = (f32[3,32,512]{2,1,0:T(8,128)S(1)}, f32[3,32,512]{2,1,0:T(8,128)S(1)}, u32[]{:S(2)}, u32[]{:S(2)}) collective-permute-start(f32[3,32,512]{2,1,0:T(8,128)S(1)} %add.27.kept0_ref.kept_ref), channel_id=1, source_target_pairs={{0,2},{1,5},{2,0},{3,7},{4,6},{5,1},{6,4},{7,3},{8,10},{9,13},{10,... | collective-permute-start | bytes 589832 | tf_op jit(solution)/shard_map/ppermute | solution.py:293
  39.3 0.0 collective-permute-start.5
  39.3 4.2 %collective-permute-done.4.sent0_ref.sent_ref = f32[3,32,512]{2,1,0:T(8,128)S(1)} collective-permute-done((f32[3,32,512]{2,1,0:T(8,128)S(1)}, f32[3,32,512]{2,1,0:T(8,128)S(1)}, u32[]{:S(2)}, u32[]{:S(2)}) %collective-permute-start.4) | collective-permute-done | bytes 196640 | tf_op jit(solution)/shard_map/ppermute | solution.py:293
  43.4 0.0 collective-permute-start.6
  43.4 0.0 copy-done.1
  43.5 7.8 %grads_1.1 = (f32[1536,512]{1,0:T(8,128)}, bf16[1536,512]{1,0:T(8,128)(2,1)}, bf16[1536,512]{1,0:T(8,128)(2,1)}) custom-call(bf16[2,1,1344,512]{3,2,1,0:T(8,128)(2,1)} %x_hbm.7, bf16[2,1,1344,512]{3,2,1,0:T(8,128)(2,1)} %o_hbm.7, bf16[2,1536,512]{2,1,0:T(8,128)(2,1)} %e_hbm.7, f32[3,32,512]{2,1,0:T(8,128)} %copy-done.1), custom_call_target="tpu_custom_call" | custom-call | tf_op jit(solution)/shard_map/grads_1/pallas_call | solution.py:140
  51.3 0.0 copy-done
  51.3 0.0 copy-done.2
  51.3 0.0 collective-permute-done.5.kept1_ref.kept_ref
  51.3 0.0 copy-start.3
  51.3 0.0 collective-permute-done.6.sent1_ref.sent_ref
  51.3 0.0 copy-start.4
  51.3 0.7 copy-done.3
  52.0 0.1 copy-done.4
  52.0 3.4 %right_1.1 = f32[64,512]{1,0:T(8,128)} custom-call(f32[3,32,512]{2,1,0:T(8,128)} %copy-done.3, f32[3,32,512]{2,1,0:T(8,128)} %copy-done.4, bf16[1536,512]{1,0:T(8,128)(2,1)} %get-tuple-element.18.hi_ref, bf16[1536,512]{1,0:T(8,128)(2,1)} %get-tuple-element.19.lo_ref), custom_call_target="tpu_custom_call" | custom-call | tf_op jit(solution)/shard_map/right_1/pallas_call | solution.py:177
  55.4 0.4 collective-permute-start.7
  55.9 7.7 %grads_0.1 = (f32[1536,512]{1,0:T(8,128)}, bf16[1536,512]{1,0:T(8,128)(2,1)}, bf16[1536,512]{1,0:T(8,128)(2,1)}) custom-call(bf16[2,1,1344,512]{3,2,1,0:T(8,128)(2,1)} %x_hbm.7, bf16[2,1,1344,512]{3,2,1,0:T(8,128)(2,1)} %o_hbm.7, bf16[2,1536,512]{2,1,0:T(8,128)(2,1)} %e_hbm.7, f32[2,3,32,512]{3,2,1,0:T(8,128)} %sums_0.1.tie_ref), custom_call_target="tpu_custom_call" | custom-call | tf_op jit(solution)/shard_map/grads_0/pallas_call | solution.py:140
  63.6 3.4 %right_0.1 = f32[64,512]{1,0:T(8,128)} custom-call(f32[3,32,512]{2,1,0:T(8,128)} %copy-done, f32[3,32,512]{2,1,0:T(8,128)} %copy-done.2, bf16[1536,512]{1,0:T(8,128)(2,1)} %get-tuple-element.16.hi_ref, bf16[1536,512]{1,0:T(8,128)(2,1)} %get-tuple-element.17.lo_ref), custom_call_target="tpu_custom_call" | custom-call | tf_op jit(solution)/shard_map/right_0/pallas_call | solution.py:177
  67.0 0.0 collective-permute-done.7
  67.0 0.9 add.28
  67.9 1.5 %collective-permute-start.8 = (f32[64,512]{1,0:T(8,128)S(1)}, f32[64,512]{1,0:T(8,128)S(1)}, u32[]{:S(2)}, u32[]{:S(2)}) collective-permute-start(f32[64,512]{1,0:T(8,128)S(1)} %add.28), channel_id=1, source_target_pairs={{0,2},{1,5},{2,0},{3,7},{4,6},{5,1},{6,4},{7,3},{8,10},{9,13},{10,... | collective-permute-start | bytes 393224 | tf_op jit(solution)/shard_map/ppermute | solution.py:293
  69.5 3.5 %collective-permute-done.8 = f32[64,512]{1,0:T(8,128)S(1)} collective-permute-done((f32[64,512]{1,0:T(8,128)S(1)}, f32[64,512]{1,0:T(8,128)S(1)}, u32[]{:S(2)}, u32[]{:S(2)}) %collective-permute-start.8) | collective-permute-done | bytes 131104 | tf_op jit(solution)/shard_map/ppermute | solution.py:293
  73.0 0.5 collective-permute-start.9
  73.4 4.6 %collective-permute-done.9 = f32[64,512]{1,0:T(8,128)S(1)} collective-permute-done((f32[64,512]{1,0:T(8,128)S(1)}, f32[64,512]{1,0:T(8,128)S(1)}, u32[]{:S(2)}, u32[]{:S(2)}) %collective-permute-start.9) | collective-permute-done | bytes 131104 | tf_op jit(solution)/shard_map/ppermute | solution.py:293
  78.0 2.4 %collective-permute-start.10 = (f32[64,512]{1,0:T(8,128)S(1)}, f32[64,512]{1,0:T(8,128)S(1)}, u32[]{:S(2)}, u32[]{:S(2)}) collective-permute-start(f32[64,512]{1,0:T(8,128)S(1)} %add.30), channel_id=1, source_target_pairs={{0,8},{1,3},{2,10},{3,1},{4,12},{5,7},{6,14},{7,5},{8,0},{9,11},{1... | collective-permute-start | bytes 393224 | tf_op jit(solution)/shard_map/ppermute | solution.py:293
  80.5 3.5 %collective-permute-done.10 = f32[64,512]{1,0:T(8,128)S(1)} collective-permute-done((f32[64,512]{1,0:T(8,128)S(1)}, f32[64,512]{1,0:T(8,128)S(1)}, u32[]{:S(2)}, u32[]{:S(2)}) %collective-permute-start.10) | collective-permute-done | bytes 131104 | tf_op jit(solution)/shard_map/ppermute | solution.py:293
  84.0 0.1 collective-permute-start.11
  84.1 11.1 %factor.1 = (f32[2,64,64]{2,1,0:T(8,128)}, f32[2,1536,64]{2,1,0:T(8,128)}, bf16[1536,192]{1,0:T(8,128)(2,1)}, bf16[1536,192]{1,0:T(8,128)(2,1)}) custom-call(f32[3,32,512]{2,1,0:T(8,128)} %copy-done, f32[3,32,512]{2,1,0:T(8,128)} %copy-done.2, f32[3,32,512]{2,1,0:T(8,128)} %copy-done.3, f32[3,32,512]{2,1,0:T(8,128)} %copy-done.4), custom_call_target="tpu_custom_call" | custom-call | tf_op jit(solution)/shard_map/factor/pallas_call | solution.py:229
  95.2 2.7 %copy.9 = f32[2,1536,64]{1,2,0:T(8,128)} copy(f32[2,1536,64]{2,1,0:T(8,128)} %get-tuple-element.27) | data formatting | bytes 1572864
  97.9 0.0 collective-permute-done.11.f1_ref
  97.9 0.0 copy-done.5
  97.9 0.6 copy-done.6
  98.6 6.7 %errors.1 = (f32[2,512,64]{2,1,0:T(8,128)}, bf16[2,1536,512]{2,1,0:T(8,128)(2,1)}) custom-call(f32[64,512]{1,0:T(8,128)} %copy-done.5, f32[64,512]{1,0:T(8,128)} %copy-done.6, f32[2,64,64]{2,1,0:T(8,128)} %get-tuple-element.20.inv_ref, bf16[1536,192]{1,0:T(8,128)(2,1)} %get-tuple-element.21.pp0_ref, bf16[1536,192]{1,0:T(8,128)(2,1)} %get-tuple-element.22.pp1_ref, ...), custom_call_target="tpu_custom_call" | custom-call | tf_op jit(solution)/shard_map/errors/pallas_call | solution.py:271
  105.2 1.9 %copy.10 = f32[2,512,64]{1,2,0:T(8,128)} copy(f32[2,512,64]{2,1,0:T(8,128)} %get-tuple-element.28) | data formatting | bytes 524288
  (10 shorter events, 0.2 us)
Async XLA Ops:
  7.9 5.9 %collective-permute-start = (f32[2,3,32,512]{3,2,1,0:T(8,128)}, f32[2,3,32,512]{3,2,1,0:T(8,128)S(1)}, u32[]{:S(2)}, u32[]{:S(2)}) collective-permute-start(f32[2,3,32,512]{3,2,1,0:T(8,128)} %sums_1.1), channel_id=1, source_target_pairs={{0,1},{1,0},{2,3},{3,2},{4,5},{5,4},{6,7},{7,6},{8,9},{9,8},{10,11... | collective-permute-start | bytes 1179656 | tf_op jit(solution)/shard_map/ppermute | solution.py:290
  15.0 6.2 %collective-permute-start.1 = (f32[3,32,512]{2,1,0:T(8,128)S(1)}, f32[3,32,512]{2,1,0:T(8,128)S(1)}, u32[]{:S(2)}, u32[]{:S(2)}) collective-permute-start(f32[3,32,512]{2,1,0:T(8,128)S(1)} %slice_bitcast_fusion), channel_id=1, source_target_pairs={{0,2},{1,5},{2,0},{3,7},{4,6},{5,1},{6,4},{7,3},{8,10},{9,13},{10,... | collective-permute-start | bytes 589832 | tf_op jit(solution)/shard_map/ppermute | solution.py:293
  21.2 22.2 %copy-start.1 = (f32[3,32,512]{2,1,0:T(8,128)}, f32[3,32,512]{2,1,0:T(8,128)S(1)}, u32[]{:S(2)}) copy-start(f32[3,32,512]{2,1,0:T(8,128)S(1)} %fusion.tie_ref) | copy-start | bytes 589828
  21.2 7.6 %collective-permute-start.2 = (f32[3,32,512]{2,1,0:T(8,128)S(1)}, f32[3,32,512]{2,1,0:T(8,128)S(1)}, u32[]{:S(2)}, u32[]{:S(2)}) collective-permute-start(f32[3,32,512]{2,1,0:T(8,128)S(1)} %fusion.tie_ref), channel_id=1, source_target_pairs={{0,4},{1,9},{2,6},{3,11},{4,0},{5,13},{6,2},{7,15},{8,12},{9,1},{1... | collective-permute-start | bytes 589832 | tf_op jit(solution)/shard_map/ppermute | solution.py:293
  28.8 8.8 %collective-permute-start.3 = (f32[3,32,512]{2,1,0:T(8,128)S(1)}, f32[3,32,512]{2,1,0:T(8,128)S(1)}, u32[]{:S(2)}, u32[]{:S(2)}) collective-permute-start(f32[3,32,512]{2,1,0:T(8,128)S(1)} %add.26), channel_id=1, source_target_pairs={{0,8},{1,3},{2,10},{3,1},{4,12},{5,7},{6,14},{7,5},{8,0},{9,11},{1... | collective-permute-start | bytes 589832 | tf_op jit(solution)/shard_map/ppermute | solution.py:293
  37.7 13.6 %copy-start = (f32[3,32,512]{2,1,0:T(8,128)}, f32[3,32,512]{2,1,0:T(8,128)S(1)}, u32[]{:S(2)}) copy-start(f32[3,32,512]{2,1,0:T(8,128)S(1)} %add.27.kept0_ref.kept_ref) | copy-start | bytes 589828
  37.7 5.7 %collective-permute-start.4 = (f32[3,32,512]{2,1,0:T(8,128)S(1)}, f32[3,32,512]{2,1,0:T(8,128)S(1)}, u32[]{:S(2)}, u32[]{:S(2)}) collective-permute-start(f32[3,32,512]{2,1,0:T(8,128)S(1)} %add.27.kept0_ref.kept_ref), channel_id=1, source_target_pairs={{0,2},{1,5},{2,0},{3,7},{4,6},{5,1},{6,4},{7,3},{8,10},{9,13},{10,... | collective-permute-start | bytes 589832 | tf_op jit(solution)/shard_map/ppermute | solution.py:293
  39.3 12.0 %collective-permute-start.5 = (f32[3,32,512]{2,1,0:T(8,128)S(1)}, f32[3,32,512]{2,1,0:T(8,128)S(1)}, u32[]{:S(2)}, u32[]{:S(2)}) collective-permute-start(f32[3,32,512]{2,1,0:T(8,128)S(1)} %add.27.kept0_ref.kept_ref), channel_id=1, source_target_pairs={{0,1},{1,0},{2,3},{3,2},{4,5},{5,4},{6,7},{7,6},{8,9},{9,8},{10,11... | collective-permute-start | bytes 589832 | tf_op jit(solution)/shard_map/ppermute | solution.py:290
  43.4 7.8 %copy-start.2 = (f32[3,32,512]{2,1,0:T(8,128)}, f32[3,32,512]{2,1,0:T(8,128)S(1)}, u32[]{:S(2)}) copy-start(f32[3,32,512]{2,1,0:T(8,128)S(1)} %collective-permute-done.4.sent0_ref.sent_ref) | copy-start | bytes 589828
  43.4 7.8 %collective-permute-start.6 = (f32[3,32,512]{2,1,0:T(8,128)S(1)}, f32[3,32,512]{2,1,0:T(8,128)S(1)}, u32[]{:S(2)}, u32[]{:S(2)}) collective-permute-start(f32[3,32,512]{2,1,0:T(8,128)S(1)} %collective-permute-done.4.sent0_ref.sent_ref), channel_id=1, source_target_pairs={{0,1},{1,0},{2,3},{3,2},{4,5},{5,4},{6,7},{7,6},{8,9},{9,8},{10,11... | collective-permute-start | bytes 589832 | tf_op jit(solution)/shard_map/ppermute | solution.py:290
  51.3 0.7 copy-start.3
  51.3 0.7 copy-start.4
  55.4 11.5 %collective-permute-start.7 = (f32[64,512]{1,0:T(8,128)}, f32[64,512]{1,0:T(8,128)S(1)}, u32[]{:S(2)}, u32[]{:S(2)}) collective-permute-start(f32[64,512]{1,0:T(8,128)} %right_1.1), channel_id=1, source_target_pairs={{0,1},{1,0},{2,3},{3,2},{4,5},{5,4},{6,7},{7,6},{8,9},{9,8},{10,11... | collective-permute-start | bytes 393224 | tf_op jit(solution)/shard_map/ppermute | solution.py:290
  67.9 5.0 %collective-permute-start.8 = (f32[64,512]{1,0:T(8,128)S(1)}, f32[64,512]{1,0:T(8,128)S(1)}, u32[]{:S(2)}, u32[]{:S(2)}) collective-permute-start(f32[64,512]{1,0:T(8,128)S(1)} %add.28), channel_id=1, source_target_pairs={{0,2},{1,5},{2,0},{3,7},{4,6},{5,1},{6,4},{7,3},{8,10},{9,13},{10,... | collective-permute-start | bytes 393224 | tf_op jit(solution)/shard_map/ppermute | solution.py:293
  73.0 5.0 %collective-permute-start.9 = (f32[64,512]{1,0:T(8,128)S(1)}, f32[64,512]{1,0:T(8,128)S(1)}, u32[]{:S(2)}, u32[]{:S(2)}) collective-permute-start(f32[64,512]{1,0:T(8,128)S(1)} %add.29), channel_id=1, source_target_pairs={{0,4},{1,9},{2,6},{3,11},{4,0},{5,13},{6,2},{7,15},{8,12},{9,1},{1... | collective-permute-start | bytes 393224 | tf_op jit(solution)/shard_map/ppermute | solution.py:293
  78.0 5.9 %collective-permute-start.10 = (f32[64,512]{1,0:T(8,128)S(1)}, f32[64,512]{1,0:T(8,128)S(1)}, u32[]{:S(2)}, u32[]{:S(2)}) collective-permute-start(f32[64,512]{1,0:T(8,128)S(1)} %add.30), channel_id=1, source_target_pairs={{0,8},{1,3},{2,10},{3,1},{4,12},{5,7},{6,14},{7,5},{8,0},{9,11},{1... | collective-permute-start | bytes 393224 | tf_op jit(solution)/shard_map/ppermute | solution.py:293
  84.0 13.9 %copy-start.5 = (f32[64,512]{1,0:T(8,128)}, f32[64,512]{1,0:T(8,128)S(1)}, u32[]{:S(2)}) copy-start(f32[64,512]{1,0:T(8,128)S(1)} %add.31.f0_ref) | copy-start | bytes 393220
  84.0 13.9 %collective-permute-start.11 = (f32[64,512]{1,0:T(8,128)S(1)}, f32[64,512]{1,0:T(8,128)S(1)}, u32[]{:S(2)}, u32[]{:S(2)}) collective-permute-start(f32[64,512]{1,0:T(8,128)S(1)} %add.31.f0_ref), channel_id=1, source_target_pairs={{0,1},{1,0},{2,3},{3,2},{4,5},{5,4},{6,7},{7,6},{8,9},{9,8},{10,11... | collective-permute-start | bytes 393224 | tf_op jit(solution)/shard_map/ppermute | solution.py:290
  97.9 0.7 copy-start.6

commit v2 on v0

v2 whole, which is shorter than its diff:
```python
import functools
import math

import jax
import jax.numpy as jnp
from jax import lax
from jax.experimental import pallas as pl
from jax.experimental.pallas import tpu as pltpu
from jax.sharding import PartitionSpec as P

C = 512
RANK = 64
LEN = 1344
LAYERS = 2
DILATION = 64
PAD = 64
STREAMS = 2
PART = RANK // (2 * STREAMS)
F32 = jnp.float32
BF16 = jnp.bfloat16
HIGH = lax.Precision.HIGHEST
VMEM_LIMIT = 14 << 20
CUTS = (18, 44)
PLAN = [((0, 0), (0, 1)), ((0, 2), (1, 0)), ((1, 1), (1, 2))]


def exchange_bits(devices):
    bits = list(range(1, devices.bit_length() - 1))
    return bits, bits[1:] + bits[:1]


def dot_nn(a, b):
    return lax.dot_general(a, b, (((1,), (0,)), ((), ())), preferred_element_type=F32)


def dot_nt(a, b):
    return lax.dot_general(a, b, (((1,), (1,)), ((), ())), preferred_element_type=F32)


def dot_tn(a, b):
    return lax.dot_general(a, b, (((0,), (0,)), ((), ())), preferred_element_type=F32)


def split2(v):
    hi = v.astype(BF16)
    return hi, (v - hi.astype(F32)).astype(BF16)


def place(which):
    core = lax.rem(lax.axis_index("dp"), 2)
    return core if which == 0 else 1 - core


def kept(devices, layer):
    orders = exchange_bits(devices)
    return (lax.axis_index("dp") >> jnp.where(layer == 0, orders[0][0], orders[1][0])) & 1


def spec(space):
    return pl.BlockSpec(memory_space=space)


def local(v):
    return pltpu.with_memory_space_constraint(v, pltpu.VMEM)


def far(v):
    return pltpu.with_memory_space_constraint(v, pltpu.HBM)


def cost(flops, nbytes):
    return pl.CostEstimate(flops=flops, transcendentals=0, bytes_accessed=nbytes)


def layer_sum(devices, layer, q_ref, x_ref, o_ref, e_ref, waits, out_ref):
    keep = kept(devices, layer)
    q_t = q_ref[layer] * (1.0 / math.sqrt(devices))
    q_hi = q_t.astype(BF16)
    q_mid, q_low = split2(q_t - q_hi.astype(F32))
    q_all = jnp.concatenate([q_hi, q_mid, q_low], axis=0)
    waits[0]()
    oq_all = dot_nt(q_all, o_ref[pl.ds(PAD, LEN + PAD)])
    oq = (oq_all[:RANK] + oq_all[RANK : 2 * RANK] + oq_all[2 * RANK :]) * (1.0 / math.sqrt(LEN))
    spacing = (DILATION // 2) * (1 + layer)
    width = LEN + PAD
    pieces = []
    for shifted in (pltpu.roll(oq, width - spacing, 1), oq, pltpu.roll(oq, spacing, 1)):
        pieces.extend(split2(shifted))
    lhs = jnp.concatenate(pieces, axis=0)
    waits[1]()
    prod = dot_nn(lhs, x_ref[...])
    waits[2]()
    for k in range(3):
        eq_all = dot_nt(q_all, e_ref[pl.ds(k * C, C)])
        eq = eq_all[:RANK] + eq_all[RANK : 2 * RANK] + eq_all[2 * RANK :]
        total = prod[k * 128 : k * 128 + RANK] + prod[k * 128 + RANK : k * 128 + 128] + eq
        for i in range(2 * STREAMS):
            slot = jnp.where(keep == i % 2, 1, 0)
            out_ref[slot, i // 2, k] = total[i * PART : (i + 1) * PART]


def kernel_load(devices, x_hbm, o_hbm, e_hbm, q_hbm, out_ref, x1, o1, e1, x0, o0, e0, q_ref, sems):
    copies = [pltpu.make_async_copy(q_hbm, q_ref, sems.at[2, 0])]
    for which, x_ref, o_ref, e_ref in ((1, x1, o1, e1), (0, x0, o0, e0)):
        layer = place(which)
        copies += [
            pltpu.make_async_copy(o_hbm.at[layer, 0], o_ref.at[pl.ds(PAD, LEN)], sems.at[which, 0]),
            pltpu.make_async_copy(x_hbm.at[layer, 0], x_ref.at[pl.ds(0, LEN)], sems.at[which, 1]),
            pltpu.make_async_copy(e_hbm.at[layer], e_ref, sems.at[which, 2]),
        ]
    for copy in copies:
        copy.start()
    zeros = jnp.zeros((PAD, C), BF16)
    for x_ref, o_ref in ((x1, o1), (x0, o0)):
        o_ref[pl.ds(0, PAD)] = zeros
        o_ref[pl.ds(PAD + LEN, PAD)] = zeros
        x_ref[pl.ds(LEN, PAD)] = zeros
    copies[0].wait()
    layer_sum(devices, place(1), q_ref, x1, o1, e1, [copy.wait for copy in copies[1:4]], out_ref)
    for copy in copies[4:]:
        copy.wait()


def load(devices, x, o, e, q):
    return pl.pallas_call(
        functools.partial(kernel_load, devices),
        out_shape=[
            pltpu.VMEM((2, STREAMS, 3, PART, C), F32),
            pltpu.VMEM((LEN + PAD, C), BF16),
            pltpu.VMEM((LEN + 2 * PAD, C), BF16),
            pltpu.VMEM((3 * C, C), BF16),
            pltpu.VMEM((LEN + PAD, C), BF16),
            pltpu.VMEM((LEN + 2 * PAD, C), BF16),
            pltpu.VMEM((3 * C, C), BF16),
            pltpu.VMEM((LAYERS, RANK, C), F32),
        ],
        in_specs=[spec(pltpu.HBM)] * 4,
        out_specs=[spec(pltpu.VMEM)] * 8,
        scratch_shapes=[pltpu.SemaphoreType.DMA((3, 3))],
        compiler_params=pltpu.CompilerParams(vmem_limit_bytes=VMEM_LIMIT),
        cost_estimate=cost(2 * 10**9, 9 * 10**6),
        name="load",
    )(far(x), far(o), far(e), far(q))


def kernel_sums(devices, q_ref, x_ref, o_ref, e_ref, out_ref):
    layer_sum(devices, place(0), q_ref, x_ref, o_ref, e_ref, [lambda: None] * 3, out_ref)


def sums(devices, q, x, o, e):
    return pl.pallas_call(
        functools.partial(kernel_sums, devices),
        out_shape=pltpu.VMEM((2, STREAMS, 3, PART, C), F32),
        in_specs=[spec(pltpu.VMEM)] * 4,
        out_specs=spec(pltpu.VMEM),
        compiler_params=pltpu.CompilerParams(vmem_limit_bytes=VMEM_LIMIT),
        cost_estimate=cost(2 * 10**9, 4 * 10**6),
        name="sums",
    )(local(q), local(x), local(o), local(e))


def kernel_grads(parts, *refs):
    ins, outs = refs[: 3 * len(parts)], refs[3 * len(parts) + 1 :]
    for i, (which, k) in enumerate(parts):
        x_ref, o_ref, e_ref = ins[3 * i : 3 * i + 3]
        g_ref, hi_ref, lo_ref = outs[3 * i : 3 * i + 3]
        spacing = (DILATION // 2) * (1 + place(which))
        start = pl.multiple_of(PAD - (k - 1) * spacing, 32)
        prod = dot_tn(x_ref[pl.ds(0, LEN)], o_ref[pl.ds(start, LEN)])
        g = prod * (1.0 / math.sqrt(LEN)) + e_ref[pl.ds(k * C, C)].astype(F32)
        g_ref[...] = g
        hi_ref[...], lo_ref[...] = split2(g)
    outs[-1][...] = jnp.zeros_like(outs[-1])


def grads(parts, arrays, tie):
    ins = [local(v) for which, _ in parts for v in arrays[which]]
    block = [pltpu.VMEM((C, C), F32), pltpu.VMEM((C, C), BF16), pltpu.VMEM((C, C), BF16)]
    out = pl.pallas_call(
        functools.partial(kernel_grads, parts),
        out_shape=block * len(parts) + [pltpu.VMEM((3, PART, C), F32)],
        in_specs=[spec(pltpu.VMEM)] * len(ins) + [spec(pl.ANY)],
        out_specs=[spec(pltpu.VMEM)] * (3 * len(parts) + 1),
        compiler_params=pltpu.CompilerParams(vmem_limit_bytes=VMEM_LIMIT),
        cost_estimate=cost(10**9 * len(parts), 3 * 10**6 * len(parts)),
        name="grads_" + "_".join(f"{which}{k}" for which, k in parts),
    )(*ins, tie)
    return {part: out[3 * i : 3 * i + 3] for i, part in enumerate(parts)}, out[-1]


def gather_parts(devices, which, part_refs, k):
    keep = kept(devices, place(which))
    rows = [(2 * (i // 2) + (keep if i % 2 == 0 else 1 - keep)) * PART for i in range(2 * STREAMS)]
    return [ref[k] for ref in part_refs], [pl.multiple_of(row, PART) for row in rows]


def kernel_right(devices, which, *refs):
    part_refs, his, los, f_ref = refs[: 2 * STREAMS], refs[2 * STREAMS :][:3], refs[2 * STREAMS + 3 :][:3], refs[-1]
    acc = jnp.zeros((2 * RANK, C), F32)
    acc_low = jnp.zeros((RANK, C), F32)
    for k in range(3):
        parts, rows = gather_parts(devices, which, part_refs, k)
        s_hi, s_lo = split2(jnp.concatenate(parts, axis=0))
        acc += dot_nn(jnp.concatenate([s_hi, s_lo], axis=0), his[k][...])
        acc_low += dot_nn(s_hi, los[k][...])
    f = acc[:RANK] + acc[RANK:] + acc_low
    for i, row in enumerate(rows):
        f_ref[pl.ds(row, PART)] = f[i * PART : (i + 1) * PART]


def right(devices, which, parts, blocks):
    his = [local(blocks[which, k][1]) for k in range(3)]
    los = [local(blocks[which, k][2]) for k in range(3)]
    return pl.pallas_call(
        functools.partial(kernel_right, devices, which),
        out_shape=pltpu.VMEM((RANK, C), F32),
        in_specs=[spec(pltpu.VMEM)] * (2 * STREAMS + 6),
        out_specs=spec(pltpu.VMEM),
        compiler_params=pltpu.CompilerParams(vmem_limit_bytes=VMEM_LIMIT),
        cost_estimate=cost(10**9, 4 * 10**6),
        name=f"right_{which}",
    )(*parts, *his, *los)


def eliminate(mats, first, last):
    row_no = lax.broadcasted_iota(jnp.int32, (RANK, 1), 0)
    mats = list(mats)
    for j in range(first, last):
        for which in range(2):
            m = mats[which]
            row = m[j : j + 1, :]
            scaled = row / row[:, j : j + 1]
            col = jnp.where(row_no > j, m[:, j : j + 1], 0.0)
            mats[which] = m - col * scaled
    return mats


def kernel_gram(devices, last, *refs):
    s_ref, m_ref, token_ref = refs[-3:]
    mats = []
    eye = (
        lax.broadcasted_iota(jnp.int32, (RANK, RANK), 0) == lax.broadcasted_iota(jnp.int32, (RANK, RANK), 1)
    ).astype(F32)
    for which in range(2):
        for k in range(3):
            parts, rows = gather_parts(devices, which, refs[which * 2 * STREAMS :][: 2 * STREAMS], k)
            for part, row in zip(parts, rows):
                s_ref[which, k, pl.ds(row, PART)] = part
        gram = jnp.zeros((RANK, RANK), F32)
        for k in range(3):
            s = s_ref[which, k]
            gram += lax.dot_general(s, s, (((1,), (1,)), ((), ())), precision=HIGH, preferred_element_type=F32)
        mats.append(jnp.concatenate([gram * (1.0 / (3 * C)), eye], axis=1))
    mats = eliminate(mats, 0, last)
    for which in range(2):
        m_ref[which] = mats[which]
    token_ref[...] = jnp.zeros_like(token_ref)


def gram(devices, last, parts, tie):
    return pl.pallas_call(
        functools.partial(kernel_gram, devices, last),
        out_shape=[
            pltpu.VMEM((LAYERS, 3, RANK, C), F32),
            pltpu.VMEM((LAYERS, RANK, 2 * RANK), F32),
            pltpu.VMEM((RANK, C), F32),
        ],
        in_specs=[spec(pltpu.VMEM)] * len(parts) + [spec(pl.ANY)],
        out_specs=[spec(pltpu.VMEM)] * 3,
        compiler_params=pltpu.CompilerParams(vmem_limit_bytes=VMEM_LIMIT),
        cost_estimate=cost(2 * 10**9, 10 * 10**6),
        name="gram",
    )(*parts, tie)


def kernel_middle(first, last, m_ref, tie_ref, out_ref, token_ref):
    mats = eliminate([m_ref[0], m_ref[1]], first, last)
    for which in range(2):
        out_ref[which] = mats[which]
    token_ref[...] = jnp.zeros_like(token_ref)


def middle(first, last, m, tie):
    return pl.pallas_call(
        functools.partial(kernel_middle, first, last),
        out_shape=[pltpu.VMEM((LAYERS, RANK, 2 * RANK), F32), pltpu.VMEM((RANK, C), F32)],
        in_specs=[spec(pltpu.VMEM), spec(pl.ANY)],
        out_specs=[spec(pltpu.VMEM)] * 2,
        compiler_params=pltpu.CompilerParams(vmem_limit_bytes=VMEM_LIMIT),
        cost_estimate=cost(2 * 10**9, 10 * 10**6),
        name=f"middle_{first}",
    )(local(m), tie)


def kernel_panels(first, s_ref, m_ref, tie_ref, inv_ref, p_ref, pp_ref, token_ref):
    mats = eliminate([m_ref[0], m_ref[1]], first, RANK)
    eye = (
        lax.broadcasted_iota(jnp.int32, (RANK, RANK), 0) == lax.broadcasted_iota(jnp.int32, (RANK, RANK), 1)
    ).astype(F32)
    for which in range(2):
        layer = place(which)
        m = mats[which]
        diag = jnp.sum(m[:, :RANK] * eye, axis=1, keepdims=True)
        inv = m[:, RANK:] * (1.0 / jnp.sqrt(diag))
        inv_ref[which] = inv
        for k in range(3):
            p_t = lax.dot_general(
                inv, s_ref[which, k], (((1,), (0,)), ((), ())), precision=HIGH, preferred_element_type=F32
            )
            p_ref[layer, :, pl.ds(k * C, C)] = p_t
            hi, lo = split2(p_t.T)
            pp_ref[which, pl.ds(k * C, C)] = jnp.concatenate([hi, lo, hi], axis=1)
    token_ref[...] = jnp.zeros_like(token_ref)


def panels(first, s, m, tie):
    return pl.pallas_call(
        functools.partial(kernel_panels, first),
        out_shape=[
            pltpu.VMEM((LAYERS, RANK, RANK), F32),
            jax.ShapeDtypeStruct((LAYERS, RANK, 3 * C), F32),
            pltpu.VMEM((LAYERS, 3 * C, 3 * RANK), BF16),
            pltpu.VMEM((RANK, C), F32),
        ],
        in_specs=[spec(pltpu.VMEM), spec(pltpu.VMEM), spec(pl.ANY)],
        out_specs=[spec(pltpu.VMEM)] * 4,
        compiler_params=pltpu.CompilerParams(vmem_limit_bytes=VMEM_LIMIT),
        cost_estimate=cost(2 * 10**9, 10 * 10**6),
        name="panels",
    )(local(s), local(m), tie)


def layer_error(devices, which, f_ref, inv_ref, pp_ref, g_refs, err_ref, each):
    norm = 1.0 / math.sqrt(3 * C * devices)
    f_t = (
        lax.dot_general(
            inv_ref[which], f_ref[...], (((1,), (0,)), ((), ())), precision=HIGH, preferred_element_type=F32
        )
        * norm
    )
    hi, lo = split2(f_t * norm)
    rhs = jnp.concatenate([hi, hi, lo], axis=0)
    for k in range(3):
        rows = pl.ds(k * C, C)
        err_ref[rows] = (g_refs[k][...] - dot_nn(pp_ref[which, rows], rhs)).astype(BF16)
        each(k)
    return f_t


def kernel_own_error(devices, f_ref, inv_ref, pp_ref, g0, g1, g2, factor_ref, err_ref):
    factor_ref[...] = layer_error(devices, 0, f_ref, inv_ref, pp_ref, (g0, g1, g2), err_ref, lambda k: None)


def kernel_errors(devices, f_ref, inv_ref, pp_ref, g0, g1, g2, own_factor, own_err, factor_ref, err_hbm, err_ref, sems):
    copies = []

    def write(source, which, k):
        rows = pl.ds(k * C, C)
        copy = pltpu.make_async_copy(source.at[rows], err_hbm.at[place(which), rows], sems.at[which, k])
        copy.start()
        copies.append(copy)

    for k in range(3):
        write(own_err, 0, k)
    factor_ref[place(0)] = own_factor[...]
    factor_ref[place(1)] = layer_error(
        devices, 1, f_ref, inv_ref, pp_ref, (g0, g1, g2), err_ref, lambda k: write(err_ref, 1, k)
    )
    for copy in copies:
        copy.wait()


def own_error(devices, f, inv, pp, blocks):
    return pl.pallas_call(
        functools.partial(kernel_own_error, devices),
        out_shape=[pltpu.VMEM((RANK, C), F32), pltpu.VMEM((3 * C, C), BF16)],
        in_specs=[spec(pltpu.VMEM)] * 6,
        out_specs=[spec(pltpu.VMEM)] * 2,
        compiler_params=pltpu.CompilerParams(vmem_limit_bytes=VMEM_LIMIT),
        cost_estimate=cost(10**9, 5 * 10**6),
        name="own_error",
    )(f, local(inv), local(pp), *[local(blocks[0, k][0]) for k in range(3)])


def errors(devices, f, inv, pp, blocks, own_factor, own_err):
    return pl.pallas_call(
        functools.partial(kernel_errors, devices),
        out_shape=[jax.ShapeDtypeStruct((LAYERS, RANK, C), F32), pltpu.HBM((LAYERS, 3 * C, C), BF16)],
        in_specs=[spec(pltpu.VMEM)] * 8,
        out_specs=[spec(pltpu.VMEM), spec(pltpu.HBM)],
        scratch_shapes=[pltpu.VMEM((3 * C, C), BF16), pltpu.SemaphoreType.DMA((2, 3))],
        compiler_params=pltpu.CompilerParams(vmem_limit_bytes=VMEM_LIMIT),
        cost_estimate=cost(10**9, 5 * 10**6),
        name="errors",
    )(f, local(inv), local(pp), *[local(blocks[1, k][0]) for k in range(3)], local(own_factor), local(own_err))


def body(devices, x, o, e, q):
    orders = exchange_bits(devices)
    steps = len(orders[0])

    def swap_core(v):
        return lax.ppermute(v, "dp", [(i, i ^ 1) for i in range(devices)])

    def swap(v, step):
        return lax.ppermute(v, "dp", [(i, i ^ (1 << orders[i & 1][step])) for i in range(devices)])

    q = jnp.swapaxes(q, 1, 2)
    other, x1, o1, e1, x0, o0, e0, q_all = load(devices, x, o, e, q)
    got = swap_core(other)
    own = sums(devices, q_all, x0, o0, e0)
    sent = [own[0, i] + got[0, i] for i in range(STREAMS)]
    held = [own[1, i] + got[1, i] for i in range(STREAMS)]
    arrays = ((x0, o0, e0), (x1, o1, e1))
    blocks = {}
    plan = PLAN if steps + 1 >= len(PLAN) else [sum(PLAN, ())]
    for step in range(steps + 1):
        if step == 0:
            arrived = [swap(v, 0) for v in sent]
        else:
            arrived = [swap(v, step % steps) for v in held]
        if step < len(plan) and plan[step]:
            formed, token = grads(plan[step], arrays, held[-1])
            blocks.update(formed)
            arrived = [v + token for v in arrived]
        if step < steps:
            held = [v + w for v, w in zip(held, arrived)]
    own_parts = [v for pair in zip(held, arrived) for v in pair]
    other_parts = [swap_core(v) for v in own_parts]
    f0 = right(devices, 0, own_parts, blocks)
    f1 = right(devices, 1, other_parts, blocks)
    f0 = f0 + swap_core(f1)
    s_all, mat, token = gram(devices, CUTS[0], own_parts + other_parts, f0)
    for step in range(steps):
        got = swap(f0, step)
        if step == 1:
            mat, token = middle(CUTS[0], CUTS[1], mat, f0)
        if step == 2:
            inv, panel, pp, token = panels(CUTS[1], s_all, mat, f0)
        if step < 3:
            got = got + token
        f0 = f0 + got
    f1 = swap_core(f0)
    own_factor, own_err = own_error(devices, f0, inv, pp, blocks)
    factors, error = errors(devices, f1, inv, pp, blocks, own_factor, own_err)
    return jnp.swapaxes(panel, 1, 2), jnp.swapaxes(factors, 1, 2), error


def solution(mesh):
    devices = mesh.shape["dp"]
    in_specs = (
        P(None, ("groups", "dp"), None, None),
        P(None, ("groups", "dp"), None, None),
        P(None, ("groups", "dp"), None),
        P(),
    )
    out_specs = (P("groups", None, None), P("groups", None, None), P(None, ("groups", "dp"), None))
    return jax.shard_map(
        functools.partial(body, devices), mesh=mesh, in_specs=in_specs, out_specs=out_specs, check_vma=False
    )
```

time: 265 us -> 61.1 us (0.23)
  waiting for transfers between devices: 181 us -> 19.1 us
  other arithmetic: 33.1 us -> 0.25 us
  matrix products: 28 us -> 0 us
  Pallas kernels: 0 us -> 24.4 us
  starting transfers between devices: 0.08 us -> 16.5 us
  between operations: 14.2 us -> 0.77 us
  local copies, waits for them, and re-layouts: 8.03 us -> 0 us
    psum x2 -> x0, waiting for transfers between devices: 181 us -> none  [the longest x1 94.8 us: body(): summed = lax.psum(panel_terms(), 'dp') / math.sqrt(devices)]
    another operation x11 -> x0, other arithmetic: 29.1 us -> none  [the longest x4 12.4 us: orthogonal_rows(): lax.linalg.triangular_solve(lower_all[layer_no], shaped[:, layer_no], lef...]
    dot_general x9 -> x0, matrix products: 24.9 us -> none  [the longest x2 6.79 us: body(): lax.dot_general(grads_list[layer_no], panel_all[:, layer_no * RANK:(layer...]
    pallas_call x0 -> x12, Pallas kernels: none -> 24.4 us  [the longest x3 5.8 us: grads(): pl.pallas_call(functools.partial(kernel_grads, parts), out_shape=block *...]
    ppermute x0 -> x18, waiting for transfers between devices: none -> 19.1 us  [the longest x11 16.7 us: swap(): lax.ppermute(v, 'dp', [(i, i ^ 1 << orders[i & 1][step]) for i in range(d...]
    ppermute x0 -> x18, starting transfers between devices: none -> 16.5 us  [the longest x11 15.2 us: swap(): lax.ppermute(v, 'dp', [(i, i ^ 1 << orders[i & 1][step]) for i in range(d...]
    unnamed x18 -> x0, local copies, waits for them, and re-layouts: 5.36 us -> none
    another operation x2 -> x0, matrix products: 3.1 us -> none  [orthogonal_rows(): lax.linalg.triangular_solve(lower_all[layer_no], shaped[:, layer_no], lef...]
  transfers between devices with their start and end apart: 2 -> 18, of which waited for: 2 -> 14; matrix products, arithmetic and copies ran while one was open for 1% -> 0% of each run, Pallas kernels for 0% -> 29%
where the time goes in v2:
time: 61.1 us; the launch traced here: 61 us
  Pallas kernels  24.4 us (40%)
  waiting for transfers between devices  19.1 us (31%)
  starting transfers between devices  16.5 us (27%)
  between operations  0.77 us (1%)
    ppermute x11, waiting for transfers between devices, swap(): lax.ppermute(v, 'dp', [(i, i ^ 1 << orders[i & 1][step]) for i in range(d...  16.7 us
    ppermute x11, starting transfers between devices, swap(): lax.ppermute(v, 'dp', [(i, i ^ 1 << orders[i & 1][step]) for i in range(d...  15.2 us
    pallas_call x3, Pallas kernels, grads(): pl.pallas_call(functools.partial(kernel_grads, parts), out_shape=block *...  5.8 us
    pallas_call x1, Pallas kernels, panels(): pl.pallas_call(functools.partial(kernel_panels, first), out_shape=[pltpu....  3.85 us
    pallas_call x1, Pallas kernels, load(): pl.pallas_call(functools.partial(kernel_load, devices), out_shape=[pltpu....  3.74 us
    pallas_call x1, Pallas kernels, errors(): pl.pallas_call(functools.partial(kernel_errors, devices), out_shape=[jax....  2.49 us
    ppermute x7, waiting for transfers between devices, swap_core(): return lax.ppermute(v, 'dp', [(i, i ^ 1) for i in range(devices)])  2.38 us
    pallas_call x1, Pallas kernels, gram(): pl.pallas_call(functools.partial(kernel_gram, devices, last), out_shape=[...  2.29 us
  transfers between devices with their start and end apart: 18, of which 14 were waited for; matrix products, arithmetic and copies ran while one was open for 0% of the time, Pallas kernels for 29%

profile of v2, /device:TPU:0, one launch (start us, length us, event | category | flops | bytes accessed | tf_op | source)
XLA Modules:
  0.0 61.0 jit_solution(6483587851130984500)
XLA Ops:
  0.6 3.7 %load.1 = (f32[2,2,3,16,512]{4,3,2,1,0:T(8,128)S(1)}, bf16[1408,512]{1,0:T(8,128)(2,1)S(1)}, bf16[1472,512]{1,0:T(8,128)(2,1)S(1)}, bf16[1536,512]{1,0:T(8,128)(...) custom-call(bf16[2,1,1344,512]{3,2,1,0:T(8,128)(2,1)} %x_hbm.1, ...), custom_call_target="tpu_custom_call" | custom-call | flops 2000000000 | bytes 9000000 | tf_op jit(solution)/shard_map/load/pallas_call | solution.py:125
  4.4 0.5 collective-permute-start
  4.9 2.0 %sums.1 = f32[2,2,3,16,512]{4,3,2,1,0:T(8,128)S(1)} custom-call(f32[2,64,512]{2,1,0:T(8,128)S(1)} %get-tuple-element.45.q_ref, bf16[1408,512]{1,0:T(8,128)(2,1)S(1)} %get-tuple-element.46.x_ref.refs_0_.refs_3_, bf16[1472,512]{1,0:T(8,128)(2,1)S(1)} %get-tuple-element.47.o_ref.refs_1_.refs_4_, bf16[1536,512]{1,0:T(8,128)(2,1)S(1)} %get-tuple-element.48.e_ref.refs_2_.refs_5_), custom_call_target="tpu_custom_call" | custom-call | flops 2000000000 | bytes 4000000 | tf_op jit(solution)/shard_map/sums/pallas_call | solution.py:151
  6.9 0.0 collective-permute-done
  6.9 2.6 %collective-permute-start.3 = (f32[3,16,512]{2,1,0:T(8,128)S(1)}, f32[3,16,512]{2,1,0:T(8,128)S(1)}, u32[]{:S(2)}, u32[]{:S(2)}) collective-permute-start(f32[3,16,512]{2,1,0:T(8,128)S(1)} %get-tuple-element.87), channel_id=1, source_target_pairs={{0,2},{1,5},{2,0},{3,7},{4,6},{5,1},{6,4},{7,3},{8,10},{9,13},{10,... | collective-permute-start | bytes 294920 | tf_op jit(solution)/shard_map/ppermute | solution.py:406
  9.5 0.1 collective-permute-start.1
  9.6 1.9 %grads_00_01.1 = (f32[512,512]{1,0:T(8,128)S(1)}, bf16[512,512]{1,0:T(8,128)(2,1)S(1)}, bf16[512,512]{1,0:T(8,128)(2,1)S(1)}, f32[512,512]{1,0:T(8,128)S(1)}, bf...) custom-call(bf16[1408,512]{1,0:T(8,128)(2,1)S(1)} %get-tuple-element.46.x_ref.refs_0_.refs_3_, ...), custom_call_target="tpu_custom_call" | custom-call | flops 2000000000 | bytes 6000000 | tf_op jit(solution)/shard_map/grads_00_01/pallas_call | solution.py:179
  11.5 0.6 collective-permute-done.3
  12.1 2.0 %collective-permute-done.1 = f32[3,16,512]{2,1,0:T(8,128)S(1)} collective-permute-done((f32[3,16,512]{2,1,0:T(8,128)S(1)}, f32[3,16,512]{2,1,0:T(8,128)S(1)}, u32[]{:S(2)}, u32[]{:S(2)}) %collective-permute-start.1) | collective-permute-done | bytes 98336 | tf_op jit(solution)/shard_map/ppermute | solution.py:406
  14.2 1.6 %collective-permute-start.2 = (f32[3,16,512]{2,1,0:T(8,128)S(1)}, f32[3,16,512]{2,1,0:T(8,128)S(1)}, u32[]{:S(2)}, u32[]{:S(2)}) collective-permute-start(f32[3,16,512]{2,1,0:T(8,128)S(1)} %get-tuple-element.95), channel_id=1, source_target_pairs={{0,4},{1,9},{2,6},{3,11},{4,0},{5,13},{6,2},{7,15},{8,12},{9,1},{1... | collective-permute-start | bytes 294920 | tf_op jit(solution)/shard_map/ppermute | solution.py:406
  15.8 0.4 collective-permute-start.5
  16.3 1.9 %grads_02_10.1 = (f32[512,512]{1,0:T(8,128)S(1)}, bf16[512,512]{1,0:T(8,128)(2,1)S(1)}, bf16[512,512]{1,0:T(8,128)(2,1)S(1)}, f32[512,512]{1,0:T(8,128)S(1)}, bf...) custom-call(bf16[1408,512]{1,0:T(8,128)(2,1)S(1)} %get-tuple-element.46.x_ref.refs_0_.refs_3_, ...), custom_call_target="tpu_custom_call" | custom-call | flops 2000000000 | bytes 6000000 | tf_op jit(solution)/shard_map/grads_02_10/pallas_call | solution.py:179
  18.2 0.9 %collective-permute-done.2 = f32[3,16,512]{2,1,0:T(8,128)S(1)} collective-permute-done((f32[3,16,512]{2,1,0:T(8,128)S(1)}, f32[3,16,512]{2,1,0:T(8,128)S(1)}, u32[]{:S(2)}, u32[]{:S(2)}) %collective-permute-start.2) | collective-permute-done | bytes 98336 | tf_op jit(solution)/shard_map/ppermute | solution.py:406
  19.1 2.4 %collective-permute-done.5 = f32[3,16,512]{2,1,0:T(8,128)S(1)} collective-permute-done((f32[3,16,512]{2,1,0:T(8,128)S(1)}, f32[3,16,512]{2,1,0:T(8,128)S(1)}, u32[]{:S(2)}, u32[]{:S(2)}) %collective-permute-start.5) | collective-permute-done | bytes 98336 | tf_op jit(solution)/shard_map/ppermute | solution.py:406
  21.5 2.1 %collective-permute-start.4 = (f32[3,16,512]{2,1,0:T(8,128)S(1)}, f32[3,16,512]{2,1,0:T(8,128)S(1)}, u32[]{:S(2)}, u32[]{:S(2)}) collective-permute-start(f32[3,16,512]{2,1,0:T(8,128)S(1)} %get-tuple-element.93), channel_id=1, source_target_pairs={{0,8},{1,3},{2,10},{3,1},{4,12},{5,7},{6,14},{7,5},{8,0},{9,11},{1... | collective-permute-start | bytes 294920 | tf_op jit(solution)/shard_map/ppermute | solution.py:406
  23.7 0.9 %collective-permute-start.7 = (f32[3,16,512]{2,1,0:T(8,128)S(1)}, f32[3,16,512]{2,1,0:T(8,128)S(1)}, u32[]{:S(2)}, u32[]{:S(2)}) collective-permute-start(f32[3,16,512]{2,1,0:T(8,128)S(1)} %get-tuple-element.92.refs_6_), channel_id=1, source_target_pairs={{0,8},{1,3},{2,10},{3,1},{4,12},{5,7},{6,14},{7,5},{8,0},{9,11},{1... | collective-permute-start | bytes 294920 | tf_op jit(solution)/shard_map/ppermute | solution.py:406
  24.5 1.9 %grads_11_12.1 = (f32[512,512]{1,0:T(8,128)S(1)}, bf16[512,512]{1,0:T(8,128)(2,1)S(1)}, bf16[512,512]{1,0:T(8,128)(2,1)S(1)}, f32[512,512]{1,0:T(8,128)S(1)}, bf...) custom-call(bf16[1408,512]{1,0:T(8,128)(2,1)S(1)} %get-tuple-element.51.refs_3_.refs_0_, ...), custom_call_target="tpu_custom_call" | custom-call | flops 2000000000 | bytes 6000000 | tf_op jit(solution)/shard_map/grads_11_12/pallas_call | solution.py:179
  26.5 0.7 %collective-permute-done.4 = f32[3,16,512]{2,1,0:T(8,128)S(1)} collective-permute-done((f32[3,16,512]{2,1,0:T(8,128)S(1)}, f32[3,16,512]{2,1,0:T(8,128)S(1)}, u32[]{:S(2)}, u32[]{:S(2)}) %collective-permute-start.4) | collective-permute-done | bytes 98336 | tf_op jit(solution)/shard_map/ppermute | solution.py:406
  27.1 2.2 %collective-permute-done.7 = f32[3,16,512]{2,1,0:T(8,128)S(1)} collective-permute-done((f32[3,16,512]{2,1,0:T(8,128)S(1)}, f32[3,16,512]{2,1,0:T(8,128)S(1)}, u32[]{:S(2)}, u32[]{:S(2)}) %collective-permute-start.7) | collective-permute-done | bytes 98336 | tf_op jit(solution)/shard_map/ppermute | solution.py:406
  29.3 1.5 %collective-permute-start.8 = (f32[3,16,512]{2,1,0:T(8,128)S(1)}, f32[3,16,512]{2,1,0:T(8,128)S(1)}, u32[]{:S(2)}, u32[]{:S(2)}) collective-permute-start(f32[3,16,512]{2,1,0:T(8,128)S(1)} %get-tuple-element.90.refs_2_), channel_id=1, source_target_pairs={{0,2},{1,5},{2,0},{3,7},{4,6},{5,1},{6,4},{7,3},{8,10},{9,13},{10,... | collective-permute-start | bytes 294920 | tf_op jit(solution)/shard_map/ppermute | solution.py:406
  30.9 0.6 collective-permute-start.6
  31.4 0.0 collective-permute-start.11
  31.4 0.5 collective-permute-start.9
  31.9 2.1 %collective-permute-done.8.refs_3_ = f32[3,16,512]{2,1,0:T(8,128)S(1)} collective-permute-done((f32[3,16,512]{2,1,0:T(8,128)S(1)}, f32[3,16,512]{2,1,0:T(8,128)S(1)}, u32[]{:S(2)}, u32[]{:S(2)}) %collective-permute-start.8) | collective-permute-done | bytes 98336 | tf_op jit(solution)/shard_map/ppermute | solution.py:406
  34.0 0.0 collective-permute-start.12
  34.0 1.5 %collective-permute-done.6.refs_1_ = f32[3,16,512]{2,1,0:T(8,128)S(1)} collective-permute-done((f32[3,16,512]{2,1,0:T(8,128)S(1)}, f32[3,16,512]{2,1,0:T(8,128)S(1)}, u32[]{:S(2)}, u32[]{:S(2)}) %collective-permute-start.6) | collective-permute-done | bytes 98336 | tf_op jit(solution)/shard_map/ppermute | solution.py:406
  35.5 0.0 collective-permute-start.10
  35.5 0.0 collective-permute-done.11.refs_2_.refs_6_
  35.5 0.0 collective-permute-done.9.refs_0_.refs_4_
  35.5 0.0 collective-permute-done.12.refs_3_.refs_7_
  35.5 1.3 %collective-permute-done.10.refs_1_.refs_5_ = f32[3,16,512]{2,1,0:T(8,128)S(1)} collective-permute-done((f32[3,16,512]{2,1,0:T(8,128)S(1)}, f32[3,16,512]{2,1,0:T(8,128)S(1)}, u32[]{:S(2)}, u32[]{:S(2)}) %collective-permute-start.10) | collective-permute-done | bytes 98336 | tf_op jit(solution)/shard_map/ppermute | solution.py:403
  36.8 0.6 %right_1.1 = f32[64,512]{1,0:T(8,128)S(1)} custom-call(f32[3,16,512]{2,1,0:T(8,128)S(1)} %collective-permute-done.9.refs_0_.refs_4_, f32[3,16,512]{2,1,0:T(8,128)S(1)} %collective-permute-done.10.refs_1_.refs_5_, f32[3,16,512]{2,1,0:T(8,128)S(1)} %collective-permute-done.11.refs_2_.refs_6_, f32[3,16,512]{2,1,0:T(8,128)S(1)} %collective-permute-done.12.refs_3_.refs_7_, ...), custom_call_target="tpu_custom_call" | custom-call | flops 1000000000 | bytes 4000000 | tf_op jit(solution)/shard_map/right_1/pallas_call | solution.py:214
  37.4 0.2 collective-permute-start.13
  37.6 0.6 %right_0.1 = f32[64,512]{1,0:T(8,128)S(1)} custom-call(f32[3,16,512]{2,1,0:T(8,128)S(1)} %get-tuple-element.91.refs_0_, f32[3,16,512]{2,1,0:T(8,128)S(1)} %collective-permute-done.6.refs_1_, f32[3,16,512]{2,1,0:T(8,128)S(1)} %get-tuple-element.90.refs_2_, f32[3,16,512]{2,1,0:T(8,128)S(1)} %collective-permute-done.8.refs_3_, ...), custom_call_target="tpu_custom_call" | custom-call | flops 1000000000 | bytes 4000000 | tf_op jit(solution)/shard_map/right_0/pallas_call | solution.py:214
  38.3 0.6 collective-permute-done.13
  38.8 1.1 %collective-permute-start.14 = (f32[64,512]{1,0:T(8,128)S(1)}, f32[64,512]{1,0:T(8,128)S(1)}, u32[]{:S(2)}, u32[]{:S(2)}) collective-permute-start(f32[64,512]{1,0:T(8,128)S(1)} %add.100.refs_8_), channel_id=1, source_target_pairs={{0,2},{1,5},{2,0},{3,7},{4,6},{5,1},{6,4},{7,3},{8,10},{9,13},{10,... | collective-permute-start | bytes 393224 | tf_op jit(solution)/shard_map/ppermute | solution.py:406
  40.0 2.3 %gram.1 = (f32[2,3,64,512]{3,2,1,0:T(8,128)S(1)}, f32[2,64,128]{2,1,0:T(8,128)S(1)}, f32[64,512]{1,0:T(8,128)S(1)}) custom-call(f32[3,16,512]{2,1,0:T(8,128)S(1)} %get-tuple-element.91.refs_0_, f32[3,16,512]{2,1,0:T(8,128)S(1)} %collective-permute-done.6.refs_1_, f32[3,16,512]{2,1,0:T(8,128)S(1)} %get-tuple-element.90.refs_2_, ...), custom_call_target="tpu_custom_call" | custom-call | flops 2000000000 | bytes 10000000 | tf_op jit(solution)/shard_map/gram/pallas_call | solution.py:261
  42.3 1.6 %collective-permute-done.14 = f32[64,512]{1,0:T(8,128)S(1)} collective-permute-done((f32[64,512]{1,0:T(8,128)S(1)}, f32[64,512]{1,0:T(8,128)S(1)}, u32[]{:S(2)}, u32[]{:S(2)}) %collective-permute-start.14) | collective-permute-done | bytes 131104 | tf_op jit(solution)/shard_map/ppermute | solution.py:406
  43.9 1.9 %collective-permute-start.15 = (f32[64,512]{1,0:T(8,128)S(1)}, f32[64,512]{1,0:T(8,128)S(1)}, u32[]{:S(2)}, u32[]{:S(2)}) collective-permute-start(f32[64,512]{1,0:T(8,128)S(1)} %add_add_fusion.2.tie_ref), channel_id=1, source_target_pairs={{0,4},{1,9},{2,6},{3,11},{4,0},{5,13},{6,2},{7,15},{8,12},{9,1},{1... | collective-permute-start | bytes 393224 | tf_op jit(solution)/shard_map/ppermute | solution.py:406
  45.8 2.2 %middle_18.1 = (f32[2,64,128]{2,1,0:T(8,128)S(1)}, f32[64,512]{1,0:T(8,128)S(1)}) custom-call(f32[2,64,128]{2,1,0:T(8,128)S(1)} %get-tuple-element.69.m_ref, f32[64,512]{1,0:T(8,128)S(1)} %add_add_fusion.2.tie_ref), custom_call_target="tpu_custom_call" | custom-call | flops 2000000000 | bytes 10000000 | tf_op jit(solution)/shard_map/middle_18/pallas_call | solution.py:284
  48.0 1.7 %collective-permute-done.15 = f32[64,512]{1,0:T(8,128)S(1)} collective-permute-done((f32[64,512]{1,0:T(8,128)S(1)}, f32[64,512]{1,0:T(8,128)S(1)}, u32[]{:S(2)}, u32[]{:S(2)}) %collective-permute-start.15) | collective-permute-done | bytes 131104 | tf_op jit(solution)/shard_map/ppermute | solution.py:406
  49.7 2.4 %collective-permute-start.16 = (f32[64,512]{1,0:T(8,128)S(1)}, f32[64,512]{1,0:T(8,128)S(1)}, u32[]{:S(2)}, u32[]{:S(2)}) collective-permute-start(f32[64,512]{1,0:T(8,128)S(1)} %add_add_fusion.1.tie_ref), channel_id=1, source_target_pairs={{0,8},{1,3},{2,10},{3,1},{4,12},{5,7},{6,14},{7,5},{8,0},{9,11},{1... | collective-permute-start | bytes 393224 | tf_op jit(solution)/shard_map/ppermute | solution.py:406
  52.1 3.9 %panels.1 = (f32[2,64,64]{2,1,0:T(8,128)S(1)}, f32[2,64,1536]{2,1,0:T(8,128)}, bf16[2,1536,192]{2,1,0:T(8,128)(2,1)S(1)}, f32[64,512]{1,0:T(8,128)S(1)}) custom-call(f32[2,3,64,512]{3,2,1,0:T(8,128)S(1)} %get-tuple-element.68.s_ref, f32[2,64,128]{2,1,0:T(8,128)S(1)} %get-tuple-element.71.m_ref, f32[64,512]{1,0:T(8,128)S(1)} %add_add_fusion.1.tie_ref), custom_call_target="tpu_custom_call" | custom-call | flops 2000000000 | bytes 10000000 | tf_op jit(solution)/shard_map/panels/pallas_call | solution.py:317
  55.9 1.1 %collective-permute-done.16 = f32[64,512]{1,0:T(8,128)S(1)} collective-permute-done((f32[64,512]{1,0:T(8,128)S(1)}, f32[64,512]{1,0:T(8,128)S(1)}, u32[]{:S(2)}, u32[]{:S(2)}) %collective-permute-start.16) | collective-permute-done | bytes 131104 | tf_op jit(solution)/shard_map/ppermute | solution.py:406
  57.1 0.1 collective-permute-start.17
  57.2 0.8 %own_error.1 = (f32[64,512]{1,0:T(8,128)S(1)}, bf16[1536,512]{1,0:T(8,128)(2,1)S(1)}) custom-call(f32[64,512]{1,0:T(8,128)S(1)} %add_add_fusion.f_ref, f32[2,64,64]{2,1,0:T(8,128)S(1)} %get-tuple-element.75.inv_ref, bf16[2,1536,192]{2,1,0:T(8,128)(2,1)S(1)} %get-tuple-element.76.pp_ref, f32[512,512]{1,0:T(8,128)S(1)} %get-tuple-element.80.g0, ...), custom_call_target="tpu_custom_call" | custom-call | flops 1000000000 | bytes 5000000 | tf_op jit(solution)/shard_map/own_error/pallas_call | solution.py:374
  58.0 0.5 collective-permute-done.17.f_ref
  58.5 2.5 %errors.1 = (f32[2,64,512]{2,1,0:T(8,128)}, bf16[2,1536,512]{2,1,0:T(8,128)(2,1)}) custom-call(f32[64,512]{1,0:T(8,128)S(1)} %collective-permute-done.17.f_ref, f32[2,64,64]{2,1,0:T(8,128)S(1)} %get-tuple-element.75.inv_ref, bf16[2,1536,192]{2,1,0:T(8,128)(2,1)S(1)} %get-tuple-element.76.pp_ref, f32[512,512]{1,0:T(8,128)S(1)} %get-tuple-element.77.g0, ...), custom_call_target="tpu_custom_call" | custom-call | flops 1000000000 | bytes 5000000 | tf_op jit(solution)/shard_map/errors/pallas_call | solution.py:386
  (8 shorter events, 0.3 us)
Async XLA Ops:
  4.4 2.5 %collective-permute-start = (f32[2,2,3,16,512]{4,3,2,1,0:T(8,128)S(1)}, f32[2,2,3,16,512]{4,3,2,1,0:T(8,128)S(1)}, u32[]{:S(2)}, u32[]{:S(2)}) collective-permute-start(f32[2,2,3,16,512]{4,3,2,1,0:T(8,128)S(1)} %get-tuple-element.49), channel_id=1, source_target_pairs={{0,1},{1,0},{2,3},{3,2},{4,5},{5,4},{6,7},{7,6},{8,9},{9,8},{10,11... | collective-permute-start | bytes 1179656 | tf_op jit(solution)/shard_map/ppermute | solution.py:403
  6.9 5.2 %collective-permute-start.3 = (f32[3,16,512]{2,1,0:T(8,128)S(1)}, f32[3,16,512]{2,1,0:T(8,128)S(1)}, u32[]{:S(2)}, u32[]{:S(2)}) collective-permute-start(f32[3,16,512]{2,1,0:T(8,128)S(1)} %get-tuple-element.87), channel_id=1, source_target_pairs={{0,2},{1,5},{2,0},{3,7},{4,6},{5,1},{6,4},{7,3},{8,10},{9,13},{10,... | collective-permute-start | bytes 294920 | tf_op jit(solution)/shard_map/ppermute | solution.py:406
  9.5 4.6 %collective-permute-start.1 = (f32[3,16,512]{2,1,0:T(8,128)S(1)}, f32[3,16,512]{2,1,0:T(8,128)S(1)}, u32[]{:S(2)}, u32[]{:S(2)}) collective-permute-start(f32[3,16,512]{2,1,0:T(8,128)S(1)} %get-tuple-element.89), channel_id=1, source_target_pairs={{0,2},{1,5},{2,0},{3,7},{4,6},{5,1},{6,4},{7,3},{8,10},{9,13},{10,... | collective-permute-start | bytes 294920 | tf_op jit(solution)/shard_map/ppermute | solution.py:406
  14.2 4.9 %collective-permute-start.2 = (f32[3,16,512]{2,1,0:T(8,128)S(1)}, f32[3,16,512]{2,1,0:T(8,128)S(1)}, u32[]{:S(2)}, u32[]{:S(2)}) collective-permute-start(f32[3,16,512]{2,1,0:T(8,128)S(1)} %get-tuple-element.95), channel_id=1, source_target_pairs={{0,4},{1,9},{2,6},{3,11},{4,0},{5,13},{6,2},{7,15},{8,12},{9,1},{1... | collective-permute-start | bytes 294920 | tf_op jit(solution)/shard_map/ppermute | solution.py:406
  15.8 5.7 %collective-permute-start.5 = (f32[3,16,512]{2,1,0:T(8,128)S(1)}, f32[3,16,512]{2,1,0:T(8,128)S(1)}, u32[]{:S(2)}, u32[]{:S(2)}) collective-permute-start(f32[3,16,512]{2,1,0:T(8,128)S(1)} %get-tuple-element.94.refs_6_), channel_id=1, source_target_pairs={{0,4},{1,9},{2,6},{3,11},{4,0},{5,13},{6,2},{7,15},{8,12},{9,1},{1... | collective-permute-start | bytes 294920 | tf_op jit(solution)/shard_map/ppermute | solution.py:406
  21.5 5.6 %collective-permute-start.4 = (f32[3,16,512]{2,1,0:T(8,128)S(1)}, f32[3,16,512]{2,1,0:T(8,128)S(1)}, u32[]{:S(2)}, u32[]{:S(2)}) collective-permute-start(f32[3,16,512]{2,1,0:T(8,128)S(1)} %get-tuple-element.93), channel_id=1, source_target_pairs={{0,8},{1,3},{2,10},{3,1},{4,12},{5,7},{6,14},{7,5},{8,0},{9,11},{1... | collective-permute-start | bytes 294920 | tf_op jit(solution)/shard_map/ppermute | solution.py:406
  23.7 5.6 %collective-permute-start.7 = (f32[3,16,512]{2,1,0:T(8,128)S(1)}, f32[3,16,512]{2,1,0:T(8,128)S(1)}, u32[]{:S(2)}, u32[]{:S(2)}) collective-permute-start(f32[3,16,512]{2,1,0:T(8,128)S(1)} %get-tuple-element.92.refs_6_), channel_id=1, source_target_pairs={{0,8},{1,3},{2,10},{3,1},{4,12},{5,7},{6,14},{7,5},{8,0},{9,11},{1... | collective-permute-start | bytes 294920 | tf_op jit(solution)/shard_map/ppermute | solution.py:406
  29.3 4.7 %collective-permute-start.8 = (f32[3,16,512]{2,1,0:T(8,128)S(1)}, f32[3,16,512]{2,1,0:T(8,128)S(1)}, u32[]{:S(2)}, u32[]{:S(2)}) collective-permute-start(f32[3,16,512]{2,1,0:T(8,128)S(1)} %get-tuple-element.90.refs_2_), channel_id=1, source_target_pairs={{0,2},{1,5},{2,0},{3,7},{4,6},{5,1},{6,4},{7,3},{8,10},{9,13},{10,... | collective-permute-start | bytes 294920 | tf_op jit(solution)/shard_map/ppermute | solution.py:406
  30.9 4.6 %collective-permute-start.6 = (f32[3,16,512]{2,1,0:T(8,128)S(1)}, f32[3,16,512]{2,1,0:T(8,128)S(1)}, u32[]{:S(2)}, u32[]{:S(2)}) collective-permute-start(f32[3,16,512]{2,1,0:T(8,128)S(1)} %get-tuple-element.91.refs_0_), channel_id=1, source_target_pairs={{0,2},{1,5},{2,0},{3,7},{4,6},{5,1},{6,4},{7,3},{8,10},{9,13},{10,... | collective-permute-start | bytes 294920 | tf_op jit(solution)/shard_map/ppermute | solution.py:406
  31.4 4.1 %collective-permute-start.11 = (f32[3,16,512]{2,1,0:T(8,128)S(1)}, f32[3,16,512]{2,1,0:T(8,128)S(1)}, u32[]{:S(2)}, u32[]{:S(2)}) collective-permute-start(f32[3,16,512]{2,1,0:T(8,128)S(1)} %get-tuple-element.90.refs_2_), channel_id=1, source_target_pairs={{0,1},{1,0},{2,3},{3,2},{4,5},{5,4},{6,7},{7,6},{8,9},{9,8},{10,11... | collective-permute-start | bytes 294920 | tf_op jit(solution)/shard_map/ppermute | solution.py:403
  31.4 4.1 %collective-permute-start.9 = (f32[3,16,512]{2,1,0:T(8,128)S(1)}, f32[3,16,512]{2,1,0:T(8,128)S(1)}, u32[]{:S(2)}, u32[]{:S(2)}) collective-permute-start(f32[3,16,512]{2,1,0:T(8,128)S(1)} %get-tuple-element.91.refs_0_), channel_id=1, source_target_pairs={{0,1},{1,0},{2,3},{3,2},{4,5},{5,4},{6,7},{7,6},{8,9},{9,8},{10,11... | collective-permute-start | bytes 294920 | tf_op jit(solution)/shard_map/ppermute | solution.py:403
  34.0 1.5 %collective-permute-start.12 = (f32[3,16,512]{2,1,0:T(8,128)S(1)}, f32[3,16,512]{2,1,0:T(8,128)S(1)}, u32[]{:S(2)}, u32[]{:S(2)}) collective-permute-start(f32[3,16,512]{2,1,0:T(8,128)S(1)} %collective-permute-done.8.refs_3_), channel_id=1, source_target_pairs={{0,1},{1,0},{2,3},{3,2},{4,5},{5,4},{6,7},{7,6},{8,9},{9,8},{10,11... | collective-permute-start | bytes 294920 | tf_op jit(solution)/shard_map/ppermute | solution.py:403
  35.5 1.3 %collective-permute-start.10 = (f32[3,16,512]{2,1,0:T(8,128)S(1)}, f32[3,16,512]{2,1,0:T(8,128)S(1)}, u32[]{:S(2)}, u32[]{:S(2)}) collective-permute-start(f32[3,16,512]{2,1,0:T(8,128)S(1)} %collective-permute-done.6.refs_1_), channel_id=1, source_target_pairs={{0,1},{1,0},{2,3},{3,2},{4,5},{5,4},{6,7},{7,6},{8,9},{9,8},{10,11... | collective-permute-start | bytes 294920 | tf_op jit(solution)/shard_map/ppermute | solution.py:403
  37.4 1.4 %collective-permute-start.13 = (f32[64,512]{1,0:T(8,128)S(1)}, f32[64,512]{1,0:T(8,128)S(1)}, u32[]{:S(2)}, u32[]{:S(2)}) collective-permute-start(f32[64,512]{1,0:T(8,128)S(1)} %right_1.1), channel_id=1, source_target_pairs={{0,1},{1,0},{2,3},{3,2},{4,5},{5,4},{6,7},{7,6},{8,9},{9,8},{10,11... | collective-permute-start | bytes 393224 | tf_op jit(solution)/shard_map/ppermute | solution.py:403
  38.8 5.0 %collective-permute-start.14 = (f32[64,512]{1,0:T(8,128)S(1)}, f32[64,512]{1,0:T(8,128)S(1)}, u32[]{:S(2)}, u32[]{:S(2)}) collective-permute-start(f32[64,512]{1,0:T(8,128)S(1)} %add.100.refs_8_), channel_id=1, source_target_pairs={{0,2},{1,5},{2,0},{3,7},{4,6},{5,1},{6,4},{7,3},{8,10},{9,13},{10,... | collective-permute-start | bytes 393224 | tf_op jit(solution)/shard_map/ppermute | solution.py:406
  43.9 5.8 %collective-permute-start.15 = (f32[64,512]{1,0:T(8,128)S(1)}, f32[64,512]{1,0:T(8,128)S(1)}, u32[]{:S(2)}, u32[]{:S(2)}) collective-permute-start(f32[64,512]{1,0:T(8,128)S(1)} %add_add_fusion.2.tie_ref), channel_id=1, source_target_pairs={{0,4},{1,9},{2,6},{3,11},{4,0},{5,13},{6,2},{7,15},{8,12},{9,1},{1... | collective-permute-start | bytes 393224 | tf_op jit(solution)/shard_map/ppermute | solution.py:406
  49.7 7.3 %collective-permute-start.16 = (f32[64,512]{1,0:T(8,128)S(1)}, f32[64,512]{1,0:T(8,128)S(1)}, u32[]{:S(2)}, u32[]{:S(2)}) collective-permute-start(f32[64,512]{1,0:T(8,128)S(1)} %add_add_fusion.1.tie_ref), channel_id=1, source_target_pairs={{0,8},{1,3},{2,10},{3,1},{4,12},{5,7},{6,14},{7,5},{8,0},{9,11},{1... | collective-permute-start | bytes 393224 | tf_op jit(solution)/shard_map/ppermute | solution.py:406
  57.1 1.4 %collective-permute-start.17 = (f32[64,512]{1,0:T(8,128)S(1)}, f32[64,512]{1,0:T(8,128)S(1)}, u32[]{:S(2)}, u32[]{:S(2)}) collective-permute-start(f32[64,512]{1,0:T(8,128)S(1)} %add_add_fusion.f_ref), channel_id=1, source_target_pairs={{0,1},{1,0},{2,3},{3,2},{4,5},{5,4},{6,7},{7,6},{8,9},{9,8},{10,11... | collective-permute-start | bytes 393224 | tf_op jit(solution)/shard_map/ppermute | solution.py:403

commit v3 on v2

--- a/solution.py
+++ b/solution.py
@@ -20,7 +20,7 @@
 BF16 = jnp.bfloat16
 HIGH = lax.Precision.HIGHEST
 VMEM_LIMIT = 14 << 20
-CUTS = (18, 44)
+CUTS = (3, 8)
 PLAN = [((0, 0), (0, 1)), ((0, 2), (1, 0)), ((1, 1), (1, 2))]
 
 
@@ -66,6 +66,14 @@
 
 def far(v):
     return pltpu.with_memory_space_constraint(v, pltpu.HBM)
+
+
+TOKENS = [pltpu.VMEM((2 * PART, C), F32)] * STREAMS
+
+
+def clear(refs):
+    for ref in refs:
+        ref[...] = jnp.zeros_like(ref)
 
 
 def cost(flops, nbytes):
@@ -170,7 +178,7 @@
         g = prod * (1.0 / math.sqrt(LEN)) + e_ref[pl.ds(k * C, C)].astype(F32)
         g_ref[...] = g
         hi_ref[...], lo_ref[...] = split2(g)
-    outs[-1][...] = jnp.zeros_like(outs[-1])
+    clear(outs[-STREAMS:])
 
 
 def grads(parts, arrays, tie):
@@ -178,24 +186,42 @@
     block = [pltpu.VMEM((C, C), F32), pltpu.VMEM((C, C), BF16), pltpu.VMEM((C, C), BF16)]
     out = pl.pallas_call(
         functools.partial(kernel_grads, parts),
-        out_shape=block * len(parts) + [pltpu.VMEM((3, PART, C), F32)],
+        out_shape=block * len(parts) + [pltpu.VMEM((3, PART, C), F32)] * STREAMS,
         in_specs=[spec(pltpu.VMEM)] * len(ins) + [spec(pl.ANY)],
-        out_specs=[spec(pltpu.VMEM)] * (3 * len(parts) + 1),
+        out_specs=[spec(pltpu.VMEM)] * (3 * len(parts) + STREAMS),
         compiler_params=pltpu.CompilerParams(vmem_limit_bytes=VMEM_LIMIT),
         cost_estimate=cost(10**9 * len(parts), 3 * 10**6 * len(parts)),
         name="grads_" + "_".join(f"{which}{k}" for which, k in parts),
     )(*ins, tie)
-    return {part: out[3 * i : 3 * i + 3] for i, part in enumerate(parts)}, out[-1]
+    return {part: out[3 * i : 3 * i + 3] for i, part in enumerate(parts)}, out[-STREAMS:]
+
+
+def kernel_gate(*refs):
+    pass
+
+
+def gate(values, tie):
+    n = len(values)
+    return pl.pallas_call(
+        kernel_gate,
+        out_shape=[pltpu.VMEM(v.shape, v.dtype) for v in values],
+        in_specs=[spec(pltpu.VMEM)] * n + [spec(pl.ANY)],
+        out_specs=[spec(pltpu.VMEM)] * n,
+        input_output_aliases={i: i for i in range(n)},
+        compiler_params=pltpu.CompilerParams(vmem_limit_bytes=VMEM_LIMIT),
+        cost_estimate=cost(0, 0),
+        name="gate",
+    )(*[local(v) for v in values], tie)
 
 
 def gather_parts(devices, which, part_refs, k):
     keep = kept(devices, place(which))
-    rows = [(2 * (i // 2) + (keep if i % 2 == 0 else 1 - keep)) * PART for i in range(2 * STREAMS)]
+    rows = [(2 * (i // 2) + (keep if i % 2 == 0 else 1 - keep)) * PART for i in range(len(part_refs))]
     return [ref[k] for ref in part_refs], [pl.multiple_of(row, PART) for row in rows]
 
 
 def kernel_right(devices, which, *refs):
-    part_refs, his, los, f_ref = refs[: 2 * STREAMS], refs[2 * STREAMS :][:3], refs[2 * STREAMS + 3 :][:3], refs[-1]
+    part_refs, his, los, f_refs = refs[: 2 * STREAMS], refs[2 * STREAMS :][:3], refs[2 * STREAMS + 3 :][:3], refs[-STREAMS:]
     acc = jnp.zeros((2 * RANK, C), F32)
     acc_low = jnp.zeros((RANK, C), F32)
     for k in range(3):
@@ -205,7 +231,8 @@
         acc_low += dot_nn(s_hi, los[k][...])
     f = acc[:RANK] + acc[RANK:] + acc_low
     for i, row in enumerate(rows):
-        f_ref[pl.ds(row, PART)] = f[i * PART : (i + 1) * PART]
+        row = pl.multiple_of(row - (i // 2) * 2 * PART, PART)
+        f_refs[i // 2][pl.ds(row, PART)] = f[i * PART : (i + 1) * PART]
 
 
 def right(devices, which, parts, blocks):
@@ -213,30 +240,55 @@
     los = [local(blocks[which, k][2]) for k in range(3)]
     return pl.pallas_call(
         functools.partial(kernel_right, devices, which),
-        out_shape=pltpu.VMEM((RANK, C), F32),
+        out_shape=[pltpu.VMEM((2 * PART, C), F32)] * STREAMS,
         in_specs=[spec(pltpu.VMEM)] * (2 * STREAMS + 6),
-        out_specs=spec(pltpu.VMEM),
+        out_specs=[spec(pltpu.VMEM)] * STREAMS,
         compiler_params=pltpu.CompilerParams(vmem_limit_bytes=VMEM_LIMIT),
         cost_estimate=cost(10**9, 4 * 10**6),
         name=f"right_{which}",
     )(*parts, *his, *los)
 
 
+def lanes(v, column):
+    return jnp.broadcast_to(v[:, column : column + 1], (8, 128))
+
+
+def subs(v, row):
+    return jnp.broadcast_to(v[row : row + 1, :], (8, 128))
+
+
 def eliminate(mats, first, last):
-    row_no = lax.broadcasted_iota(jnp.int32, (RANK, 1), 0)
-    mats = list(mats)
-    for j in range(first, last):
-        for which in range(2):
-            m = mats[which]
-            row = m[j : j + 1, :]
-            scaled = row / row[:, j : j + 1]
-            col = jnp.where(row_no > j, m[:, j : j + 1], 0.0)
-            mats[which] = m - col * scaled
-    return mats
+    tiles = [[m[8 * i : 8 * i + 8] for i in range(RANK // 8)] for m in mats]
+    row_no = lax.broadcasted_iota(jnp.int32, (8, 128), 0)
+    both = range(len(mats))
+    for step in range(first, last):
+        cols = [[lanes(tiles[w][step], 8 * step + m) for m in range(8)] for w in both]
+        below = [
+            {i: [lanes(tiles[w][i], 8 * step + m) for m in range(8)] for i in range(step + 1, RANK // 8)} for w in both
+        ]
+        lower = [tiles[w][step] for w in both]
+        solved = [tiles[w][step] for w in both]
+        for i in range(8):
+            for w in both:
+                inv = 1.0 / subs(cols[w][i], i)
+                pivot_row = subs(lower[w], i) * inv
+                others = jnp.where(row_no != i, cols[w][i], 0.0)
+                for m in range(i + 1, 8):
+                    pivot = subs(cols[w][m], i) * inv
+                    cols[w][m] = jnp.where(row_no == i, pivot, cols[w][m] - others * pivot)
+                lower[w] = lower[w] - jnp.where(row_no > i, cols[w][i], 0.0) * pivot_row
+                solved[w] = jnp.where(row_no == i, pivot_row, solved[w] - others * pivot_row)
+        for w in both:
+            tiles[w][step] = lower[w]
+            rows = [subs(solved[w], m) for m in range(8)]
+            for i in range(step + 1, RANK // 8):
+                for m in range(8):
+                    tiles[w][i] = tiles[w][i] - below[w][i][m] * rows[m]
+    return [jnp.concatenate(t, axis=0) for t in tiles]
 
 
 def kernel_gram(devices, last, *refs):
-    s_ref, m_ref, token_ref = refs[-3:]
+    s_ref, m_ref = refs[-2 - STREAMS : -STREAMS]
     mats = []
     eye = (
         lax.broadcasted_iota(jnp.int32, (RANK, RANK), 0) == lax.broadcasted_iota(jnp.int32, (RANK, RANK), 1)
@@ -254,7 +306,7 @@
     mats = eliminate(mats, 0, last)
     for which in range(2):
         m_ref[which] = mats[which]
-    token_ref[...] = jnp.zeros_like(token_ref)
+    clear(refs[-STREAMS:])
 
 
 def gram(devices, last, parts, tie):
@@ -263,37 +315,37 @@
         out_shape=[
             pltpu.VMEM((LAYERS, 3, RANK, C), F32),
             pltpu.VMEM((LAYERS, RANK, 2 * RANK), F32),
-            pltpu.VMEM((RANK, C), F32),
-        ],
+        ]
+        + TOKENS,
         in_specs=[spec(pltpu.VMEM)] * len(parts) + [spec(pl.ANY)],
-        out_specs=[spec(pltpu.VMEM)] * 3,
+        out_specs=[spec(pltpu.VMEM)] * (2 + STREAMS),
         compiler_params=pltpu.CompilerParams(vmem_limit_bytes=VMEM_LIMIT),
         cost_estimate=cost(2 * 10**9, 10 * 10**6),
         name="gram",
     )(*parts, tie)
 
 
-def kernel_middle(first, last, m_ref, tie_ref, out_ref, token_ref):
+def kernel_middle(first, last, m_ref, tie_ref, out_ref, *token_refs):
     mats = eliminate([m_ref[0], m_ref[1]], first, last)
     for which in range(2):
         out_ref[which] = mats[which]
-    token_ref[...] = jnp.zeros_like(token_ref)
+    clear(token_refs)
 
 
 def middle(first, last, m, tie):
     return pl.pallas_call(
         functools.partial(kernel_middle, first, last),
-        out_shape=[pltpu.VMEM((LAYERS, RANK, 2 * RANK), F32), pltpu.VMEM((RANK, C), F32)],
+        out_shape=[pltpu.VMEM((LAYERS, RANK, 2 * RANK), F32)] + TOKENS,
         in_specs=[spec(pltpu.VMEM), spec(pl.ANY)],
-        out_specs=[spec(pltpu.VMEM)] * 2,
+        out_specs=[spec(pltpu.VMEM)] * (1 + STREAMS),
         compiler_params=pltpu.CompilerParams(vmem_limit_bytes=VMEM_LIMIT),
         cost_estimate=cost(2 * 10**9, 10 * 10**6),
         name=f"middle_{first}",
     )(local(m), tie)
 
 
-def kernel_panels(first, s_ref, m_ref, tie_ref, inv_ref, p_ref, pp_ref, token_ref):
-    mats = eliminate([m_ref[0], m_ref[1]], first, RANK)
+def kernel_panels(first, s_ref, m_ref, tie_ref, inv_ref, p_ref, pp_ref, *token_refs):
+    mats = eliminate([m_ref[0], m_ref[1]], first, RANK // 8)
     eye = (
         lax.broadcasted_iota(jnp.int32, (RANK, RANK), 0) == lax.broadcasted_iota(jnp.int32, (RANK, RANK), 1)
     ).astype(F32)
@@ -310,7 +362,7 @@
             p_ref[layer, :, pl.ds(k * C, C)] = p_t
             hi, lo = split2(p_t.T)
             pp_ref[which, pl.ds(k * C, C)] = jnp.concatenate([hi, lo, hi], axis=1)
-    token_ref[...] = jnp.zeros_like(token_ref)
+    clear(token_refs)
 
 
 def panels(first, s, m, tie):
@@ -320,38 +372,46 @@
             pltpu.VMEM((LAYERS, RANK, RANK), F32),
             jax.ShapeDtypeStruct((LAYERS, RANK, 3 * C), F32),
             pltpu.VMEM((LAYERS, 3 * C, 3 * RANK), BF16),
-            pltpu.VMEM((RANK, C), F32),
-        ],
+        ]
+        + TOKENS,
         in_specs=[spec(pltpu.VMEM), spec(pltpu.VMEM), spec(pl.ANY)],
-        out_specs=[spec(pltpu.VMEM)] * 4,
+        out_specs=[spec(pltpu.VMEM)] * (3 + STREAMS),
         compiler_params=pltpu.CompilerParams(vmem_limit_bytes=VMEM_LIMIT),
         cost_estimate=cost(2 * 10**9, 10 * 10**6),
         name="panels",
     )(local(s), local(m), tie)
 
 
-def layer_error(devices, which, f_ref, inv_ref, pp_ref, g_refs, err_ref, each):
+def layer_error(devices, which, f_refs, inv_ref, pp_ref, g_refs, err_ref, first, each):
     norm = 1.0 / math.sqrt(3 * C * devices)
+    f = jnp.concatenate([f_ref[...] for f_ref in f_refs], axis=0)
     f_t = (
         lax.dot_general(
-            inv_ref[which], f_ref[...], (((1,), (0,)), ((), ())), precision=HIGH, preferred_element_type=F32
+            inv_ref[which], f, (((1,), (0,)), ((), ())), precision=HIGH, preferred_element_type=F32
         )
         * norm
     )
+    first(f_t)
     hi, lo = split2(f_t * norm)
     rhs = jnp.concatenate([hi, hi, lo], axis=0)
     for k in range(3):
         rows = pl.ds(k * C, C)
         err_ref[rows] = (g_refs[k][...] - dot_nn(pp_ref[which, rows], rhs)).astype(BF16)
         each(k)
-    return f_t
-
-
-def kernel_own_error(devices, f_ref, inv_ref, pp_ref, g0, g1, g2, factor_ref, err_ref):
-    factor_ref[...] = layer_error(devices, 0, f_ref, inv_ref, pp_ref, (g0, g1, g2), err_ref, lambda k: None)
-
-
-def kernel_errors(devices, f_ref, inv_ref, pp_ref, g0, g1, g2, own_factor, own_err, factor_ref, err_hbm, err_ref, sems):
+
+
+def kernel_own_error(devices, *refs):
+    f_refs, (inv_ref, pp_ref, g0, g1, g2, factor_ref, err_ref) = refs[:STREAMS], refs[STREAMS:]
+
+    def keep_factor(f_t):
+        factor_ref[...] = f_t
+
+    layer_error(devices, 0, f_refs, inv_ref, pp_ref, (g0, g1, g2), err_ref, keep_factor, lambda k: None)
+
+
+def kernel_errors(devices, *refs):
+    f_refs, (inv_ref, pp_ref, g0, g1, g2, own_factor, own_err) = refs[:STREAMS], refs[STREAMS : STREAMS + 7]
+    factor_hbm, err_hbm, err_ref, factor_ref, sems = refs[STREAMS + 7 :]
     copies = []
 
     def write(source, which, k):
@@ -360,12 +420,19 @@
         copy.start()
         copies.append(copy)
 
+    def write_factor(source, which):
+        copy = pltpu.make_async_copy(source, factor_hbm.at[place(which)], sems.at[which, 3])
+        copy.start()
+        copies.append(copy)
+
+    def keep_factor(f_t):
+        factor_ref[...] = f_t
+        write_factor(factor_ref, 1)
+
     for k in range(3):
         write(own_err, 0, k)
-    factor_ref[place(0)] = own_factor[...]
-    factor_ref[place(1)] = layer_error(
-        devices, 1, f_ref, inv_ref, pp_ref, (g0, g1, g2), err_ref, lambda k: write(err_ref, 1, k)
-    )
+    write_factor(own_factor, 0)
+    layer_error(devices, 1, f_refs, inv_ref, pp_ref, (g0, g1, g2), err_ref, keep_factor, lambda k: write(err_ref, 1, k))
     for copy in copies:
         copy.wait()
 
@@ -374,25 +441,29 @@
     return pl.pallas_call(
         functools.partial(kernel_own_error, devices),
         out_shape=[pltpu.VMEM((RANK, C), F32), pltpu.VMEM((3 * C, C), BF16)],
-        in_specs=[spec(pltpu.VMEM)] * 6,
+        in_specs=[spec(pltpu.VMEM)] * (5 + STREAMS),
         out_specs=[spec(pltpu.VMEM)] * 2,
         compiler_params=pltpu.CompilerParams(vmem_limit_bytes=VMEM_LIMIT),
         cost_estimate=cost(10**9, 5 * 10**6),
         name="own_error",
-    )(f, local(inv), local(pp), *[local(blocks[0, k][0]) for k in range(3)])
+    )(*f, local(inv), local(pp), *[local(blocks[0, k][0]) for k in range(3)])
 
 
 def errors(devices, f, inv, pp, blocks, own_factor, own_err):
     return pl.pallas_call(
         functools.partial(kernel_errors, devices),
-        out_shape=[jax.ShapeDtypeStruct((LAYERS, RANK, C), F32), pltpu.HBM((LAYERS, 3 * C, C), BF16)],
-        in_specs=[spec(pltpu.VMEM)] * 8,
-        out_specs=[spec(pltpu.VMEM), spec(pltpu.HBM)],
-        scratch_shapes=[pltpu.VMEM((3 * C, C), BF16), pltpu.SemaphoreType.DMA((2, 3))],
+        out_shape=[pltpu.HBM((LAYERS, RANK, C), F32), pltpu.HBM((LAYERS, 3 * C, C), BF16)],
+        in_specs=[spec(pltpu.VMEM)] * (7 + STREAMS),
+        out_specs=[spec(pltpu.HBM)] * 2,
+        scratch_shapes=[
+            pltpu.VMEM((3 * C, C), BF16),
+            pltpu.VMEM((RANK, C), F32),
+            pltpu.SemaphoreType.DMA((2, 4)),
+        ],
         compiler_params=pltpu.CompilerParams(vmem_limit_bytes=VMEM_LIMIT),
         cost_estimate=cost(10**9, 5 * 10**6),
         name="errors",
-    )(f, local(inv), local(pp), *[local(blocks[1, k][0]) for k in range(3)], local(own_factor), local(own_err))
+    )(*f, local(inv), local(pp), *[local(blocks[1, k][0]) for k in range(3)], local(own_factor), local(own_err))
 
 
 def body(devices, x, o, e, q):
@@ -401,6 +472,16 @@
 
     def swap_core(v):
         return lax.ppermute(v, "dp", [(i, i ^ 1) for i in range(devices)])
+
+    def added(held, arrived, tokens):
+        return [v + w + token for v, w, token in zip(held, arrived, tokens)]
+
+    def added_in_turn(held, arrived, tokens):
+        total = list(held)
+        for i in reversed(range(STREAMS)):
+            token = tokens[i] if i == STREAMS - 1 else gate([tokens[i]], total[i + 1])[0]
+            total[i] = held[i] + (arrived[i] + token)
+        return total
 
     def swap(v, step):
         return lax.ppermute(v, "dp", [(i, i ^ (1 << orders[i & 1][step])) for i in range(devices)])
@@ -420,27 +501,27 @@
         else:
             arrived = [swap(v, step % steps) for v in held]
         if step < len(plan) and plan[step]:
-            formed, token = grads(plan[step], arrays, held[-1])
+            formed, tokens = grads(plan[step], arrays, held[-1])
             blocks.update(formed)
-            arrived = [v + token for v in arrived]
         if step < steps:
-            held = [v + w for v, w in zip(held, arrived)]
+            if step < len(plan) and plan[step]:
+                held = added(held, arrived, tokens)
+            else:
+                held = [v + w for v, w in zip(held, arrived)]
     own_parts = [v for pair in zip(held, arrived) for v in pair]
     other_parts = [swap_core(v) for v in own_parts]
+    f1 = right(devices, 1, other_parts, blocks)
     f0 = right(devices, 0, own_parts, blocks)
-    f1 = right(devices, 1, other_parts, blocks)
-    f0 = f0 + swap_core(f1)
-    s_all, mat, token = gram(devices, CUTS[0], own_parts + other_parts, f0)
+    f0 = [v + swap_core(w) for v, w in zip(f0, f1)]
+    s_all, mat, *tokens = gram(devices, CUTS[0], own_parts + other_parts, f0[-1])
     for step in range(steps):
-        got = swap(f0, step)
+        arrived = [swap(v, step) for v in f0]
         if step == 1:
-            mat, token = middle(CUTS[0], CUTS[1], mat, f0)
+            mat, *tokens = middle(CUTS[0], CUTS[1], mat, f0[-1])
         if step == 2:
-            inv, panel, pp, token = panels(CUTS[1], s_all, mat, f0)
-        if step < 3:
-            got = got + token
-        f0 = f0 + got
-    f1 = swap_core(f0)
+            inv, panel, pp, *tokens = panels(CUTS[1], s_all, mat, f0[-1])
+        f0 = added_in_turn(f0, arrived, tokens) if step < 3 else [v + w for v, w in zip(f0, arrived)]
+    f1 = [swap_core(v) for v in f0]
     own_factor, own_err = own_error(devices, f0, inv, pp, blocks)
     factors, error = errors(devices, f1, inv, pp, blocks, own_factor, own_err)
     return jnp.swapaxes(panel, 1, 2), jnp.swapaxes(factors, 1, 2), error

time: 61.1 us -> 54.6 us (0.89)
  waiting for transfers between devices: 19.1 us -> 7.48 us
  starting transfers between devices: 16.5 us -> 25.3 us
  Pallas kernels: 24.4 us -> 20.6 us
    ppermute x11 -> x14, waiting for transfers between devices: 16.7 us -> 5.64 us  [swap(): lax.ppermute(v, 'dp', [(i, i ^ 1 << orders[i & 1][step]) for i in range(d...]
    ppermute x11 -> x14, starting transfers between devices: 15.2 us -> 23.6 us  [swap(): lax.ppermute(v, 'dp', [(i, i ^ 1 << orders[i & 1][step]) for i in range(d...]
    pallas_call x1, Pallas kernels: 3.85 us -> 2.17 us  [panels(): pl.pallas_call(functools.partial(kernel_panels, first), out_shape=[pltpu....]
    pallas_call x1, Pallas kernels: 2.19 us -> 1.31 us  [middle(): pl.pallas_call(functools.partial(kernel_middle, first, last), out_shape=[...]
    pallas_call x1 -> x4, Pallas kernels: 2.49 us -> 1.83 us  [the longest x1 1.82 us: errors(): pl.pallas_call(functools.partial(kernel_errors, devices), out_shape=[pltp...]
    pallas_call x1, Pallas kernels: 2.29 us -> 1.64 us  [gram(): pl.pallas_call(functools.partial(kernel_gram, devices, last), out_shape=[...]
    ppermute x7 -> x9, waiting for transfers between devices: 2.38 us -> 1.83 us  [swap_core(): return lax.ppermute(v, 'dp', [(i, i ^ 1) for i in range(devices)])]
    ppermute x7 -> x9, starting transfers between devices: 1.32 us -> 1.75 us  [swap_core(): return lax.ppermute(v, 'dp', [(i, i ^ 1) for i in range(devices)])]
  transfers between devices with their start and end apart: 18 -> 23, of which waited for: 14 -> 10; matrix products, arithmetic and copies ran while one was open for 0% -> 0% of each run, Pallas kernels for 29% -> 26%
where the time goes in v3:
time: 54.6 us; the launch traced here: 54.5 us
  starting transfers between devices  25.3 us (46%)
  Pallas kernels  20.6 us (38%)
  waiting for transfers between devices  7.48 us (14%)
  between operations  0.84 us (2%)
    ppermute x14, starting transfers between devices, swap(): lax.ppermute(v, 'dp', [(i, i ^ 1 << orders[i & 1][step]) for i in range(d...  23.6 us
    pallas_call x3, Pallas kernels, grads(): pl.pallas_call(functools.partial(kernel_grads, parts), out_shape=block *...  5.83 us
    ppermute x14, waiting for transfers between devices, swap(): lax.ppermute(v, 'dp', [(i, i ^ 1 << orders[i & 1][step]) for i in range(d...  5.64 us
    pallas_call x1, Pallas kernels, load(): pl.pallas_call(functools.partial(kernel_load, devices), out_shape=[pltpu....  3.74 us
    pallas_call x1, Pallas kernels, panels(): pl.pallas_call(functools.partial(kernel_panels, first), out_shape=[pltpu....  2.17 us
    pallas_call x1, Pallas kernels, sums(): pl.pallas_call(functools.partial(kernel_sums, devices), out_shape=pltpu.V...  1.98 us
    ppermute x9, waiting for transfers between devices, swap_core(): return lax.ppermute(v, 'dp', [(i, i ^ 1) for i in range(devices)])  1.83 us
    pallas_call x1, Pallas kernels, errors(): pl.pallas_call(functools.partial(kernel_errors, devices), out_shape=[pltp...  1.82 us
  transfers between devices with their start and end apart: 23, of which 10 were waited for; matrix products, arithmetic and copies ran while one was open for 0% of the time, Pallas kernels for 26%

profile of v3, /device:TPU:0, one launch (start us, length us, event | category | flops | bytes accessed | tf_op | source)
XLA Modules:
  0.0 54.5 jit_solution(16205693012010641376)
XLA Ops:
  0.6 3.7 %load.1 = (f32[2,2,3,16,512]{4,3,2,1,0:T(8,128)S(1)}, bf16[1408,512]{1,0:T(8,128)(2,1)S(1)}, bf16[1472,512]{1,0:T(8,128)(2,1)S(1)}, bf16[1536,512]{1,0:T(8,128)(...) custom-call(bf16[2,1,1344,512]{3,2,1,0:T(8,128)(2,1)} %x_hbm.1, ...), custom_call_target="tpu_custom_call" | custom-call | flops 2000000000 | bytes 9000000 | tf_op jit(solution)/shard_map/load/pallas_call | solution.py:133
  4.4 0.5 collective-permute-start
  4.9 2.0 %sums.1 = f32[2,2,3,16,512]{4,3,2,1,0:T(8,128)S(1)} custom-call(f32[2,64,512]{2,1,0:T(8,128)S(1)} %get-tuple-element.55.q_ref, bf16[1408,512]{1,0:T(8,128)(2,1)S(1)} %get-tuple-element.56.x_ref.refs_0_.refs_3_, bf16[1472,512]{1,0:T(8,128)(2,1)S(1)} %get-tuple-element.57.o_ref.refs_1_.refs_4_, bf16[1536,512]{1,0:T(8,128)(2,1)S(1)} %get-tuple-element.58.e_ref.refs_2_.refs_5_), custom_call_target="tpu_custom_call" | custom-call | flops 2000000000 | bytes 4000000 | tf_op jit(solution)/shard_map/sums/pallas_call | solution.py:159
  6.9 0.0 collective-permute-done
  6.9 2.6 %collective-permute-start.1 = (f32[3,16,512]{2,1,0:T(8,128)S(1)}, f32[3,16,512]{2,1,0:T(8,128)S(1)}, u32[]{:S(2)}, u32[]{:S(2)}) collective-permute-start(f32[3,16,512]{2,1,0:T(8,128)S(1)} %get-tuple-element.107), channel_id=1, source_target_pairs={{0,2},{1,5},{2,0},{3,7},{4,6},{5,1},{6,4},{7,3},{8,10},{9,13},{10,... | collective-permute-start | bytes 294920 | tf_op jit(solution)/shard_map/ppermute | solution.py:487
  9.5 0.1 collective-permute-start.3
  9.6 1.9 %grads_00_01.1 = (f32[512,512]{1,0:T(8,128)S(1)}, bf16[512,512]{1,0:T(8,128)(2,1)S(1)}, bf16[512,512]{1,0:T(8,128)(2,1)S(1)}, f32[512,512]{1,0:T(8,128)S(1)}, bf...) custom-call(bf16[1408,512]{1,0:T(8,128)(2,1)S(1)} %get-tuple-element, ...), custom_call_target="tpu_custom_call" | custom-call | flops 2000000000 | bytes 6000000 | tf_op jit(solution)/shard_map/grads_00_01/pallas_call | solution.py:187
  11.5 0.6 %collective-permute-done.1 = f32[3,16,512]{2,1,0:T(8,128)S(1)} collective-permute-done((f32[3,16,512]{2,1,0:T(8,128)S(1)}, f32[3,16,512]{2,1,0:T(8,128)S(1)}, u32[]{:S(2)}, u32[]{:S(2)}) %collective-permute-start.1) | collective-permute-done | bytes 98336 | tf_op jit(solution)/shard_map/ppermute | solution.py:487
  12.1 2.2 %collective-permute-start.2 = (f32[3,16,512]{2,1,0:T(8,128)S(1)}, f32[3,16,512]{2,1,0:T(8,128)S(1)}, u32[]{:S(2)}, u32[]{:S(2)}) collective-permute-start(f32[3,16,512]{2,1,0:T(8,128)S(1)} %fusion.5), channel_id=1, source_target_pairs={{0,4},{1,9},{2,6},{3,11},{4,0},{5,13},{6,2},{7,15},{8,12},{9,1},{1... | collective-permute-start | bytes 294920 | tf_op jit(solution)/shard_map/ppermute | solution.py:487
  14.3 0.0 collective-permute-done.3
  14.3 1.5 %collective-permute-start.5 = (f32[3,16,512]{2,1,0:T(8,128)S(1)}, f32[3,16,512]{2,1,0:T(8,128)S(1)}, u32[]{:S(2)}, u32[]{:S(2)}) collective-permute-start(f32[3,16,512]{2,1,0:T(8,128)S(1)} %add_add_fusion.3.refs_6_), channel_id=1, source_target_pairs={{0,4},{1,9},{2,6},{3,11},{4,0},{5,13},{6,2},{7,15},{8,12},{9,1},{1... | collective-permute-start | bytes 294920 | tf_op jit(solution)/shard_map/ppermute | solution.py:487
  15.8 1.9 %grads_02_10.1 = (f32[512,512]{1,0:T(8,128)S(1)}, bf16[512,512]{1,0:T(8,128)(2,1)S(1)}, bf16[512,512]{1,0:T(8,128)(2,1)S(1)}, f32[512,512]{1,0:T(8,128)S(1)}, bf...) custom-call(bf16[1408,512]{1,0:T(8,128)(2,1)S(1)} %get-tuple-element, ...), custom_call_target="tpu_custom_call" | custom-call | flops 2000000000 | bytes 6000000 | tf_op jit(solution)/shard_map/grads_02_10/pallas_call | solution.py:187
  17.7 0.2 collective-permute-done.2
  17.9 2.5 %collective-permute-start.4 = (f32[3,16,512]{2,1,0:T(8,128)S(1)}, f32[3,16,512]{2,1,0:T(8,128)S(1)}, u32[]{:S(2)}, u32[]{:S(2)}) collective-permute-start(f32[3,16,512]{2,1,0:T(8,128)S(1)} %add_add_fusion.4), channel_id=1, source_target_pairs={{0,8},{1,3},{2,10},{3,1},{4,12},{5,7},{6,14},{7,5},{8,0},{9,11},{1... | collective-permute-start | bytes 294920 | tf_op jit(solution)/shard_map/ppermute | solution.py:487
  20.4 0.0 collective-permute-done.5
  20.5 1.7 %collective-permute-start.7 = (f32[3,16,512]{2,1,0:T(8,128)S(1)}, f32[3,16,512]{2,1,0:T(8,128)S(1)}, u32[]{:S(2)}, u32[]{:S(2)}) collective-permute-start(f32[3,16,512]{2,1,0:T(8,128)S(1)} %add_add_fusion.1.refs_6_), channel_id=1, source_target_pairs={{0,8},{1,3},{2,10},{3,1},{4,12},{5,7},{6,14},{7,5},{8,0},{9,11},{1... | collective-permute-start | bytes 294920 | tf_op jit(solution)/shard_map/ppermute | solution.py:487
  22.2 1.9 %grads_11_12.1 = (f32[512,512]{1,0:T(8,128)S(1)}, bf16[512,512]{1,0:T(8,128)(2,1)S(1)}, bf16[512,512]{1,0:T(8,128)(2,1)S(1)}, f32[512,512]{1,0:T(8,128)S(1)}, bf...) custom-call(bf16[1408,512]{1,0:T(8,128)(2,1)S(1)} %get-tuple-element, ...), custom_call_target="tpu_custom_call" | custom-call | flops 2000000000 | bytes 6000000 | tf_op jit(solution)/shard_map/grads_11_12/pallas_call | solution.py:187
  24.1 0.0 collective-permute-done.4
  24.2 1.6 %collective-permute-start.6 = (f32[3,16,512]{2,1,0:T(8,128)S(1)}, f32[3,16,512]{2,1,0:T(8,128)S(1)}, u32[]{:S(2)}, u32[]{:S(2)}) collective-permute-start(f32[3,16,512]{2,1,0:T(8,128)S(1)} %add_add_fusion.2.refs_0_), channel_id=1, source_target_pairs={{0,2},{1,5},{2,0},{3,7},{4,6},{5,1},{6,4},{7,3},{8,10},{9,13},{10,... | collective-permute-start | bytes 294920 | tf_op jit(solution)/shard_map/ppermute | solution.py:487
  25.7 0.4 collective-permute-done.7
  26.1 1.6 %collective-permute-start.8 = (f32[3,16,512]{2,1,0:T(8,128)S(1)}, f32[3,16,512]{2,1,0:T(8,128)S(1)}, u32[]{:S(2)}, u32[]{:S(2)}) collective-permute-start(f32[3,16,512]{2,1,0:T(8,128)S(1)} %add_add_fusion.refs_2_), channel_id=1, source_target_pairs={{0,2},{1,5},{2,0},{3,7},{4,6},{5,1},{6,4},{7,3},{8,10},{9,13},{10,... | collective-permute-start | bytes 294920 | tf_op jit(solution)/shard_map/ppermute | solution.py:487
  27.8 0.0 collective-permute-start.9
  27.8 0.5 collective-permute-start.11
  28.3 0.6 %collective-permute-done.6.refs_1_ = f32[3,16,512]{2,1,0:T(8,128)S(1)} collective-permute-done((f32[3,16,512]{2,1,0:T(8,128)S(1)}, f32[3,16,512]{2,1,0:T(8,128)S(1)}, u32[]{:S(2)}, u32[]{:S(2)}) %collective-permute-start.6) | collective-permute-done | bytes 98336 | tf_op jit(solution)/shard_map/ppermute | solution.py:487
  28.9 0.0 collective-permute-start.10
  28.9 2.0 %collective-permute-done.8.refs_3_ = f32[3,16,512]{2,1,0:T(8,128)S(1)} collective-permute-done((f32[3,16,512]{2,1,0:T(8,128)S(1)}, f32[3,16,512]{2,1,0:T(8,128)S(1)}, u32[]{:S(2)}, u32[]{:S(2)}) %collective-permute-start.8) | collective-permute-done | bytes 98336 | tf_op jit(solution)/shard_map/ppermute | solution.py:487
  30.9 1.3 %collective-permute-done.12.refs_3_.refs_7_ = f32[3,16,512]{2,1,0:T(8,128)S(1)} collective-permute-done((f32[3,16,512]{2,1,0:T(8,128)S(1)}, f32[3,16,512]{2,1,0:T(8,128)S(1)}, u32[]{:S(2)}, u32[]{:S(2)}) %collective-permute-start.12) | collective-permute-done | bytes 98336 | tf_op jit(solution)/shard_map/ppermute | solution.py:474
  32.1 0.6 %right_1.1 = (f32[32,512]{1,0:T(8,128)S(1)}, f32[32,512]{1,0:T(8,128)S(1)}) custom-call(f32[3,16,512]{2,1,0:T(8,128)S(1)} %collective-permute-done.9.refs_0_.refs_4_, f32[3,16,512]{2,1,0:T(8,128)S(1)} %collective-permute-done.10.refs_1_.refs_5_, f32[3,16,512]{2,1,0:T(8,128)S(1)} %collective-permute-done.11.refs_2_.refs_6_, ...), custom_call_target="tpu_custom_call" | custom-call | flops 1000000000 | bytes 4000000 | tf_op jit(solution)/shard_map/right_1/pallas_call | solution.py:241
  32.8 0.2 collective-permute-start.13
  33.0 0.4 collective-permute-start.16
  33.3 0.6 %right_0.1 = (f32[32,512]{1,0:T(8,128)S(1)}, f32[32,512]{1,0:T(8,128)S(1)}) custom-call(f32[3,16,512]{2,1,0:T(8,128)S(1)} %add_add_fusion.2.refs_0_, f32[3,16,512]{2,1,0:T(8,128)S(1)} %collective-permute-done.6.refs_1_, f32[3,16,512]{2,1,0:T(8,128)S(1)} %add_add_fusion.refs_2_, f32[3,16,512]{2,1,0:T(8,128)S(1)} %collective-permute-done.8.refs_3_, ...), custom_call_target="tpu_custom_call" | custom-call | flops 1000000000 | bytes 4000000 | tf_op jit(solution)/shard_map/right_0/pallas_call | solution.py:241
  34.0 0.1 collective-permute-done.13
  34.1 1.6 %collective-permute-start.14 = (f32[32,512]{1,0:T(8,128)S(1)}, f32[32,512]{1,0:T(8,128)S(1)}, u32[]{:S(2)}, u32[]{:S(2)}) collective-permute-start(f32[32,512]{1,0:T(8,128)S(1)} %add.121.refs_8_), channel_id=1, source_target_pairs={{0,2},{1,5},{2,0},{3,7},{4,6},{5,1},{6,4},{7,3},{8,10},{9,13},{10,... | collective-permute-start | bytes 196616 | tf_op jit(solution)/shard_map/ppermute | solution.py:487
  35.7 0.5 %collective-permute-start.17 = (f32[32,512]{1,0:T(8,128)S(1)}, f32[32,512]{1,0:T(8,128)S(1)}, u32[]{:S(2)}, u32[]{:S(2)}) collective-permute-start(f32[32,512]{1,0:T(8,128)S(1)} %add.126), channel_id=1, source_target_pairs={{0,2},{1,5},{2,0},{3,7},{4,6},{5,1},{6,4},{7,3},{8,10},{9,13},{10,... | collective-permute-start | bytes 196616 | tf_op jit(solution)/shard_map/ppermute | solution.py:487
  36.3 1.6 %gram.1 = (f32[2,3,64,512]{3,2,1,0:T(8,128)S(1)}, f32[2,64,128]{2,1,0:T(8,128)S(1)}, f32[32,512]{1,0:T(8,128)S(1)}, f32[32,512]{1,0:T(8,128)S(1)}) custom-call(f32[3,16,512]{2,1,0:T(8,128)S(1)} %add_add_fusion.2.refs_0_, f32[3,16,512]{2,1,0:T(8,128)S(1)} %collective-permute-done.6.refs_1_, f32[3,16,512]{2,1,0:T(8,128)S(1)} %add_add_fusion.refs_2_, ...), custom_call_target="tpu_custom_call" | custom-call | flops 2000000000 | bytes 10000000 | tf_op jit(solution)/shard_map/gram/pallas_call | solution.py:313
  37.9 0.5 collective-permute-done.14
  38.4 2.6 %collective-permute-start.15 = (f32[32,512]{1,0:T(8,128)S(1)}, f32[32,512]{1,0:T(8,128)S(1)}, u32[]{:S(2)}, u32[]{:S(2)}) collective-permute-start(f32[32,512]{1,0:T(8,128)S(1)} %add_add_fusion.10.tie_ref.refs_1_), channel_id=1, source_target_pairs={{0,4},{1,9},{2,6},{3,11},{4,0},{5,13},{6,2},{7,15},{8,12},{9,1},{1... | collective-permute-start | bytes 196616 | tf_op jit(solution)/shard_map/ppermute | solution.py:487
  41.1 2.1 %collective-permute-start.18 = (f32[32,512]{1,0:T(8,128)S(1)}, f32[32,512]{1,0:T(8,128)S(1)}, u32[]{:S(2)}, u32[]{:S(2)}) collective-permute-start(f32[32,512]{1,0:T(8,128)S(1)} %add_add_fusion.8), channel_id=1, source_target_pairs={{0,4},{1,9},{2,6},{3,11},{4,0},{5,13},{6,2},{7,15},{8,12},{9,1},{1... | collective-permute-start | bytes 196616 | tf_op jit(solution)/shard_map/ppermute | solution.py:487
  43.2 1.3 %middle_3.1 = (f32[2,64,128]{2,1,0:T(8,128)S(1)}, f32[32,512]{1,0:T(8,128)S(1)}, f32[32,512]{1,0:T(8,128)S(1)}) custom-call(f32[2,64,128]{2,1,0:T(8,128)S(1)} %get-tuple-element.84.m_ref, f32[32,512]{1,0:T(8,128)S(1)} %add_add_fusion.10.tie_ref.refs_1_), custom_call_target="tpu_custom_call" | custom-call | flops 2000000000 | bytes 10000000 | tf_op jit(solution)/shard_map/middle_3/pallas_call | solution.py:336
  44.5 1.5 %collective-permute-start.20 = (f32[32,512]{1,0:T(8,128)S(1)}, f32[32,512]{1,0:T(8,128)S(1)}, u32[]{:S(2)}, u32[]{:S(2)}) collective-permute-start(f32[32,512]{1,0:T(8,128)S(1)} %add_add_fusion.9.tie_ref.refs_1_), channel_id=1, source_target_pairs={{0,8},{1,3},{2,10},{3,1},{4,12},{5,7},{6,14},{7,5},{8,0},{9,11},{1... | collective-permute-start | bytes 196616 | tf_op jit(solution)/shard_map/ppermute | solution.py:487
  46.0 1.6 %collective-permute-start.19 = (f32[32,512]{1,0:T(8,128)S(1)}, f32[32,512]{1,0:T(8,128)S(1)}, u32[]{:S(2)}, u32[]{:S(2)}) collective-permute-start(f32[32,512]{1,0:T(8,128)S(1)} %add_add_fusion.7), channel_id=1, source_target_pairs={{0,8},{1,3},{2,10},{3,1},{4,12},{5,7},{6,14},{7,5},{8,0},{9,11},{1... | collective-permute-start | bytes 196616 | tf_op jit(solution)/shard_map/ppermute | solution.py:487
  47.6 2.2 %panels.1 = (f32[2,64,64]{2,1,0:T(8,128)S(1)}, f32[2,64,1536]{2,1,0:T(8,128)}, bf16[2,1536,192]{2,1,0:T(8,128)(2,1)S(1)}, f32[32,512]{1,0:T(8,128)S(1)}, f32[32,512]{1,0:T(8,128)S(1)}) custom-call(f32[2,3,64,512]{3,2,1,0:T(8,128)S(1)} %get-tuple-element.83.s_ref, f32[2,64,128]{2,1,0:T(8,128)S(1)} %get-tuple-element.86.m_ref, ...), custom_call_target="tpu_custom_call" | custom-call | flops 2000000000 | bytes 10000000 | tf_op jit(solution)/shard_map/panels/pallas_call | solution.py:369
  49.8 0.1 collective-permute-start.22
  49.9 1.4 %collective-permute-done.19 = f32[32,512]{1,0:T(8,128)S(1)} collective-permute-done((f32[32,512]{1,0:T(8,128)S(1)}, f32[32,512]{1,0:T(8,128)S(1)}, u32[]{:S(2)}, u32[]{:S(2)}) %collective-permute-start.19) | collective-permute-done | bytes 65568 | tf_op jit(solution)/shard_map/ppermute | solution.py:487
  51.4 0.1 collective-permute-start.21
  51.4 0.8 %own_error.1 = (f32[64,512]{1,0:T(8,128)S(1)}, bf16[1536,512]{1,0:T(8,128)(2,1)S(1)}) custom-call(f32[32,512]{1,0:T(8,128)S(1)} %add_add_fusion.5.refs_0_, f32[32,512]{1,0:T(8,128)S(1)} %add_add_fusion.6.refs_1_, f32[2,64,64]{2,1,0:T(8,128)S(1)} %get-tuple-element.95.refs_2_, bf16[2,1536,192]{2,1,0:T(8,128)(2,1)S(1)} %get-tuple-element.96.refs_3_, ...), custom_call_target="tpu_custom_call" | custom-call | flops 1000000000 | bytes 5000000 | tf_op jit(solution)/shard_map/own_error/pallas_call | solution.py:441
  52.3 0.4 collective-permute-done.21.refs_0_
  52.7 1.8 %errors.1 = (f32[2,64,512]{2,1,0:T(8,128)}, bf16[2,1536,512]{2,1,0:T(8,128)(2,1)}) custom-call(f32[32,512]{1,0:T(8,128)S(1)} %collective-permute-done.21.refs_0_, f32[32,512]{1,0:T(8,128)S(1)} %collective-permute-done.22.refs_1_, f32[2,64,64]{2,1,0:T(8,128)S(1)} %get-tuple-element.95.refs_2_, bf16[2,1536,192]{2,1,0:T(8,128)(2,1)S(1)} %get-tuple-element.96.refs_3_, ...), custom_call_target="tpu_custom_call" | custom-call | flops 1000000000 | bytes 5000000 | tf_op jit(solution)/shard_map/errors/pallas_call | solution.py:453
  (28 shorter events, 0.3 us)
Async XLA Ops:
  4.4 2.5 %collective-permute-start = (f32[2,2,3,16,512]{4,3,2,1,0:T(8,128)S(1)}, f32[2,2,3,16,512]{4,3,2,1,0:T(8,128)S(1)}, u32[]{:S(2)}, u32[]{:S(2)}) collective-permute-start(f32[2,2,3,16,512]{4,3,2,1,0:T(8,128)S(1)} %get-tuple-element.59), channel_id=1, source_target_pairs={{0,1},{1,0},{2,3},{3,2},{4,5},{5,4},{6,7},{7,6},{8,9},{9,8},{10,11... | collective-permute-start | bytes 1179656 | tf_op jit(solution)/shard_map/ppermute | solution.py:474
  6.9 5.2 %collective-permute-start.1 = (f32[3,16,512]{2,1,0:T(8,128)S(1)}, f32[3,16,512]{2,1,0:T(8,128)S(1)}, u32[]{:S(2)}, u32[]{:S(2)}) collective-permute-start(f32[3,16,512]{2,1,0:T(8,128)S(1)} %get-tuple-element.107), channel_id=1, source_target_pairs={{0,2},{1,5},{2,0},{3,7},{4,6},{5,1},{6,4},{7,3},{8,10},{9,13},{10,... | collective-permute-start | bytes 294920 | tf_op jit(solution)/shard_map/ppermute | solution.py:487
  9.5 4.8 %collective-permute-start.3 = (f32[3,16,512]{2,1,0:T(8,128)S(1)}, f32[3,16,512]{2,1,0:T(8,128)S(1)}, u32[]{:S(2)}, u32[]{:S(2)}) collective-permute-start(f32[3,16,512]{2,1,0:T(8,128)S(1)} %get-tuple-element.108), channel_id=1, source_target_pairs={{0,2},{1,5},{2,0},{3,7},{4,6},{5,1},{6,4},{7,3},{8,10},{9,13},{10,... | collective-permute-start | bytes 294920 | tf_op jit(solution)/shard_map/ppermute | solution.py:487
  12.1 5.8 %collective-permute-start.2 = (f32[3,16,512]{2,1,0:T(8,128)S(1)}, f32[3,16,512]{2,1,0:T(8,128)S(1)}, u32[]{:S(2)}, u32[]{:S(2)}) collective-permute-start(f32[3,16,512]{2,1,0:T(8,128)S(1)} %fusion.5), channel_id=1, source_target_pairs={{0,4},{1,9},{2,6},{3,11},{4,0},{5,13},{6,2},{7,15},{8,12},{9,1},{1... | collective-permute-start | bytes 294920 | tf_op jit(solution)/shard_map/ppermute | solution.py:487
  14.3 6.1 %collective-permute-start.5 = (f32[3,16,512]{2,1,0:T(8,128)S(1)}, f32[3,16,512]{2,1,0:T(8,128)S(1)}, u32[]{:S(2)}, u32[]{:S(2)}) collective-permute-start(f32[3,16,512]{2,1,0:T(8,128)S(1)} %add_add_fusion.3.refs_6_), channel_id=1, source_target_pairs={{0,4},{1,9},{2,6},{3,11},{4,0},{5,13},{6,2},{7,15},{8,12},{9,1},{1... | collective-permute-start | bytes 294920 | tf_op jit(solution)/shard_map/ppermute | solution.py:487
  17.9 6.2 %collective-permute-start.4 = (f32[3,16,512]{2,1,0:T(8,128)S(1)}, f32[3,16,512]{2,1,0:T(8,128)S(1)}, u32[]{:S(2)}, u32[]{:S(2)}) collective-permute-start(f32[3,16,512]{2,1,0:T(8,128)S(1)} %add_add_fusion.4), channel_id=1, source_target_pairs={{0,8},{1,3},{2,10},{3,1},{4,12},{5,7},{6,14},{7,5},{8,0},{9,11},{1... | collective-permute-start | bytes 294920 | tf_op jit(solution)/shard_map/ppermute | solution.py:487
  20.5 5.7 %collective-permute-start.7 = (f32[3,16,512]{2,1,0:T(8,128)S(1)}, f32[3,16,512]{2,1,0:T(8,128)S(1)}, u32[]{:S(2)}, u32[]{:S(2)}) collective-permute-start(f32[3,16,512]{2,1,0:T(8,128)S(1)} %add_add_fusion.1.refs_6_), channel_id=1, source_target_pairs={{0,8},{1,3},{2,10},{3,1},{4,12},{5,7},{6,14},{7,5},{8,0},{9,11},{1... | collective-permute-start | bytes 294920 | tf_op jit(solution)/shard_map/ppermute | solution.py:487
  24.2 4.7 %collective-permute-start.6 = (f32[3,16,512]{2,1,0:T(8,128)S(1)}, f32[3,16,512]{2,1,0:T(8,128)S(1)}, u32[]{:S(2)}, u32[]{:S(2)}) collective-permute-start(f32[3,16,512]{2,1,0:T(8,128)S(1)} %add_add_fusion.2.refs_0_), channel_id=1, source_target_pairs={{0,2},{1,5},{2,0},{3,7},{4,6},{5,1},{6,4},{7,3},{8,10},{9,13},{10,... | collective-permute-start | bytes 294920 | tf_op jit(solution)/shard_map/ppermute | solution.py:487
  26.1 4.7 %collective-permute-start.8 = (f32[3,16,512]{2,1,0:T(8,128)S(1)}, f32[3,16,512]{2,1,0:T(8,128)S(1)}, u32[]{:S(2)}, u32[]{:S(2)}) collective-permute-start(f32[3,16,512]{2,1,0:T(8,128)S(1)} %add_add_fusion.refs_2_), channel_id=1, source_target_pairs={{0,2},{1,5},{2,0},{3,7},{4,6},{5,1},{6,4},{7,3},{8,10},{9,13},{10,... | collective-permute-start | bytes 294920 | tf_op jit(solution)/shard_map/ppermute | solution.py:487
  27.8 3.1 %collective-permute-start.9 = (f32[3,16,512]{2,1,0:T(8,128)S(1)}, f32[3,16,512]{2,1,0:T(8,128)S(1)}, u32[]{:S(2)}, u32[]{:S(2)}) collective-permute-start(f32[3,16,512]{2,1,0:T(8,128)S(1)} %add_add_fusion.2.refs_0_), channel_id=1, source_target_pairs={{0,1},{1,0},{2,3},{3,2},{4,5},{5,4},{6,7},{7,6},{8,9},{9,8},{10,11... | collective-permute-start | bytes 294920 | tf_op jit(solution)/shard_map/ppermute | solution.py:474
  27.8 3.1 %collective-permute-start.11 = (f32[3,16,512]{2,1,0:T(8,128)S(1)}, f32[3,16,512]{2,1,0:T(8,128)S(1)}, u32[]{:S(2)}, u32[]{:S(2)}) collective-permute-start(f32[3,16,512]{2,1,0:T(8,128)S(1)} %add_add_fusion.refs_2_), channel_id=1, source_target_pairs={{0,1},{1,0},{2,3},{3,2},{4,5},{5,4},{6,7},{7,6},{8,9},{9,8},{10,11... | collective-permute-start | bytes 294920 | tf_op jit(solution)/shard_map/ppermute | solution.py:474
  28.9 2.0 %collective-permute-start.10 = (f32[3,16,512]{2,1,0:T(8,128)S(1)}, f32[3,16,512]{2,1,0:T(8,128)S(1)}, u32[]{:S(2)}, u32[]{:S(2)}) collective-permute-start(f32[3,16,512]{2,1,0:T(8,128)S(1)} %collective-permute-done.6.refs_1_), channel_id=1, source_target_pairs={{0,1},{1,0},{2,3},{3,2},{4,5},{5,4},{6,7},{7,6},{8,9},{9,8},{10,11... | collective-permute-start | bytes 294920 | tf_op jit(solution)/shard_map/ppermute | solution.py:474
  30.8 1.3 %collective-permute-start.12 = (f32[3,16,512]{2,1,0:T(8,128)S(1)}, f32[3,16,512]{2,1,0:T(8,128)S(1)}, u32[]{:S(2)}, u32[]{:S(2)}) collective-permute-start(f32[3,16,512]{2,1,0:T(8,128)S(1)} %collective-permute-done.8.refs_3_), channel_id=1, source_target_pairs={{0,1},{1,0},{2,3},{3,2},{4,5},{5,4},{6,7},{7,6},{8,9},{9,8},{10,11... | collective-permute-start | bytes 294920 | tf_op jit(solution)/shard_map/ppermute | solution.py:474
  32.8 1.3 %collective-permute-start.13 = (f32[32,512]{1,0:T(8,128)S(1)}, f32[32,512]{1,0:T(8,128)S(1)}, u32[]{:S(2)}, u32[]{:S(2)}) collective-permute-start(f32[32,512]{1,0:T(8,128)S(1)} %get-tuple-element.82), channel_id=1, source_target_pairs={{0,1},{1,0},{2,3},{3,2},{4,5},{5,4},{6,7},{7,6},{8,9},{9,8},{10,11... | collective-permute-start | bytes 196616 | tf_op jit(solution)/shard_map/ppermute | solution.py:474
  33.0 2.7 %collective-permute-start.16 = (f32[32,512]{1,0:T(8,128)S(1)}, f32[32,512]{1,0:T(8,128)S(1)}, u32[]{:S(2)}, u32[]{:S(2)}) collective-permute-start(f32[32,512]{1,0:T(8,128)S(1)} %get-tuple-element.90), channel_id=1, source_target_pairs={{0,1},{1,0},{2,3},{3,2},{4,5},{5,4},{6,7},{7,6},{8,9},{9,8},{10,11... | collective-permute-start | bytes 196616 | tf_op jit(solution)/shard_map/ppermute | solution.py:474
  34.1 4.3 %collective-permute-start.14 = (f32[32,512]{1,0:T(8,128)S(1)}, f32[32,512]{1,0:T(8,128)S(1)}, u32[]{:S(2)}, u32[]{:S(2)}) collective-permute-start(f32[32,512]{1,0:T(8,128)S(1)} %add.121.refs_8_), channel_id=1, source_target_pairs={{0,2},{1,5},{2,0},{3,7},{4,6},{5,1},{6,4},{7,3},{8,10},{9,13},{10,... | collective-permute-start | bytes 196616 | tf_op jit(solution)/shard_map/ppermute | solution.py:487
  35.7 5.4 %collective-permute-start.17 = (f32[32,512]{1,0:T(8,128)S(1)}, f32[32,512]{1,0:T(8,128)S(1)}, u32[]{:S(2)}, u32[]{:S(2)}) collective-permute-start(f32[32,512]{1,0:T(8,128)S(1)} %add.126), channel_id=1, source_target_pairs={{0,2},{1,5},{2,0},{3,7},{4,6},{5,1},{6,4},{7,3},{8,10},{9,13},{10,... | collective-permute-start | bytes 196616 | tf_op jit(solution)/shard_map/ppermute | solution.py:487
  38.4 6.1 %collective-permute-start.15 = (f32[32,512]{1,0:T(8,128)S(1)}, f32[32,512]{1,0:T(8,128)S(1)}, u32[]{:S(2)}, u32[]{:S(2)}) collective-permute-start(f32[32,512]{1,0:T(8,128)S(1)} %add_add_fusion.10.tie_ref.refs_1_), channel_id=1, source_target_pairs={{0,4},{1,9},{2,6},{3,11},{4,0},{5,13},{6,2},{7,15},{8,12},{9,1},{1... | collective-permute-start | bytes 196616 | tf_op jit(solution)/shard_map/ppermute | solution.py:487
  41.1 4.9 %collective-permute-start.18 = (f32[32,512]{1,0:T(8,128)S(1)}, f32[32,512]{1,0:T(8,128)S(1)}, u32[]{:S(2)}, u32[]{:S(2)}) collective-permute-start(f32[32,512]{1,0:T(8,128)S(1)} %add_add_fusion.8), channel_id=1, source_target_pairs={{0,4},{1,9},{2,6},{3,11},{4,0},{5,13},{6,2},{7,15},{8,12},{9,1},{1... | collective-permute-start | bytes 196616 | tf_op jit(solution)/shard_map/ppermute | solution.py:487
  44.5 5.3 %collective-permute-start.20 = (f32[32,512]{1,0:T(8,128)S(1)}, f32[32,512]{1,0:T(8,128)S(1)}, u32[]{:S(2)}, u32[]{:S(2)}) collective-permute-start(f32[32,512]{1,0:T(8,128)S(1)} %add_add_fusion.9.tie_ref.refs_1_), channel_id=1, source_target_pairs={{0,8},{1,3},{2,10},{3,1},{4,12},{5,7},{6,14},{7,5},{8,0},{9,11},{1... | collective-permute-start | bytes 196616 | tf_op jit(solution)/shard_map/ppermute | solution.py:487
  46.0 5.3 %collective-permute-start.19 = (f32[32,512]{1,0:T(8,128)S(1)}, f32[32,512]{1,0:T(8,128)S(1)}, u32[]{:S(2)}, u32[]{:S(2)}) collective-permute-start(f32[32,512]{1,0:T(8,128)S(1)} %add_add_fusion.7), channel_id=1, source_target_pairs={{0,8},{1,3},{2,10},{3,1},{4,12},{5,7},{6,14},{7,5},{8,0},{9,11},{1... | collective-permute-start | bytes 196616 | tf_op jit(solution)/shard_map/ppermute | solution.py:487
  49.8 2.9 %collective-permute-start.22 = (f32[32,512]{1,0:T(8,128)S(1)}, f32[32,512]{1,0:T(8,128)S(1)}, u32[]{:S(2)}, u32[]{:S(2)}) collective-permute-start(f32[32,512]{1,0:T(8,128)S(1)} %add_add_fusion.6.refs_1_), channel_id=1, source_target_pairs={{0,1},{1,0},{2,3},{3,2},{4,5},{5,4},{6,7},{7,6},{8,9},{9,8},{10,11... | collective-permute-start | bytes 196616 | tf_op jit(solution)/shard_map/ppermute | solution.py:474
  51.4 1.3 %collective-permute-start.21 = (f32[32,512]{1,0:T(8,128)S(1)}, f32[32,512]{1,0:T(8,128)S(1)}, u32[]{:S(2)}, u32[]{:S(2)}) collective-permute-start(f32[32,512]{1,0:T(8,128)S(1)} %add_add_fusion.5.refs_0_), channel_id=1, source_target_pairs={{0,1},{1,0},{2,3},{3,2},{4,5},{5,4},{6,7},{7,6},{8,9},{9,8},{10,11... | collective-permute-start | bytes 196616 | tf_op jit(solution)/shard_map/ppermute | solution.py:474

commit v4 on v3

--- a/solution.py
+++ b/solution.py
@@ -370,7 +370,7 @@
         functools.partial(kernel_panels, first),
         out_shape=[
             pltpu.VMEM((LAYERS, RANK, RANK), F32),
-            jax.ShapeDtypeStruct((LAYERS, RANK, 3 * C), F32),
+            pltpu.VMEM((LAYERS, RANK, 3 * C), F32),
             pltpu.VMEM((LAYERS, 3 * C, 3 * RANK), BF16),
         ]
         + TOKENS,
@@ -401,12 +401,16 @@
 
 
 def kernel_own_error(devices, *refs):
-    f_refs, (inv_ref, pp_ref, g0, g1, g2, factor_ref, err_ref) = refs[:STREAMS], refs[STREAMS:]
+    f_refs, (inv_ref, pp_ref, g0, g1, g2, p_ref) = refs[:STREAMS], refs[STREAMS : STREAMS + 6]
+    factor_ref, err_ref, p_hbm, sem = refs[STREAMS + 6 :]
+    copy = pltpu.make_async_copy(p_ref, p_hbm, sem)
+    copy.start()
 
     def keep_factor(f_t):
         factor_ref[...] = f_t
 
     layer_error(devices, 0, f_refs, inv_ref, pp_ref, (g0, g1, g2), err_ref, keep_factor, lambda k: None)
+    copy.wait()
 
 
 def kernel_errors(devices, *refs):
@@ -437,16 +441,17 @@
         copy.wait()
 
 
-def own_error(devices, f, inv, pp, blocks):
+def own_error(devices, f, inv, pp, blocks, panel):
     return pl.pallas_call(
         functools.partial(kernel_own_error, devices),
-        out_shape=[pltpu.VMEM((RANK, C), F32), pltpu.VMEM((3 * C, C), BF16)],
-        in_specs=[spec(pltpu.VMEM)] * (5 + STREAMS),
-        out_specs=[spec(pltpu.VMEM)] * 2,
+        out_shape=[pltpu.VMEM((RANK, C), F32), pltpu.VMEM((3 * C, C), BF16), pltpu.HBM(panel.shape, F32)],
+        in_specs=[spec(pltpu.VMEM)] * (6 + STREAMS),
+        out_specs=[spec(pltpu.VMEM)] * 2 + [spec(pltpu.HBM)],
+        scratch_shapes=[pltpu.SemaphoreType.DMA],
         compiler_params=pltpu.CompilerParams(vmem_limit_bytes=VMEM_LIMIT),
         cost_estimate=cost(10**9, 5 * 10**6),
         name="own_error",
-    )(*f, local(inv), local(pp), *[local(blocks[0, k][0]) for k in range(3)])
+    )(*f, local(inv), local(pp), *[local(blocks[0, k][0]) for k in range(3)], local(panel))
 
 
 def errors(devices, f, inv, pp, blocks, own_factor, own_err):
@@ -478,8 +483,8 @@
 
     def added_in_turn(held, arrived, tokens):
         total = list(held)
-        for i in reversed(range(STREAMS)):
-            token = tokens[i] if i == STREAMS - 1 else gate([tokens[i]], total[i + 1])[0]
+        for i in range(STREAMS):
+            token = tokens[i] if i == 0 else gate([tokens[i]], total[i - 1])[0]
             total[i] = held[i] + (arrived[i] + token)
         return total
 
@@ -522,7 +527,7 @@
             inv, panel, pp, *tokens = panels(CUTS[1], s_all, mat, f0[-1])
         f0 = added_in_turn(f0, arrived, tokens) if step < 3 else [v + w for v, w in zip(f0, arrived)]
     f1 = [swap_core(v) for v in f0]
-    own_factor, own_err = own_error(devices, f0, inv, pp, blocks)
+    own_factor, own_err, panel = own_error(devices, f0, inv, pp, blocks, panel)
     factors, error = errors(devices, f1, inv, pp, blocks, own_factor, own_err)
     return jnp.swapaxes(panel, 1, 2), jnp.swapaxes(factors, 1, 2), error
 

time: 54.6 us -> 54.6 us (level)
  Pallas kernels: 20.6 us -> 19.9 us
  waiting for transfers between devices: 7.48 us -> 8.14 us
    pallas_call x1, Pallas kernels: 2.17 us -> 1.43 us  [panels(): pl.pallas_call(functools.partial(kernel_panels, first), out_shape=[pltpu....]
    ppermute x14, waiting for transfers between devices: 5.64 us -> 6.38 us  [swap(): lax.ppermute(v, 'dp', [(i, i ^ 1 << orders[i & 1][step]) for i in range(d...]
  transfers between devices with their start and end apart: 23 -> 23, of which waited for: 10 -> 11; matrix products, arithmetic and copies ran while one was open for 0% -> 0% of each run, Pallas kernels for 26% -> 25%
where the time goes in v4:
time: 54.6 us; the launch traced here: 54.5 us
  starting transfers between devices  25.3 us (46%)
  Pallas kernels  19.9 us (36%)
  waiting for transfers between devices  8.14 us (15%)
  between operations  0.85 us (2%)
    ppermute x14, starting transfers between devices, swap(): lax.ppermute(v, 'dp', [(i, i ^ 1 << orders[i & 1][step]) for i in range(d...  23.6 us
    ppermute x14, waiting for transfers between devices, swap(): lax.ppermute(v, 'dp', [(i, i ^ 1 << orders[i & 1][step]) for i in range(d...  6.38 us
    pallas_call x3, Pallas kernels, grads(): pl.pallas_call(functools.partial(kernel_grads, parts), out_shape=block *...  5.83 us
    pallas_call x1, Pallas kernels, load(): pl.pallas_call(functools.partial(kernel_load, devices), out_shape=[pltpu....  3.74 us
    pallas_call x1, Pallas kernels, sums(): pl.pallas_call(functools.partial(kernel_sums, devices), out_shape=pltpu.V...  1.98 us
    pallas_call x1, Pallas kernels, errors(): pl.pallas_call(functools.partial(kernel_errors, devices), out_shape=[pltp...  1.82 us
    ppermute x9, waiting for transfers between devices, swap_core(): return lax.ppermute(v, 'dp', [(i, i ^ 1) for i in range(devices)])  1.76 us
    ppermute x9, starting transfers between devices, swap_core(): return lax.ppermute(v, 'dp', [(i, i ^ 1) for i in range(devices)])  1.75 us
  transfers between devices with their start and end apart: 23, of which 11 were waited for; matrix products, arithmetic and copies ran while one was open for 0% of the time, Pallas kernels for 25%

profile of v4, /device:TPU:0, one launch (start us, length us, event | category | flops | bytes accessed | tf_op | source)
XLA Modules:
  0.0 54.5 jit_solution(13308979351483054089)
XLA Ops:
  0.6 3.7 %load.1 = (f32[2,2,3,16,512]{4,3,2,1,0:T(8,128)S(1)}, bf16[1408,512]{1,0:T(8,128)(2,1)S(1)}, bf16[1472,512]{1,0:T(8,128)(2,1)S(1)}, bf16[1536,512]{1,0:T(8,128)(...) custom-call(bf16[2,1,1344,512]{3,2,1,0:T(8,128)(2,1)} %x_hbm.1, ...), custom_call_target="tpu_custom_call" | custom-call | flops 2000000000 | bytes 9000000 | tf_op jit(solution)/shard_map/load/pallas_call | solution.py:133
  4.4 0.5 collective-permute-start
  4.9 2.0 %sums.1 = f32[2,2,3,16,512]{4,3,2,1,0:T(8,128)S(1)} custom-call(f32[2,64,512]{2,1,0:T(8,128)S(1)} %get-tuple-element.56.q_ref, bf16[1408,512]{1,0:T(8,128)(2,1)S(1)} %get-tuple-element.57.x_ref.refs_0_.refs_3_, bf16[1472,512]{1,0:T(8,128)(2,1)S(1)} %get-tuple-element.58.o_ref.refs_1_.refs_4_, bf16[1536,512]{1,0:T(8,128)(2,1)S(1)} %get-tuple-element.59.e_ref.refs_2_.refs_5_), custom_call_target="tpu_custom_call" | custom-call | flops 2000000000 | bytes 4000000 | tf_op jit(solution)/shard_map/sums/pallas_call | solution.py:159
  6.9 0.0 collective-permute-done
  6.9 2.6 %collective-permute-start.1 = (f32[3,16,512]{2,1,0:T(8,128)S(1)}, f32[3,16,512]{2,1,0:T(8,128)S(1)}, u32[]{:S(2)}, u32[]{:S(2)}) collective-permute-start(f32[3,16,512]{2,1,0:T(8,128)S(1)} %get-tuple-element.109), channel_id=1, source_target_pairs={{0,2},{1,5},{2,0},{3,7},{4,6},{5,1},{6,4},{7,3},{8,10},{9,13},{10,... | collective-permute-start | bytes 294920 | tf_op jit(solution)/shard_map/ppermute | solution.py:492
  9.5 0.1 collective-permute-start.3
  9.6 1.9 %grads_00_01.1 = (f32[512,512]{1,0:T(8,128)S(1)}, bf16[512,512]{1,0:T(8,128)(2,1)S(1)}, bf16[512,512]{1,0:T(8,128)(2,1)S(1)}, f32[512,512]{1,0:T(8,128)S(1)}, bf...) custom-call(bf16[1408,512]{1,0:T(8,128)(2,1)S(1)} %get-tuple-element, ...), custom_call_target="tpu_custom_call" | custom-call | flops 2000000000 | bytes 6000000 | tf_op jit(solution)/shard_map/grads_00_01/pallas_call | solution.py:187
  11.5 0.6 %collective-permute-done.1 = f32[3,16,512]{2,1,0:T(8,128)S(1)} collective-permute-done((f32[3,16,512]{2,1,0:T(8,128)S(1)}, f32[3,16,512]{2,1,0:T(8,128)S(1)}, u32[]{:S(2)}, u32[]{:S(2)}) %collective-permute-start.1) | collective-permute-done | bytes 98336 | tf_op jit(solution)/shard_map/ppermute | solution.py:492
  12.1 2.2 %collective-permute-start.2 = (f32[3,16,512]{2,1,0:T(8,128)S(1)}, f32[3,16,512]{2,1,0:T(8,128)S(1)}, u32[]{:S(2)}, u32[]{:S(2)}) collective-permute-start(f32[3,16,512]{2,1,0:T(8,128)S(1)} %fusion.5), channel_id=1, source_target_pairs={{0,4},{1,9},{2,6},{3,11},{4,0},{5,13},{6,2},{7,15},{8,12},{9,1},{1... | collective-permute-start | bytes 294920 | tf_op jit(solution)/shard_map/ppermute | solution.py:492
  14.3 0.0 collective-permute-done.3
  14.3 1.5 %collective-permute-start.5 = (f32[3,16,512]{2,1,0:T(8,128)S(1)}, f32[3,16,512]{2,1,0:T(8,128)S(1)}, u32[]{:S(2)}, u32[]{:S(2)}) collective-permute-start(f32[3,16,512]{2,1,0:T(8,128)S(1)} %add_add_fusion.3.refs_6_), channel_id=1, source_target_pairs={{0,4},{1,9},{2,6},{3,11},{4,0},{5,13},{6,2},{7,15},{8,12},{9,1},{1... | collective-permute-start | bytes 294920 | tf_op jit(solution)/shard_map/ppermute | solution.py:492
  15.8 1.9 %grads_02_10.1 = (f32[512,512]{1,0:T(8,128)S(1)}, bf16[512,512]{1,0:T(8,128)(2,1)S(1)}, bf16[512,512]{1,0:T(8,128)(2,1)S(1)}, f32[512,512]{1,0:T(8,128)S(1)}, bf...) custom-call(bf16[1408,512]{1,0:T(8,128)(2,1)S(1)} %get-tuple-element, ...), custom_call_target="tpu_custom_call" | custom-call | flops 2000000000 | bytes 6000000 | tf_op jit(solution)/shard_map/grads_02_10/pallas_call | solution.py:187
  17.7 0.2 collective-permute-done.2
  17.9 2.5 %collective-permute-start.4 = (f32[3,16,512]{2,1,0:T(8,128)S(1)}, f32[3,16,512]{2,1,0:T(8,128)S(1)}, u32[]{:S(2)}, u32[]{:S(2)}) collective-permute-start(f32[3,16,512]{2,1,0:T(8,128)S(1)} %add_add_fusion.4), channel_id=1, source_target_pairs={{0,8},{1,3},{2,10},{3,1},{4,12},{5,7},{6,14},{7,5},{8,0},{9,11},{1... | collective-permute-start | bytes 294920 | tf_op jit(solution)/shard_map/ppermute | solution.py:492
  20.4 0.0 collective-permute-done.5
  20.5 1.7 %collective-permute-start.7 = (f32[3,16,512]{2,1,0:T(8,128)S(1)}, f32[3,16,512]{2,1,0:T(8,128)S(1)}, u32[]{:S(2)}, u32[]{:S(2)}) collective-permute-start(f32[3,16,512]{2,1,0:T(8,128)S(1)} %add_add_fusion.1.refs_6_), channel_id=1, source_target_pairs={{0,8},{1,3},{2,10},{3,1},{4,12},{5,7},{6,14},{7,5},{8,0},{9,11},{1... | collective-permute-start | bytes 294920 | tf_op jit(solution)/shard_map/ppermute | solution.py:492
  22.2 1.9 %grads_11_12.1 = (f32[512,512]{1,0:T(8,128)S(1)}, bf16[512,512]{1,0:T(8,128)(2,1)S(1)}, bf16[512,512]{1,0:T(8,128)(2,1)S(1)}, f32[512,512]{1,0:T(8,128)S(1)}, bf...) custom-call(bf16[1408,512]{1,0:T(8,128)(2,1)S(1)} %get-tuple-element, ...), custom_call_target="tpu_custom_call" | custom-call | flops 2000000000 | bytes 6000000 | tf_op jit(solution)/shard_map/grads_11_12/pallas_call | solution.py:187
  24.1 0.0 collective-permute-done.4
  24.2 1.6 %collective-permute-start.6 = (f32[3,16,512]{2,1,0:T(8,128)S(1)}, f32[3,16,512]{2,1,0:T(8,128)S(1)}, u32[]{:S(2)}, u32[]{:S(2)}) collective-permute-start(f32[3,16,512]{2,1,0:T(8,128)S(1)} %add_add_fusion.2.refs_0_), channel_id=1, source_target_pairs={{0,2},{1,5},{2,0},{3,7},{4,6},{5,1},{6,4},{7,3},{8,10},{9,13},{10,... | collective-permute-start | bytes 294920 | tf_op jit(solution)/shard_map/ppermute | solution.py:492
  25.7 0.4 collective-permute-done.7
  26.1 1.6 %collective-permute-start.8 = (f32[3,16,512]{2,1,0:T(8,128)S(1)}, f32[3,16,512]{2,1,0:T(8,128)S(1)}, u32[]{:S(2)}, u32[]{:S(2)}) collective-permute-start(f32[3,16,512]{2,1,0:T(8,128)S(1)} %add_add_fusion.refs_2_), channel_id=1, source_target_pairs={{0,2},{1,5},{2,0},{3,7},{4,6},{5,1},{6,4},{7,3},{8,10},{9,13},{10,... | collective-permute-start | bytes 294920 | tf_op jit(solution)/shard_map/ppermute | solution.py:492
  27.8 0.0 collective-permute-start.9
  27.8 0.5 collective-permute-start.11
  28.3 0.6 %collective-permute-done.6.refs_1_ = f32[3,16,512]{2,1,0:T(8,128)S(1)} collective-permute-done((f32[3,16,512]{2,1,0:T(8,128)S(1)}, f32[3,16,512]{2,1,0:T(8,128)S(1)}, u32[]{:S(2)}, u32[]{:S(2)}) %collective-permute-start.6) | collective-permute-done | bytes 98336 | tf_op jit(solution)/shard_map/ppermute | solution.py:492
  28.9 2.0 %collective-permute-done.8.refs_3_ = f32[3,16,512]{2,1,0:T(8,128)S(1)} collective-permute-done((f32[3,16,512]{2,1,0:T(8,128)S(1)}, f32[3,16,512]{2,1,0:T(8,128)S(1)}, u32[]{:S(2)}, u32[]{:S(2)}) %collective-permute-start.8) | collective-permute-done | bytes 98336 | tf_op jit(solution)/shard_map/ppermute | solution.py:492
  30.9 1.3 %collective-permute-done.12.refs_3_.refs_7_ = f32[3,16,512]{2,1,0:T(8,128)S(1)} collective-permute-done((f32[3,16,512]{2,1,0:T(8,128)S(1)}, f32[3,16,512]{2,1,0:T(8,128)S(1)}, u32[]{:S(2)}, u32[]{:S(2)}) %collective-permute-start.12) | collective-permute-done | bytes 98336 | tf_op jit(solution)/shard_map/ppermute | solution.py:479
  32.1 0.6 %right_1.1 = (f32[32,512]{1,0:T(8,128)S(1)}, f32[32,512]{1,0:T(8,128)S(1)}) custom-call(f32[3,16,512]{2,1,0:T(8,128)S(1)} %collective-permute-done.9.refs_0_.refs_4_, f32[3,16,512]{2,1,0:T(8,128)S(1)} %collective-permute-done.10.refs_1_.refs_5_, f32[3,16,512]{2,1,0:T(8,128)S(1)} %collective-permute-done.11.refs_2_.refs_6_, ...), custom_call_target="tpu_custom_call" | custom-call | flops 1000000000 | bytes 4000000 | tf_op jit(solution)/shard_map/right_1/pallas_call | solution.py:241
  32.8 0.2 collective-permute-start.13
  33.0 0.4 collective-permute-start.15
  33.3 0.6 %right_0.1 = (f32[32,512]{1,0:T(8,128)S(1)}, f32[32,512]{1,0:T(8,128)S(1)}) custom-call(f32[3,16,512]{2,1,0:T(8,128)S(1)} %add_add_fusion.2.refs_0_, f32[3,16,512]{2,1,0:T(8,128)S(1)} %collective-permute-done.6.refs_1_, f32[3,16,512]{2,1,0:T(8,128)S(1)} %add_add_fusion.refs_2_, f32[3,16,512]{2,1,0:T(8,128)S(1)} %collective-permute-done.8.refs_3_, ...), custom_call_target="tpu_custom_call" | custom-call | flops 1000000000 | bytes 4000000 | tf_op jit(solution)/shard_map/right_0/pallas_call | solution.py:241
  34.0 0.1 collective-permute-done.13
  34.1 1.6 %collective-permute-start.14 = (f32[32,512]{1,0:T(8,128)S(1)}, f32[32,512]{1,0:T(8,128)S(1)}, u32[]{:S(2)}, u32[]{:S(2)}) collective-permute-start(f32[32,512]{1,0:T(8,128)S(1)} %add.121), channel_id=1, source_target_pairs={{0,2},{1,5},{2,0},{3,7},{4,6},{5,1},{6,4},{7,3},{8,10},{9,13},{10,... | collective-permute-start | bytes 196616 | tf_op jit(solution)/shard_map/ppermute | solution.py:492
  35.7 0.5 %collective-permute-start.17 = (f32[32,512]{1,0:T(8,128)S(1)}, f32[32,512]{1,0:T(8,128)S(1)}, u32[]{:S(2)}, u32[]{:S(2)}) collective-permute-start(f32[32,512]{1,0:T(8,128)S(1)} %add.122.refs_8_), channel_id=1, source_target_pairs={{0,2},{1,5},{2,0},{3,7},{4,6},{5,1},{6,4},{7,3},{8,10},{9,13},{10,... | collective-permute-start | bytes 196616 | tf_op jit(solution)/shard_map/ppermute | solution.py:492
  36.3 1.6 %gram.1 = (f32[2,3,64,512]{3,2,1,0:T(8,128)S(1)}, f32[2,64,128]{2,1,0:T(8,128)S(1)}, f32[32,512]{1,0:T(8,128)S(1)}, f32[32,512]{1,0:T(8,128)S(1)}) custom-call(f32[3,16,512]{2,1,0:T(8,128)S(1)} %add_add_fusion.2.refs_0_, f32[3,16,512]{2,1,0:T(8,128)S(1)} %collective-permute-done.6.refs_1_, f32[3,16,512]{2,1,0:T(8,128)S(1)} %add_add_fusion.refs_2_, ...), custom_call_target="tpu_custom_call" | custom-call | flops 2000000000 | bytes 10000000 | tf_op jit(solution)/shard_map/gram/pallas_call | solution.py:313
  37.9 0.5 collective-permute-done.14
  38.4 2.6 %collective-permute-start.16 = (f32[32,512]{1,0:T(8,128)S(1)}, f32[32,512]{1,0:T(8,128)S(1)}, u32[]{:S(2)}, u32[]{:S(2)}) collective-permute-start(f32[32,512]{1,0:T(8,128)S(1)} %add_add_fusion.10.refs_1_), channel_id=1, source_target_pairs={{0,4},{1,9},{2,6},{3,11},{4,0},{5,13},{6,2},{7,15},{8,12},{9,1},{1... | collective-permute-start | bytes 196616 | tf_op jit(solution)/shard_map/ppermute | solution.py:492
  41.1 2.1 %collective-permute-start.19 = (f32[32,512]{1,0:T(8,128)S(1)}, f32[32,512]{1,0:T(8,128)S(1)}, u32[]{:S(2)}, u32[]{:S(2)}) collective-permute-start(f32[32,512]{1,0:T(8,128)S(1)} %add_add_fusion.9.tie_ref), channel_id=1, source_target_pairs={{0,4},{1,9},{2,6},{3,11},{4,0},{5,13},{6,2},{7,15},{8,12},{9,1},{1... | collective-permute-start | bytes 196616 | tf_op jit(solution)/shard_map/ppermute | solution.py:492
  43.2 1.3 %middle_3.1 = (f32[2,64,128]{2,1,0:T(8,128)S(1)}, f32[32,512]{1,0:T(8,128)S(1)}, f32[32,512]{1,0:T(8,128)S(1)}) custom-call(f32[2,64,128]{2,1,0:T(8,128)S(1)} %get-tuple-element.87.m_ref, f32[32,512]{1,0:T(8,128)S(1)} %add_add_fusion.9.tie_ref), custom_call_target="tpu_custom_call" | custom-call | flops 2000000000 | bytes 10000000 | tf_op jit(solution)/shard_map/middle_3/pallas_call | solution.py:336
  44.5 1.5 %collective-permute-start.18 = (f32[32,512]{1,0:T(8,128)S(1)}, f32[32,512]{1,0:T(8,128)S(1)}, u32[]{:S(2)}, u32[]{:S(2)}) collective-permute-start(f32[32,512]{1,0:T(8,128)S(1)} %add_add_fusion.8.refs_1_), channel_id=1, source_target_pairs={{0,8},{1,3},{2,10},{3,1},{4,12},{5,7},{6,14},{7,5},{8,0},{9,11},{1... | collective-permute-start | bytes 196616 | tf_op jit(solution)/shard_map/ppermute | solution.py:492
  46.0 1.6 %collective-permute-start.20 = (f32[32,512]{1,0:T(8,128)S(1)}, f32[32,512]{1,0:T(8,128)S(1)}, u32[]{:S(2)}, u32[]{:S(2)}) collective-permute-start(f32[32,512]{1,0:T(8,128)S(1)} %add_add_fusion.7.tie_ref), channel_id=1, source_target_pairs={{0,8},{1,3},{2,10},{3,1},{4,12},{5,7},{6,14},{7,5},{8,0},{9,11},{1... | collective-permute-start | bytes 196616 | tf_op jit(solution)/shard_map/ppermute | solution.py:492
  47.6 1.4 %panels.1 = (f32[2,64,64]{2,1,0:T(8,128)S(1)}, f32[2,64,1536]{2,1,0:T(8,128)S(1)}, bf16[2,1536,192]{2,1,0:T(8,128)(2,1)S(1)}, f32[32,512]{1,0:T(8,128)S(1)}, f32[32,512]{1,0:T(8,128)S(1)}) custom-call(f32[2,3,64,512]{3,2,1,0:T(8,128)S(1)} %get-tuple-element.90.s_ref, f32[2,64,128]{2,1,0:T(8,128)S(1)} %get-tuple-element.91.m_ref, ...), custom_call_target="tpu_custom_call" | custom-call | flops 2000000000 | bytes 10000000 | tf_op jit(solution)/shard_map/panels/pallas_call | solution.py:369
  49.0 0.7 %collective-permute-done.18 = f32[32,512]{1,0:T(8,128)S(1)} collective-permute-done((f32[32,512]{1,0:T(8,128)S(1)}, f32[32,512]{1,0:T(8,128)S(1)}, u32[]{:S(2)}, u32[]{:S(2)}) %collective-permute-start.18) | collective-permute-done | bytes 65568 | tf_op jit(solution)/shard_map/ppermute | solution.py:492
  49.8 0.1 collective-permute-start.21
  49.9 1.5 %collective-permute-done.20 = f32[32,512]{1,0:T(8,128)S(1)} collective-permute-done((f32[32,512]{1,0:T(8,128)S(1)}, f32[32,512]{1,0:T(8,128)S(1)}, u32[]{:S(2)}, u32[]{:S(2)}) %collective-permute-start.20) | collective-permute-done | bytes 65568 | tf_op jit(solution)/shard_map/ppermute | solution.py:492
  51.4 0.1 collective-permute-start.22
  51.4 0.9 %own_error.1 = (f32[64,512]{1,0:T(8,128)S(1)}, bf16[1536,512]{1,0:T(8,128)(2,1)S(1)}, f32[2,64,1536]{2,1,0:T(8,128)}) custom-call(f32[32,512]{1,0:T(8,128)S(1)} %add_add_fusion.6.refs_1_.refs_0_, f32[32,512]{1,0:T(8,128)S(1)} %add_add_fusion.5.refs_1_, f32[2,64,64]{2,1,0:T(8,128)S(1)} %get-tuple-element.95.refs_2_, ...), custom_call_target="tpu_custom_call" | custom-call | flops 1000000000 | bytes 5000000 | tf_op jit(solution)/shard_map/own_error/pallas_call | solution.py:445
  52.3 0.3 collective-permute-done.22.refs_1_
  52.7 1.8 %errors.1 = (f32[2,64,512]{2,1,0:T(8,128)}, bf16[2,1536,512]{2,1,0:T(8,128)(2,1)}) custom-call(f32[32,512]{1,0:T(8,128)S(1)} %collective-permute-done.21.refs_0_, f32[32,512]{1,0:T(8,128)S(1)} %collective-permute-done.22.refs_1_, f32[2,64,64]{2,1,0:T(8,128)S(1)} %get-tuple-element.95.refs_2_, bf16[2,1536,192]{2,1,0:T(8,128)(2,1)S(1)} %get-tuple-element.96.refs_3_, ...), custom_call_target="tpu_custom_call" | custom-call | flops 1000000000 | bytes 5000000 | tf_op jit(solution)/shard_map/errors/pallas_call | solution.py:458
  (28 shorter events, 0.3 us)
Async XLA Ops:
  4.4 2.5 %collective-permute-start = (f32[2,2,3,16,512]{4,3,2,1,0:T(8,128)S(1)}, f32[2,2,3,16,512]{4,3,2,1,0:T(8,128)S(1)}, u32[]{:S(2)}, u32[]{:S(2)}) collective-permute-start(f32[2,2,3,16,512]{4,3,2,1,0:T(8,128)S(1)} %get-tuple-element.60), channel_id=1, source_target_pairs={{0,1},{1,0},{2,3},{3,2},{4,5},{5,4},{6,7},{7,6},{8,9},{9,8},{10,11... | collective-permute-start | bytes 1179656 | tf_op jit(solution)/shard_map/ppermute | solution.py:479
  6.9 5.2 %collective-permute-start.1 = (f32[3,16,512]{2,1,0:T(8,128)S(1)}, f32[3,16,512]{2,1,0:T(8,128)S(1)}, u32[]{:S(2)}, u32[]{:S(2)}) collective-permute-start(f32[3,16,512]{2,1,0:T(8,128)S(1)} %get-tuple-element.109), channel_id=1, source_target_pairs={{0,2},{1,5},{2,0},{3,7},{4,6},{5,1},{6,4},{7,3},{8,10},{9,13},{10,... | collective-permute-start | bytes 294920 | tf_op jit(solution)/shard_map/ppermute | solution.py:492
  9.5 4.8 %collective-permute-start.3 = (f32[3,16,512]{2,1,0:T(8,128)S(1)}, f32[3,16,512]{2,1,0:T(8,128)S(1)}, u32[]{:S(2)}, u32[]{:S(2)}) collective-permute-start(f32[3,16,512]{2,1,0:T(8,128)S(1)} %get-tuple-element.110), channel_id=1, source_target_pairs={{0,2},{1,5},{2,0},{3,7},{4,6},{5,1},{6,4},{7,3},{8,10},{9,13},{10,... | collective-permute-start | bytes 294920 | tf_op jit(solution)/shard_map/ppermute | solution.py:492
  12.1 5.8 %collective-permute-start.2 = (f32[3,16,512]{2,1,0:T(8,128)S(1)}, f32[3,16,512]{2,1,0:T(8,128)S(1)}, u32[]{:S(2)}, u32[]{:S(2)}) collective-permute-start(f32[3,16,512]{2,1,0:T(8,128)S(1)} %fusion.5), channel_id=1, source_target_pairs={{0,4},{1,9},{2,6},{3,11},{4,0},{5,13},{6,2},{7,15},{8,12},{9,1},{1... | collective-permute-start | bytes 294920 | tf_op jit(solution)/shard_map/ppermute | solution.py:492
  14.3 6.1 %collective-permute-start.5 = (f32[3,16,512]{2,1,0:T(8,128)S(1)}, f32[3,16,512]{2,1,0:T(8,128)S(1)}, u32[]{:S(2)}, u32[]{:S(2)}) collective-permute-start(f32[3,16,512]{2,1,0:T(8,128)S(1)} %add_add_fusion.3.refs_6_), channel_id=1, source_target_pairs={{0,4},{1,9},{2,6},{3,11},{4,0},{5,13},{6,2},{7,15},{8,12},{9,1},{1... | collective-permute-start | bytes 294920 | tf_op jit(solution)/shard_map/ppermute | solution.py:492
  17.9 6.2 %collective-permute-start.4 = (f32[3,16,512]{2,1,0:T(8,128)S(1)}, f32[3,16,512]{2,1,0:T(8,128)S(1)}, u32[]{:S(2)}, u32[]{:S(2)}) collective-permute-start(f32[3,16,512]{2,1,0:T(8,128)S(1)} %add_add_fusion.4), channel_id=1, source_target_pairs={{0,8},{1,3},{2,10},{3,1},{4,12},{5,7},{6,14},{7,5},{8,0},{9,11},{1... | collective-permute-start | bytes 294920 | tf_op jit(solution)/shard_map/ppermute | solution.py:492
  20.5 5.7 %collective-permute-start.7 = (f32[3,16,512]{2,1,0:T(8,128)S(1)}, f32[3,16,512]{2,1,0:T(8,128)S(1)}, u32[]{:S(2)}, u32[]{:S(2)}) collective-permute-start(f32[3,16,512]{2,1,0:T(8,128)S(1)} %add_add_fusion.1.refs_6_), channel_id=1, source_target_pairs={{0,8},{1,3},{2,10},{3,1},{4,12},{5,7},{6,14},{7,5},{8,0},{9,11},{1... | collective-permute-start | bytes 294920 | tf_op jit(solution)/shard_map/ppermute | solution.py:492
  24.2 4.7 %collective-permute-start.6 = (f32[3,16,512]{2,1,0:T(8,128)S(1)}, f32[3,16,512]{2,1,0:T(8,128)S(1)}, u32[]{:S(2)}, u32[]{:S(2)}) collective-permute-start(f32[3,16,512]{2,1,0:T(8,128)S(1)} %add_add_fusion.2.refs_0_), channel_id=1, source_target_pairs={{0,2},{1,5},{2,0},{3,7},{4,6},{5,1},{6,4},{7,3},{8,10},{9,13},{10,... | collective-permute-start | bytes 294920 | tf_op jit(solution)/shard_map/ppermute | solution.py:492
  26.1 4.7 %collective-permute-start.8 = (f32[3,16,512]{2,1,0:T(8,128)S(1)}, f32[3,16,512]{2,1,0:T(8,128)S(1)}, u32[]{:S(2)}, u32[]{:S(2)}) collective-permute-start(f32[3,16,512]{2,1,0:T(8,128)S(1)} %add_add_fusion.refs_2_), channel_id=1, source_target_pairs={{0,2},{1,5},{2,0},{3,7},{4,6},{5,1},{6,4},{7,3},{8,10},{9,13},{10,... | collective-permute-start | bytes 294920 | tf_op jit(solution)/shard_map/ppermute | solution.py:492
  27.8 3.1 %collective-permute-start.9 = (f32[3,16,512]{2,1,0:T(8,128)S(1)}, f32[3,16,512]{2,1,0:T(8,128)S(1)}, u32[]{:S(2)}, u32[]{:S(2)}) collective-permute-start(f32[3,16,512]{2,1,0:T(8,128)S(1)} %add_add_fusion.2.refs_0_), channel_id=1, source_target_pairs={{0,1},{1,0},{2,3},{3,2},{4,5},{5,4},{6,7},{7,6},{8,9},{9,8},{10,11... | collective-permute-start | bytes 294920 | tf_op jit(solution)/shard_map/ppermute | solution.py:479
  27.8 3.1 %collective-permute-start.11 = (f32[3,16,512]{2,1,0:T(8,128)S(1)}, f32[3,16,512]{2,1,0:T(8,128)S(1)}, u32[]{:S(2)}, u32[]{:S(2)}) collective-permute-start(f32[3,16,512]{2,1,0:T(8,128)S(1)} %add_add_fusion.refs_2_), channel_id=1, source_target_pairs={{0,1},{1,0},{2,3},{3,2},{4,5},{5,4},{6,7},{7,6},{8,9},{9,8},{10,11... | collective-permute-start | bytes 294920 | tf_op jit(solution)/shard_map/ppermute | solution.py:479
  28.9 2.0 %collective-permute-start.10 = (f32[3,16,512]{2,1,0:T(8,128)S(1)}, f32[3,16,512]{2,1,0:T(8,128)S(1)}, u32[]{:S(2)}, u32[]{:S(2)}) collective-permute-start(f32[3,16,512]{2,1,0:T(8,128)S(1)} %collective-permute-done.6.refs_1_), channel_id=1, source_target_pairs={{0,1},{1,0},{2,3},{3,2},{4,5},{5,4},{6,7},{7,6},{8,9},{9,8},{10,11... | collective-permute-start | bytes 294920 | tf_op jit(solution)/shard_map/ppermute | solution.py:479
  30.8 1.3 %collective-permute-start.12 = (f32[3,16,512]{2,1,0:T(8,128)S(1)}, f32[3,16,512]{2,1,0:T(8,128)S(1)}, u32[]{:S(2)}, u32[]{:S(2)}) collective-permute-start(f32[3,16,512]{2,1,0:T(8,128)S(1)} %collective-permute-done.8.refs_3_), channel_id=1, source_target_pairs={{0,1},{1,0},{2,3},{3,2},{4,5},{5,4},{6,7},{7,6},{8,9},{9,8},{10,11... | collective-permute-start | bytes 294920 | tf_op jit(solution)/shard_map/ppermute | solution.py:479
  32.8 1.3 %collective-permute-start.13 = (f32[32,512]{1,0:T(8,128)S(1)}, f32[32,512]{1,0:T(8,128)S(1)}, u32[]{:S(2)}, u32[]{:S(2)}) collective-permute-start(f32[32,512]{1,0:T(8,128)S(1)} %get-tuple-element.83), channel_id=1, source_target_pairs={{0,1},{1,0},{2,3},{3,2},{4,5},{5,4},{6,7},{7,6},{8,9},{9,8},{10,11... | collective-permute-start | bytes 196616 | tf_op jit(solution)/shard_map/ppermute | solution.py:479
  33.0 2.7 %collective-permute-start.15 = (f32[32,512]{1,0:T(8,128)S(1)}, f32[32,512]{1,0:T(8,128)S(1)}, u32[]{:S(2)}, u32[]{:S(2)}) collective-permute-start(f32[32,512]{1,0:T(8,128)S(1)} %get-tuple-element.85), channel_id=1, source_target_pairs={{0,1},{1,0},{2,3},{3,2},{4,5},{5,4},{6,7},{7,6},{8,9},{9,8},{10,11... | collective-permute-start | bytes 196616 | tf_op jit(solution)/shard_map/ppermute | solution.py:479
  34.1 4.3 %collective-permute-start.14 = (f32[32,512]{1,0:T(8,128)S(1)}, f32[32,512]{1,0:T(8,128)S(1)}, u32[]{:S(2)}, u32[]{:S(2)}) collective-permute-start(f32[32,512]{1,0:T(8,128)S(1)} %add.121), channel_id=1, source_target_pairs={{0,2},{1,5},{2,0},{3,7},{4,6},{5,1},{6,4},{7,3},{8,10},{9,13},{10,... | collective-permute-start | bytes 196616 | tf_op jit(solution)/shard_map/ppermute | solution.py:492
  35.7 5.4 %collective-permute-start.17 = (f32[32,512]{1,0:T(8,128)S(1)}, f32[32,512]{1,0:T(8,128)S(1)}, u32[]{:S(2)}, u32[]{:S(2)}) collective-permute-start(f32[32,512]{1,0:T(8,128)S(1)} %add.122.refs_8_), channel_id=1, source_target_pairs={{0,2},{1,5},{2,0},{3,7},{4,6},{5,1},{6,4},{7,3},{8,10},{9,13},{10,... | collective-permute-start | bytes 196616 | tf_op jit(solution)/shard_map/ppermute | solution.py:492
  38.4 6.1 %collective-permute-start.16 = (f32[32,512]{1,0:T(8,128)S(1)}, f32[32,512]{1,0:T(8,128)S(1)}, u32[]{:S(2)}, u32[]{:S(2)}) collective-permute-start(f32[32,512]{1,0:T(8,128)S(1)} %add_add_fusion.10.refs_1_), channel_id=1, source_target_pairs={{0,4},{1,9},{2,6},{3,11},{4,0},{5,13},{6,2},{7,15},{8,12},{9,1},{1... | collective-permute-start | bytes 196616 | tf_op jit(solution)/shard_map/ppermute | solution.py:492
  41.1 4.9 %collective-permute-start.19 = (f32[32,512]{1,0:T(8,128)S(1)}, f32[32,512]{1,0:T(8,128)S(1)}, u32[]{:S(2)}, u32[]{:S(2)}) collective-permute-start(f32[32,512]{1,0:T(8,128)S(1)} %add_add_fusion.9.tie_ref), channel_id=1, source_target_pairs={{0,4},{1,9},{2,6},{3,11},{4,0},{5,13},{6,2},{7,15},{8,12},{9,1},{1... | collective-permute-start | bytes 196616 | tf_op jit(solution)/shard_map/ppermute | solution.py:492
  44.5 5.2 %collective-permute-start.18 = (f32[32,512]{1,0:T(8,128)S(1)}, f32[32,512]{1,0:T(8,128)S(1)}, u32[]{:S(2)}, u32[]{:S(2)}) collective-permute-start(f32[32,512]{1,0:T(8,128)S(1)} %add_add_fusion.8.refs_1_), channel_id=1, source_target_pairs={{0,8},{1,3},{2,10},{3,1},{4,12},{5,7},{6,14},{7,5},{8,0},{9,11},{1... | collective-permute-start | bytes 196616 | tf_op jit(solution)/shard_map/ppermute | solution.py:492
  46.0 5.3 %collective-permute-start.20 = (f32[32,512]{1,0:T(8,128)S(1)}, f32[32,512]{1,0:T(8,128)S(1)}, u32[]{:S(2)}, u32[]{:S(2)}) collective-permute-start(f32[32,512]{1,0:T(8,128)S(1)} %add_add_fusion.7.tie_ref), channel_id=1, source_target_pairs={{0,8},{1,3},{2,10},{3,1},{4,12},{5,7},{6,14},{7,5},{8,0},{9,11},{1... | collective-permute-start | bytes 196616 | tf_op jit(solution)/shard_map/ppermute | solution.py:492
  49.8 2.9 %collective-permute-start.21 = (f32[32,512]{1,0:T(8,128)S(1)}, f32[32,512]{1,0:T(8,128)S(1)}, u32[]{:S(2)}, u32[]{:S(2)}) collective-permute-start(f32[32,512]{1,0:T(8,128)S(1)} %add_add_fusion.6.refs_1_.refs_0_), channel_id=1, source_target_pairs={{0,1},{1,0},{2,3},{3,2},{4,5},{5,4},{6,7},{7,6},{8,9},{9,8},{10,11... | collective-permute-start | bytes 196616 | tf_op jit(solution)/shard_map/ppermute | solution.py:479
  51.4 1.3 %collective-permute-start.22 = (f32[32,512]{1,0:T(8,128)S(1)}, f32[32,512]{1,0:T(8,128)S(1)}, u32[]{:S(2)}, u32[]{:S(2)}) collective-permute-start(f32[32,512]{1,0:T(8,128)S(1)} %add_add_fusion.5.refs_1_), channel_id=1, source_target_pairs={{0,1},{1,0},{2,3},{3,2},{4,5},{5,4},{6,7},{7,6},{8,9},{9,8},{10,11... | collective-permute-start | bytes 196616 | tf_op jit(solution)/shard_map/ppermute | solution.py:479
